TPU v7x, 256 devices: a whole 4x4x8 slice. The times are simulated.
256 devices in a mesh: lat: 16 (over z, y_hi), lon: 16 (over y_lo, x, core).
Axes of the slice: x: 4, y: 4 (y_hi: 2, y_lo: 2; y = y_hi * 2 + y_lo), z: 8, core: 2. Of those that a mesh axis runs over, the one named last changes fastest.
Arguments:
- fields: bfloat16 [69, 256, 2048], P(None, 'lat', 'lon'), may hold values from -6 to 6
- enc_kernel: bfloat16 [3, 3, 256, 69], replicated, may hold values from -0.25 to 0.25
- gen_kernel: bfloat16 [3, 3, 69, 256], replicated, may hold values from -0.125 to 0.125
- recon_grad: bfloat16 [69, 256, 2048], P(None, 'lat', 'lon'), may hold values from -6 to 6
Outputs:
- rebuilt: bfloat16 [69, 256, 2048], P(None, 'lat', 'lon')
- feat_grad: bfloat16 [256, 256, 2048], P(None, 'lat', 'lon')
- enc_grad: float32 [3, 3, 256, 69], replicated
- gen_grad: float32 [3, 3, 69, 256], replicated
All inputs are finite; a program needn't handle non-finite values.
Results may differ from a plain program's by a relative error of at most 0.0085.
Values may be sent and summed in bfloat16 or wider, within the bound.
No kernel may reach another device: no remote copies, remote signals or barrier semaphores. Data moves between devices by JAX's collectives and lax.ppermute only.
A program may use at most 64 MiB of HBM per device.

v0:
```python
import jax
import jax.numpy as jnp
from jax import lax
from jax.sharding import PartitionSpec as P


def extended(cells, sides, width, closed):
    for axis, dim in sides:
        count = lax.axis_size(axis)
        ends = count if closed else count - 1
        head = lax.slice_in_dim(cells, 0, width, axis=dim)
        tail = lax.slice_in_dim(cells, cells.shape[dim] - width, cells.shape[dim], axis=dim)
        cells = jnp.concatenate(
            [
                lax.ppermute(tail, axis, [(i, (i + 1) % count) for i in range(ends)]),
                cells,
                lax.ppermute(head, axis, [((i + 1) % count, i) for i in range(ends)]),
            ],
            axis=dim,
        )
    return cells


def from_behind(value, axis, steps):
    count = lax.axis_size(axis)
    pairs = [(source, (source + steps) % count) for source in range(count)]
    return lax.ppermute(value, axis, pairs)


def face_pad(source):
    lon_count = lax.axis_size("lon")
    widened = extended(source, (("lon", 2),), 1, True)
    edge_rows = jnp.concatenate([widened[:, :1], widened[:, -1:]], axis=1)
    pole_rows = from_behind(edge_rows, "lon", lon_count // 2)
    plain_pad = extended(widened, (("lat", 1),), 1, False)
    result = (plain_pad, pole_rows)
    return result


def with_poles(plain_pad, pole_rows):
    lat_index = lax.axis_index("lat")
    lat_count = lax.axis_size("lat")
    upper = jnp.where(lat_index == 0, pole_rows[:, :1], plain_pad[:, :1])
    lower = jnp.where(lat_index == lat_count - 1, pole_rows[:, 1:], plain_pad[:, -1:])
    return jnp.concatenate([upper, plain_pad[:, 1:-1], lower], axis=1)


def convolve(padded, kernel, height, width):
    running = None
    for row_tap in range(3):
        for col_tap in range(3):
            section = padded[:, row_tap : row_tap + height, col_tap : col_tap + width].reshape(
                padded.shape[0], height * width
            )
            product = jnp.dot(kernel[row_tap, col_tap], section, preferred_element_type=jnp.float32)
            running = product if running is None else running + product
    return running.reshape(kernel.shape[2], height, width)


def adjoint_conv(padded, kernel, height, width):
    running = None
    for row_tap in range(3):
        for col_tap in range(3):
            section = padded[
                :, 2 - row_tap : 2 - row_tap + height, 2 - col_tap : 2 - col_tap + width
            ].reshape(padded.shape[0], height * width)
            product = lax.dot_general(
                kernel[row_tap, col_tap],
                section,
                (((0,), (0,)), ((), ())),
                preferred_element_type=jnp.float32,
            )
            running = product if running is None else running + product
    return running.reshape(kernel.shape[3], height, width)


def pole_terms(pole_rows, kernel, width):
    terms = []
    for which, row_tap in ((0, 0), (1, 2)):
        running = None
        for col_tap in range(3):
            section = pole_rows[:, which, 2 - col_tap : 2 - col_tap + width]
            product = lax.dot_general(
                kernel[row_tap, col_tap],
                section,
                (((0,), (0,)), ((), ())),
                preferred_element_type=jnp.float32,
            )
            running = product if running is None else running + product
        terms.append(running)
    return (terms[0], terms[1])


def weight_grad(cotangent, padded, height, width):
    flat_cot = cotangent.reshape(cotangent.shape[0], height * width)
    taps = []
    for row_tap in range(3):
        row_list = []
        for col_tap in range(3):
            section = padded[:, row_tap : row_tap + height, col_tap : col_tap + width].reshape(
                padded.shape[0], height * width
            )
            row_list.append(
                lax.dot_general(
                    flat_cot, section, (((1,), (1,)), ((), ())), preferred_element_type=jnp.float32
                )
            )
        taps.append(jnp.stack(row_list))
    return jnp.stack(taps)


def sum_grads(enc_part, gen_part):
    summed = lax.psum((enc_part, gen_part), ("lat", "lon"))
    return summed


def on_device(fields, enc_kernel, gen_kernel, recon_grad):
    height = fields.shape[1]
    width = fields.shape[2]
    lat_index = lax.axis_index("lat")
    lat_count = lax.axis_size("lat")
    lon_count = lax.axis_size("lon")
    plain_in, pole_in = face_pad(fields)
    plain_cot, pole_cot = face_pad(recon_grad)
    padded_in = with_poles(plain_in, pole_in)
    pre_act = convolve(padded_in, enc_kernel, height, width)
    hidden = jax.nn.silu(pre_act).astype(jnp.bfloat16)
    plain_hid, pole_hid = face_pad(hidden)
    padded_hid = with_poles(plain_hid, pole_hid)
    rebuilt = convolve(padded_hid, gen_kernel, height, width).astype(jnp.bfloat16)
    feat_f32 = adjoint_conv(plain_cot, gen_kernel, height, width)
    upper_term, lower_term = pole_terms(pole_cot, gen_kernel, width)
    feat_f32 = feat_f32.at[:, 0].add(jnp.where(lat_index == 0, upper_term, 0.0))
    feat_f32 = feat_f32.at[:, -1].add(jnp.where(lat_index == lat_count - 1, lower_term, 0.0))
    feat_grad = feat_f32.astype(jnp.bfloat16)
    logistic = jax.nn.sigmoid(pre_act)
    pre_grad = (
        feat_grad.astype(jnp.float32) * logistic * (1.0 + pre_act * (1.0 - logistic))
    ).astype(jnp.bfloat16)
    gen_part = weight_grad(recon_grad, padded_hid, height, width)
    enc_part = weight_grad(pre_grad, padded_in, height, width)
    enc_sum, gen_sum = sum_grads(enc_part, gen_part)
    norm_scale = 1.0 / jnp.sqrt(jnp.float32(height * lat_count * width * lon_count))
    return (rebuilt, feat_grad, enc_sum * norm_scale, gen_sum * norm_scale)


def solution(mesh):
    return jax.shard_map(
        on_device,
        mesh=mesh,
        in_specs=(P(None, "lat", "lon"), P(), P(), P(None, "lat", "lon")),
        out_specs=(P(None, "lat", "lon"), P(None, "lat", "lon"), P(), P()),
        check_vma=False,
    )
```

profile of v0, /device:TPU:1, one launch (start us, length us, event | category | flops | bytes accessed | tf_op | source)
XLA Modules:
  0.0 362.6 jit_solution(568976448779188085)
XLA Ops:
  7.2 1.1 copy.107
  9.2 2.6 collective-permute-start.10
  12.4 1.0 copy.93
  13.6 1.2 collective-permute-start
  14.8 2.8 collective-permute-start.1
  18.4 4.8 %collective-permute-start.13 = (bf16[69,1,130]{2,0,1:T(8,128)(2,1)S(1)}, bf16[69,1,130]{2,0,1:T(8,128)(2,1)S(1)}, u32[]{:S(2)}, u32[]{:S(2)}) collective-permute-start(bf16[69,1,130]{2,0,1:T(8,128)(2,1)S(1)} %get-tuple-element.61), channel_id=1, source_target_pairs={{0,16},{16,32},{32,48},{48,64},{64,80},{80,96},{96,112},{112,128},... | collective-permute-start | bytes 53828 | tf_op jit(solution)/shard_map/ppermute | solution.py:15
  23.2 1.3 collective-permute-start.12
  24.6 1.3 collective-permute-start.4
  25.9 6.1 %collective-permute-start.3 = (bf16[69,1,130]{2,0,1:T(8,128)(2,1)S(1)}, bf16[69,1,130]{2,0,1:T(8,128)(2,1)S(1)}, u32[]{:S(2)}, u32[]{:S(2)}) collective-permute-start(bf16[69,1,130]{2,0,1:T(8,128)(2,1)S(1)} %get-tuple-element.66), channel_id=1, source_target_pairs={{0,16},{16,32},{32,48},{48,64},{64,80},{80,96},{96,112},{112,128},... | collective-permute-start | bytes 53828 | tf_op jit(solution)/shard_map/ppermute | solution.py:15
  33.9 1.3 collective-permute-start.2
  49.3 1.7 fusion.23
  52.5 0.9 multiply_convert_fusion
  57.3 1.4 collective-permute-start.5
  58.8 1.8 collective-permute-start.6
  60.7 0.9 pad_maximum_fusion.3
  61.6 1.8 copy.147
  63.4 6.0 %collective-permute-start.8 = (bf16[256,1,130]{0,2,1:T(8,128)(2,1)S(1)}, bf16[256,1,130]{0,2,1:T(8,128)(2,1)S(1)}, u32[]{:S(2)}, u32[]{:S(2)}) collective-permute-start(bf16[256,1,130]{0,2,1:T(8,128)(2,1)S(1)} %get-tuple-element.53), channel_id=1, source_target_pairs={{0,16},{16,32},{32,48},{48,64},{64,80},{80,96},{96,112},{112,128},... | collective-permute-start | bytes 199688 | tf_op jit(solution)/shard_map/ppermute | solution.py:15
  69.4 1.3 collective-permute-start.9
  72.7 3.3 collective-permute-done.9
  78.9 1.5 fusion.121
  80.5 1.9 fusion.122
  82.3 2.0 fusion.34
  84.4 2.0 fusion.53
  87.4 2.0 convolution_add_fusion.13
  89.4 1.3 convolution_add_fusion.12
  90.7 1.2 fusion.10
  91.9 1.3 fusion.11
  93.2 1.2 convolution_add_fusion.9
  94.4 1.2 fusion.12
  96.4 255.3 %all-reduce.3.cloned.1.call-done = (f32[3,3,256,69]{2,3,1,0:T(8,128)}, f32[3,3,69,256]{3,2,1,0:T(8,128)}) async-done(((f32[3,3,256,69]{2,3,1,0:T(8,128)}, f32[3,3,69,256]{3,2,1,0:T(8,128)}), (f32[3,3,256,69]{2,3,1,0:T(8,128)}, f32[3,3,69,256]{3,2,1,0:T(8,128)})) %all-reduce.3.cloned.1.call-update) | async-done | bytes 1271824 | tf_op jit(solution)/shard_map/psum | solution.py:113
  351.8 2.0 broadcast_multiply_fusion.1
  353.7 2.0 broadcast_multiply_fusion
  (159 shorter events, 29.8 us)
Async XLA Ops:
  7.2 10.5 %copy-start = (bf16[69,16,128]{2,1,0:T(8,128)(2,1)S(1)}, bf16[69,16,128]{2,1,0:T(8,128)(2,1)}, u32[]{:S(2)}) copy-start(bf16[69,16,128]{2,1,0:T(8,128)(2,1)} %param.11) | copy-start | bytes 847876
  7.2 10.5 %copy-start.3 = (bf16[69,16,128]{2,1,0:T(8,128)(2,1)S(1)}, bf16[69,16,128]{2,1,0:T(8,128)(2,1)}, u32[]{:S(2)}) copy-start(bf16[69,16,128]{2,1,0:T(8,128)(2,1)} %param.8) | copy-start | bytes 847876
  7.2 344.6 %all-reduce.3.cloned.1.call-start = ((), (), s32[]{:S(2)}) async-start(), calls=%async_computation | async-start | bytes 2654208 | tf_op jit(solution)/shard_map/psum | solution.py:113
  9.2 8.7 %collective-permute-start.10 = (bf16[69,16,1]{2,0,1:T(8,128)(2,1)}, bf16[69,16,1]{2,0,1:T(8,128)(2,1)S(1)}, u32[]{:S(2)}, u32[]{:S(2)}) collective-permute-start(bf16[69,16,1]{2,0,1:T(8,128)(2,1)} %get-tuple-element.79), channel_id=1, source_target_pairs={{0,1},{1,2},{2,3},{3,4},{4,5},{5,6},{6,7},{7,8},{8,9},{9,10},{10,1... | collective-permute-start | bytes 6632 | tf_op jit(solution)/shard_map/ppermute | solution.py:15
  11.8 6.4 %collective-permute-start.11 = (bf16[69,16,1]{2,0,1:T(8,128)(2,1)S(1)}, bf16[69,16,1]{2,0,1:T(8,128)(2,1)S(1)}, u32[]{:S(2)}, u32[]{:S(2)}) collective-permute-start(bf16[69,16,1]{2,0,1:T(8,128)(2,1)S(1)} %get-tuple-element.80), channel_id=1, source_target_pairs={{1,0},{2,1},{3,2},{4,3},{5,4},{6,5},{7,6},{8,7},{9,8},{10,9},{11,1... | collective-permute-start | bytes 6632 | tf_op jit(solution)/shard_map/ppermute | solution.py:17
  13.6 10.9 %collective-permute-start = (bf16[69,16,1]{2,0,1:T(8,128)(2,1)S(1)}, bf16[69,16,1]{2,0,1:T(8,128)(2,1)S(1)}, u32[]{:S(2)}, u32[]{:S(2)}) collective-permute-start(bf16[69,16,1]{2,0,1:T(8,128)(2,1)S(1)} %get-tuple-element.83), channel_id=1, source_target_pairs={{0,1},{1,2},{2,3},{3,4},{4,5},{5,6},{6,7},{7,8},{8,9},{9,10},{10,1... | collective-permute-start | bytes 6632 | tf_op jit(solution)/shard_map/ppermute | solution.py:15
  14.8 9.7 %collective-permute-start.1 = (bf16[69,16,1]{2,0,1:T(8,128)(2,1)S(1)}, bf16[69,16,1]{2,0,1:T(8,128)(2,1)S(1)}, u32[]{:S(2)}, u32[]{:S(2)}) collective-permute-start(bf16[69,16,1]{2,0,1:T(8,128)(2,1)S(1)} %get-tuple-element.84), channel_id=1, source_target_pairs={{1,0},{2,1},{3,2},{4,3},{5,4},{6,5},{7,6},{8,7},{9,8},{10,9},{11,1... | collective-permute-start | bytes 6632 | tf_op jit(solution)/shard_map/ppermute | solution.py:17
  18.4 15.6 %collective-permute-start.13 = (bf16[69,1,130]{2,0,1:T(8,128)(2,1)S(1)}, bf16[69,1,130]{2,0,1:T(8,128)(2,1)S(1)}, u32[]{:S(2)}, u32[]{:S(2)}) collective-permute-start(bf16[69,1,130]{2,0,1:T(8,128)(2,1)S(1)} %get-tuple-element.61), channel_id=1, source_target_pairs={{0,16},{16,32},{32,48},{48,64},{64,80},{80,96},{96,112},{112,128},... | collective-permute-start | bytes 53828 | tf_op jit(solution)/shard_map/ppermute | solution.py:15
  23.2 12.1 %collective-permute-start.12 = (bf16[69,1,130]{2,0,1:T(8,128)(2,1)S(1)}, bf16[69,1,130]{2,0,1:T(8,128)(2,1)S(1)}, u32[]{:S(2)}, u32[]{:S(2)}) collective-permute-start(bf16[69,1,130]{2,0,1:T(8,128)(2,1)S(1)} %get-tuple-element.62), channel_id=1, source_target_pairs={{16,0},{32,16},{48,32},{64,48},{80,64},{96,80},{112,96},{128,112},... | collective-permute-start | bytes 53828 | tf_op jit(solution)/shard_map/ppermute | solution.py:17
  24.6 17.6 %collective-permute-start.4 = (bf16[69,1,130]{2,0,1:T(8,128)(2,1)S(1)}, bf16[69,1,130]{2,0,1:T(8,128)(2,1)S(1)}, u32[]{:S(2)}, u32[]{:S(2)}) collective-permute-start(bf16[69,1,130]{2,0,1:T(8,128)(2,1)S(1)} %get-tuple-element.65), channel_id=1, source_target_pairs={{16,0},{32,16},{48,32},{64,48},{80,64},{96,80},{112,96},{128,112},... | collective-permute-start | bytes 53828 | tf_op jit(solution)/shard_map/ppermute | solution.py:17
  25.9 16.3 %collective-permute-start.3 = (bf16[69,1,130]{2,0,1:T(8,128)(2,1)S(1)}, bf16[69,1,130]{2,0,1:T(8,128)(2,1)S(1)}, u32[]{:S(2)}, u32[]{:S(2)}) collective-permute-start(bf16[69,1,130]{2,0,1:T(8,128)(2,1)S(1)} %get-tuple-element.66), channel_id=1, source_target_pairs={{0,16},{16,32},{32,48},{48,64},{64,80},{80,96},{96,112},{112,128},... | collective-permute-start | bytes 53828 | tf_op jit(solution)/shard_map/ppermute | solution.py:15
  32.1 18.9 %collective-permute-start.14 = (bf16[69,2,130]{2,0,1:T(8,128)(2,1)S(1)}, bf16[69,2,130]{2,0,1:T(8,128)(2,1)S(1)}, u32[]{:S(2)}, u32[]{:S(2)}) collective-permute-start(bf16[69,2,130]{2,0,1:T(8,128)(2,1)S(1)} %pad_maximum_fusion.13), channel_id=1, source_target_pairs={{0,8},{1,9},{2,10},{3,11},{4,12},{5,13},{6,14},{7,15},{8,0},{9,1},... | collective-permute-start | bytes 107648 | tf_op jit(solution)/shard_map/ppermute | solution.py:27
  33.9 8.4 %collective-permute-start.2 = (bf16[69,2,130]{2,0,1:T(8,128)(2,1)S(1)}, bf16[69,2,130]{2,0,1:T(8,128)(2,1)S(1)}, u32[]{:S(2)}, u32[]{:S(2)}) collective-permute-start(bf16[69,2,130]{2,0,1:T(8,128)(2,1)S(1)} %pad_maximum_fusion.12), channel_id=1, source_target_pairs={{0,8},{1,9},{2,10},{3,11},{4,12},{5,13},{6,14},{7,15},{8,0},{9,1},... | collective-permute-start | bytes 107648 | tf_op jit(solution)/shard_map/ppermute | solution.py:27
  36.9 1.0 copy-start.6
  43.9 1.0 copy-start.8
  55.0 1.0 copy-start.4
  57.3 6.0 %collective-permute-start.5 = (bf16[256,16,1]{0,2,1:T(2,128)(2,1)}, bf16[256,16,1]{0,2,1:T(2,128)(2,1)S(1)}, u32[]{:S(2)}, u32[]{:S(2)}) collective-permute-start(bf16[256,16,1]{0,2,1:T(2,128)(2,1)} %get-tuple-element.57), channel_id=1, source_target_pairs={{0,1},{1,2},{2,3},{3,4},{4,5},{5,6},{6,7},{7,8},{8,9},{9,10},{10,1... | collective-permute-start | bytes 24584 | tf_op jit(solution)/shard_map/ppermute | solution.py:15
  58.8 4.6 %collective-permute-start.6 = (bf16[256,16,1]{0,2,1:T(2,128)(2,1)S(1)}, bf16[256,16,1]{0,2,1:T(2,128)(2,1)S(1)}, u32[]{:S(2)}, u32[]{:S(2)}) collective-permute-start(bf16[256,16,1]{0,2,1:T(2,128)(2,1)S(1)} %get-tuple-element.58), channel_id=1, source_target_pairs={{1,0},{2,1},{3,2},{4,3},{5,4},{6,5},{7,6},{8,7},{9,8},{10,9},{11,1... | collective-permute-start | bytes 24584 | tf_op jit(solution)/shard_map/ppermute | solution.py:17
  63.4 9.3 %collective-permute-start.8 = (bf16[256,1,130]{0,2,1:T(8,128)(2,1)S(1)}, bf16[256,1,130]{0,2,1:T(8,128)(2,1)S(1)}, u32[]{:S(2)}, u32[]{:S(2)}) collective-permute-start(bf16[256,1,130]{0,2,1:T(8,128)(2,1)S(1)} %get-tuple-element.53), channel_id=1, source_target_pairs={{0,16},{16,32},{32,48},{48,64},{64,80},{80,96},{96,112},{112,128},... | collective-permute-start | bytes 199688 | tf_op jit(solution)/shard_map/ppermute | solution.py:15
  69.4 6.6 %collective-permute-start.9 = (bf16[256,1,130]{0,2,1:T(8,128)(2,1)S(1)}, bf16[256,1,130]{0,2,1:T(8,128)(2,1)S(1)}, u32[]{:S(2)}, u32[]{:S(2)}) collective-permute-start(bf16[256,1,130]{0,2,1:T(8,128)(2,1)S(1)} %get-tuple-element.54), channel_id=1, source_target_pairs={{16,0},{32,16},{48,32},{64,48},{80,64},{96,80},{112,96},{128,112},... | collective-permute-start | bytes 199688 | tf_op jit(solution)/shard_map/ppermute | solution.py:17
  70.8 5.2 %collective-permute-start.7 = (bf16[256,2,130]{0,2,1:T(8,128)(2,1)S(1)}, bf16[256,2,130]{0,2,1:T(8,128)(2,1)S(1)}, u32[]{:S(2)}, u32[]{:S(2)}) collective-permute-start(bf16[256,2,130]{0,2,1:T(8,128)(2,1)S(1)} %pad_maximum_fusion.11), channel_id=1, source_target_pairs={{0,8},{1,9},{2,10},{3,11},{4,12},{5,13},{6,14},{7,15},{8,0},{9,1},... | collective-permute-start | bytes 399368 | tf_op jit(solution)/shard_map/ppermute | solution.py:27
  87.4 2.0 copy-start.1
  87.4 3.3 copy-start.7
  89.4 2.5 copy-start.5
  91.9 2.5 copy-start.2
Sparse Core Ops, SparseCore 0:
  87.5 264.2 all-reduce.2
where the time goes:
time: 363 us
  waiting for transfers between devices  259 us (71%)
  starting transfers between devices  34 us (9%)
  matrix products  30 us (8%)
  between operations  15 us (4%)
  local copies, waits for them, and re-layouts  14.2 us (4%)
  other arithmetic  10.3 us (3%)
    psum x1, waiting for transfers between devices, sum_grads(): summed = lax.psum((enc_part, gen_part), ('lat', 'lon'))  255 us
    ppermute x6, starting transfers between devices, extended(): lax.ppermute(tail, axis, [(i, (i + 1) % count) for i in range(ends)])  22.2 us
    dot_general x18, matrix products, convolve(): jnp.dot(kernel[row_tap, col_tap], section, preferred_element_type=jnp.flo...  18.3 us
    ppermute x6, starting transfers between devices, extended(): lax.ppermute(head, axis, [((i + 1) % count, i) for i in range(ends)])  9.19 us
  transfers between devices with their start and end apart: 16, of which 3 were waited for; matrix products, arithmetic and copies ran while one was open for 8% of the time, Pallas kernels for 0%

commit v1 on v0

v1 whole, which is shorter than its diff:
```python
import functools

import jax
import jax.numpy as jnp
from jax import lax
from jax.experimental import pallas as pl
from jax.experimental.pallas import tpu as pltpu
from jax.sharding import Mesh
from jax.sharding import PartitionSpec as P

CHIPS = ("z", "y_hi", "y_lo", "x")
LAT = ("z", "y_hi")
LON = ("y_lo", "x", "core")

LANES = 128
ROWS = 16
DEEP = 80
BAND = 3 * DEEP
TAPS = 3 * BAND
PACK = 640
F32 = jnp.float32
BF16 = jnp.bfloat16
NT = (((1,), (1,)), ((), ()))
TN = (((0,), (0,)), ((), ()))
FULL = pl.BlockSpec(memory_space=pltpu.VMEM)
FLAGS = pl.BlockSpec(memory_space=pltpu.SMEM)


def lane_of(shape):
    return lax.broadcasted_iota(jnp.int32, shape, len(shape) - 1)


def dot(a, b, dims=(((1,), (0,)), ((), ()))):
    return lax.dot_general(a, b, dims, preferred_element_type=F32)


def call(kernel, outs, cost, scratch=(), limit=48):
    return functools.partial(
        pl.pallas_call,
        kernel,
        out_shape=outs,
        scratch_shapes=list(scratch),
        compiler_params=pltpu.CompilerParams(vmem_limit_bytes=limit << 20),
        cost_estimate=pl.CostEstimate(flops=cost, bytes_accessed=cost // 500, transcendentals=0),
    )


def pick(row, lane):
    rows = lax.broadcasted_iota(jnp.int32, (8, LANES), 0)
    lanes = lax.broadcasted_iota(jnp.int32, (8, LANES), 1)
    return (rows == row) & (lanes == lane)


def picks(pairs):
    hot = pick(*pairs[0])
    for pair in pairs[1:]:
        hot = hot | pick(*pair)
    return jnp.where(hot, 1.0, 0.0).astype(BF16)


def columns_kernel(x_ref, r_ref, east_ref, west_ref):
    x = x_ref[...].reshape(ROWS * DEEP, LANES)
    r = r_ref[...].reshape(ROWS * DEEP, LANES)
    east = dot(picks([(0, 126), (1, 127)]), x, NT) + dot(picks([(2, 127)]), r, NT)
    west = dot(picks([(0, 0), (1, 1)]), x, NT) + dot(picks([(2, 0)]), r, NT)
    east_ref[...] = east.astype(BF16)
    west_ref[...] = west.astype(BF16)


def rows_kernel(flags_ref, x_ref, r_ref, east_ref, west_ref, hx_ref, hr_ref, a_ref, b_ref):
    low = flags_ref[3] == 1
    left = east_ref[...].astype(F32).T.astype(BF16)
    right = west_ref[...].astype(F32).T.astype(BF16)
    hx = dot(left, picks([(0, 126), (1, 127)])) + dot(right, picks([(0, 0), (1, 1)]))
    hr = dot(left, picks([(2, 127)])) + dot(right, picks([(2, 0)]))
    hx_ref[...] = hx.astype(BF16).reshape(ROWS, DEEP, LANES)
    hr_ref[...] = hr.astype(BF16).reshape(ROWS, DEEP, LANES)
    top = (x_ref[0], x_ref[1], r_ref[0], hx_ref[0], hx_ref[1], hr_ref[0])
    end = ROWS - 1
    bottom = (x_ref[end], x_ref[end - 1], r_ref[end], hx_ref[end], hx_ref[end - 1], hr_ref[end])
    for k in range(6):
        t, b = top[k].astype(F32), bottom[k].astype(F32)
        a_ref[k] = jnp.where(low, b, t).astype(BF16)
        b_ref[k] = jnp.where(low, t, b).astype(BF16)


def shifts(x, h):
    lane = lane_of(x.shape)
    left = pltpu.roll(jnp.where(lane == LANES - 1, h, x), 1, 1)
    right = pltpu.roll(jnp.where(lane == 0, h, x), LANES - 1, 1)
    return left, right


def main_kernel(
    flags_ref, x_ref, r_ref, hx_ref, hr_ref, pa_ref, pb_ref, we_ref, gt_ref,
    feat_ref, hid_ref, strip_ref, sent_ref, kept_ref,
    f_s, r_s, pole_s, u_s, fx_s, acc_s, pack_s,
):
    north, south = flags_ref[0] == 1, flags_ref[1] == 1
    core, low = flags_ref[2], flags_ref[3] == 1
    lane = lane_of((DEEP, LANES))
    u_s[...] = jnp.zeros_like(u_s)

    def put_field(slot, x, h):
        left, right = shifts(x, h)
        f_s[slot, :DEEP, :] = left.astype(BF16)
        f_s[slot, DEEP : 2 * DEEP, :] = x.astype(BF16)
        f_s[slot, 2 * DEEP :, :] = right.astype(BF16)
        spot = 2 * slot
        hit = (lane == spot) | (lane == spot + 1)
        sides = (
            (jnp.where(lane == LANES - 1, x, h), spot + 2),
            (h, spot + 1),
            (jnp.where(lane == 0, x, h), spot),
        )
        for tap, (plane, turn) in enumerate(sides):
            turned = pltpu.roll(plane, turn, 1)
            rows = pl.ds(tap * DEEP, DEEP)
            u_s[rows, :] = jnp.where(hit, turned, u_s[rows, :])

    def put_cot(ref, slot, x, h):
        left, right = shifts(x, h)
        ref[slot, :DEEP, :] = right.astype(BF16)
        ref[slot, DEEP : 2 * DEEP, :] = x.astype(BF16)
        ref[slot, 2 * DEEP :, :] = left.astype(BF16)

    def fill(row, carry):
        put_field(row + 2, x_ref[row].astype(F32), hx_ref[row].astype(F32))
        put_cot(r_s, ROWS - row, r_ref[row].astype(F32), hr_ref[row].astype(F32))
        return carry

    lax.fori_loop(0, ROWS, fill, 0)
    pa = [pa_ref[k].astype(F32) for k in range(6)]
    pb = [pb_ref[k].astype(F32) for k in range(6)]
    up = [jnp.where(low, a, b) for a, b in zip(pa, pb)]
    down = [jnp.where(low, b, a) for a, b in zip(pa, pb)]
    put_field(1, up[0], up[3])
    put_field(0, up[1], up[4])
    put_field(ROWS + 2, down[0], down[3])
    put_field(ROWS + 3, down[1], down[4])
    put_cot(r_s, ROWS + 1, jnp.where(north, 0.0, up[2]), jnp.where(north, 0.0, up[5]))
    put_cot(r_s, 0, jnp.where(south, 0.0, down[2]), jnp.where(south, 0.0, down[5]))
    put_cot(pole_s, 0, jnp.where(north, up[2], 0.0), jnp.where(north, up[5], 0.0))
    put_cot(pole_s, 1, jnp.where(south, down[2], 0.0), jnp.where(south, down[5], 0.0))

    we, gt = we_ref[...], gt_ref[...]

    def band(slot):
        return f_s[slot].astype(F32)

    def swapped(flag, first, last):
        return jnp.where(flag, last, first).astype(BF16), jnp.where(flag, first, last).astype(BF16)

    def silu(v):
        return v * (1.0 / (1.0 + jnp.exp(-v)))

    n0, n2 = swapped(north, band(0), band(2))
    s0, s2 = swapped(south, band(ROWS + 1), band(ROWS + 3))
    ring = jnp.concatenate(
        [
            jnp.concatenate([n0, f_s[1], n2], axis=0),
            jnp.concatenate([s0, f_s[ROWS + 2], s2], axis=0),
        ],
        axis=1,
    )
    halo = silu(dot(we, ring)).astype(BF16)
    hid_ref[0] = halo[:, :LANES]
    hid_ref[ROWS + 1] = halo[:, LANES:]

    u = u_s[...]
    u2 = pltpu.roll(u, LANES - 2, 1)
    u4 = pltpu.roll(u, LANES - 4, 1)
    wide = lane_of(u.shape)
    last = 2 * (ROWS + 1)
    flip = (north & (wide < 2)) | (south & ((wide == last) | (wide == last + 1)))
    strip = jnp.concatenate(
        [jnp.where(flip, u4, u).astype(BF16), u2.astype(BF16), jnp.where(flip, u, u4).astype(BF16)],
        axis=0,
    )
    strip_ref[...] = silu(dot(we, strip)).astype(BF16)

    fx_s[:, :LANES] = dot(gt[:, :BAND], pole_s[0])
    fx_s[:, LANES:] = dot(gt[:, 2 * BAND :], pole_s[1])
    acc_s[...] = jnp.zeros_like(acc_s)

    def two(ref, first, second):
        a = ref[pl.ds(first, 3)].reshape(TAPS, LANES)
        b = ref[pl.ds(second, 3)].reshape(TAPS, LANES)
        return jnp.concatenate([a, b], axis=1)

    half = lane_of(fx_s.shape) < LANES

    def step(pair, carry):
        f2 = two(f_s, 2 * pair + 1, 2 * pair + 2)
        r2 = two(r_s, ROWS - 1 - 2 * pair, ROWS - 2 - 2 * pair)
        pre = dot(we_ref[...], f2)
        gate = 1.0 / (1.0 + jnp.exp(-pre))
        hid = (pre * gate).astype(BF16)
        edge = ((pair == 0) & half) | ((pair == ROWS // 2 - 1) & ~half)
        feat = (dot(gt_ref[...], r2) + jnp.where(edge, fx_s[...], 0.0)).astype(BF16)
        feat_ref[2 * pair] = feat[:, :LANES]
        feat_ref[2 * pair + 1] = feat[:, LANES:]
        hid_ref[2 * pair + 1] = hid[:, :LANES]
        hid_ref[2 * pair + 2] = hid[:, LANES:]
        back = (feat.astype(F32) * gate * (1.0 + pre * (1.0 - gate))).astype(BF16)
        acc_s[0] += dot(r2, hid, NT)
        acc_s[1] += dot(f2, back, NT)
        return carry

    lax.fori_loop(0, ROWS // 2, step, 0)
    acc_s[0, :BAND, :] += dot(pole_s[0], hid_ref[1], NT)
    acc_s[0, 2 * BAND :, :] += dot(pole_s[1], hid_ref[ROWS], NT)

    def pack(which, out_ref):
        for tap in range(9):
            pack_s[69 * tap : 69 * tap + 69, :] = acc_s[which, DEEP * tap : DEEP * tap + 69, :]
        pack_s[621:, :] = jnp.zeros((pack_s.shape[0] - 621, pack_s.shape[1]), F32)
        out_ref[:PACK, :] = pack_s[:PACK, :LANES].astype(out_ref.dtype)
        out_ref[PACK:, :] = pack_s[:PACK, LANES:].astype(out_ref.dtype)

    pack(1 - core, sent_ref)
    pack(core, kept_ref)


def rebuilt_kernel(hid_ref, strip_ref, ga_ref, out_ref, z_s, t_s):
    ga = ga_ref[...]
    zs = dot(ga, strip_ref[...])
    t0 = zs[:DEEP]
    t2 = zs[2 * DEEP : BAND]
    for a in (1, 2):
        t0 = t0 + pltpu.roll(zs[a * BAND : a * BAND + DEEP], LANES - 2 * a, 1)
        t2 = t2 + pltpu.roll(zs[a * BAND + 2 * DEEP : (a + 1) * BAND], LANES - 2 * a, 1)
    lane = lane_of((DEEP, LANES))
    even = lax.rem(lane, 2) == 0
    t_s[...] = jnp.where(even, pltpu.roll(t2, LANES - 1, 1), pltpu.roll(t0, 1, 1))

    def fill(pair, carry):
        z = dot(ga, jnp.concatenate([hid_ref[2 * pair], hid_ref[2 * pair + 1]], axis=1))
        z_s[2 * pair] = z[:, :LANES]
        z_s[2 * pair + 1] = z[:, LANES:]
        return carry

    lax.fori_loop(0, ROWS // 2 + 1, fill, 0)

    def emit(row, carry):
        sums = []
        for b in range(3):
            total = z_s[row, b * DEEP : (b + 1) * DEEP, :]
            for a in (1, 2):
                start = a * BAND + b * DEEP
                total = total + z_s[row + a, start : start + DEEP, :]
            sums.append(total)
        out = sums[1]
        out = out + jnp.where(lane == 0, 0.0, pltpu.roll(sums[0], 1, 1))
        out = out + jnp.where(lane == LANES - 1, 0.0, pltpu.roll(sums[2], LANES - 1, 1))
        side = pltpu.roll(t_s[...], LANES - 1 - 2 * row, 1)
        out = out + jnp.where((lane == 0) | (lane == LANES - 1), side, 0.0)
        out_ref[row] = out.astype(BF16)
        return carry

    lax.fori_loop(0, ROWS, emit, 0)


def total_kernel(pieces_ref, out_ref):
    count = pieces_ref.shape[0]
    group = count // 128
    rows = lax.broadcasted_iota(jnp.int32, (16, count), 0)
    cells = lax.broadcasted_iota(jnp.int32, (16, count), 1)
    hot = jnp.where(lax.rem(cells, group) == rows, 1.0, 0.0).astype(BF16)
    total = dot(hot, pieces_ref[...]).astype(BF16)
    out_ref[...] = dot(hot, total, TN).astype(BF16)


def final_kernel(norm, flags_ref, own_ref, other_ref, enc_ref, gen_ref, pack_s):
    first = flags_ref[2] == 0
    own, other = own_ref[...].astype(F32), other_ref[...].astype(F32)
    gen = jnp.where(first, own, other) * norm
    enc = jnp.where(first, other, own) * norm
    for value, out in ((gen, gen_ref), (enc, enc_ref)):
        pack_s[...] = value
        for tap in range(9):
            out[tap, :, :LANES] = pack_s[69 * tap : 69 * tap + 69, :]
            out[tap, :, LANES:] = pack_s[PACK + 69 * tap : PACK + 69 * tap + 69, :]


def swap_cores(value):
    return lax.ppermute(value, "core", [(0, 1), (1, 0)])


def planes(v):
    return jnp.pad(jnp.transpose(v, (1, 0, 2)), ((0, 0), (0, DEEP - v.shape[0]), (0, 0)))


def great_circles(lat_count, lon_count):
    pairs = []
    for la in range(lat_count):
        for lo in range(lon_count):
            if lo < lon_count // 2:
                to = (la + 1, lo) if la < lat_count - 1 else (la, lo + lon_count // 2)
            else:
                to = (la - 1, lo) if la > 0 else (la, lo - lon_count // 2)
            pairs.append((la * lon_count + lo, to[0] * lon_count + to[1]))
    return pairs, [(b, a) for a, b in pairs]


def on_device(fields, enc_kernel, gen_kernel, recon_grad):
    variables, height, width = fields.shape
    channels = gen_kernel.shape[3]
    lat_index, lat_count = lax.axis_index(LAT), lax.axis_size(LAT)
    lon_count = lax.axis_size(LON)
    chips = lax.axis_size(CHIPS)
    core = lax.axis_index("core")
    low = lax.axis_index("y_lo") == 0
    flags = jnp.stack(
        [
            (lat_index == 0).astype(jnp.int32),
            (lat_index == lat_count - 1).astype(jnp.int32),
            core.astype(jnp.int32),
            low.astype(jnp.int32),
        ]
    )
    pad = ((0, 0), (0, 0), (0, DEEP - variables), (0, 0))
    gen_rows = jnp.pad(gen_kernel, pad).reshape(TAPS, channels)
    enc_rows = jnp.pad(jnp.swapaxes(enc_kernel, 2, 3), pad).reshape(TAPS, channels)
    x, r = planes(fields), planes(recon_grad)

    plane = jax.ShapeDtypeStruct((ROWS, DEEP, LANES), BF16)
    side = jax.ShapeDtypeStruct((8, ROWS * DEEP), BF16)
    east, west = call(columns_kernel, (side, side), 10**7)(
        in_specs=[FULL] * 2, out_specs=(FULL, FULL)
    )(x, r)
    right = [(i, (i + 1) % lon_count) for i in range(lon_count)]
    left = [(b, a) for a, b in right]
    from_left = lax.ppermute(east, LON, right)
    from_right = lax.ppermute(west, LON, left)
    packet = jax.ShapeDtypeStruct((6, DEEP, LANES), BF16)
    hx, hr, pa, pb = call(rows_kernel, (plane, plane, packet, packet), 10**7)(
        in_specs=[FLAGS] + [FULL] * 4, out_specs=(FULL,) * 4
    )(flags, x, r, from_left, from_right)
    ahead, behind = great_circles(lat_count, lon_count)
    pa = lax.ppermute(pa, LAT + LON, ahead)
    pb = lax.ppermute(pb, LAT + LON, behind)

    packed = (2 * PACK, LANES)
    feat, hid, strip, sent, kept = call(
        main_kernel,
        (
            jax.ShapeDtypeStruct((ROWS, channels, LANES), BF16),
            jax.ShapeDtypeStruct((ROWS + 2, channels, LANES), BF16),
            jax.ShapeDtypeStruct((channels, LANES), BF16),
            jax.ShapeDtypeStruct(packed, BF16),
            jax.ShapeDtypeStruct(packed, F32),
        ),
        3 * 10**9,
        [
            pltpu.VMEM((ROWS + 4, BAND, LANES), BF16),
            pltpu.VMEM((ROWS + 2, BAND, LANES), BF16),
            pltpu.VMEM((2, BAND, LANES), BF16),
            pltpu.VMEM((BAND, LANES), F32),
            pltpu.VMEM((channels, 2 * LANES), F32),
            pltpu.VMEM((2, TAPS, channels), F32),
            pltpu.VMEM((PACK + 8, channels), F32),
        ],
    )(in_specs=[FLAGS] + [FULL] * 8, out_specs=(FULL,) * 5)(
        flags, x, r, hx, hr, pa, pb, enc_rows.T, gen_rows.T
    )
    rows = call(
        rebuilt_kernel,
        plane,
        10**9,
        [pltpu.VMEM((ROWS + 2, TAPS, LANES), F32), pltpu.VMEM((DEEP, LANES), F32)],
    )(in_specs=[FULL] * 3, out_specs=FULL)(hid, strip, gen_rows)
    rebuilt = jnp.transpose(rows[:, :variables], (1, 0, 2))
    feat_grad = jnp.transpose(feat, (1, 0, 2))

    half = (kept + swap_cores(sent).astype(F32)).astype(BF16)
    cut = (chips, 2 * PACK // chips // 2, 2, LANES)
    pieces = lax.all_to_all(half.reshape(cut), CHIPS, 0, 0, tiled=True).reshape(packed)
    spread = call(total_kernel, jax.ShapeDtypeStruct(packed, BF16), 10**7)(
        in_specs=[FULL], out_specs=FULL
    )(pieces)
    own = lax.all_to_all(spread.reshape(cut), CHIPS, 0, 0, tiled=True).reshape(packed)
    other = swap_cores(own)
    norm = (height * lat_count * width * lon_count) ** -0.5
    grad = jax.ShapeDtypeStruct((9, variables, channels), F32)
    enc, gen = call(
        functools.partial(final_kernel, norm), (grad, grad), 10**7, [pltpu.VMEM(packed, F32)]
    )(in_specs=[FLAGS, FULL, FULL], out_specs=(FULL, FULL))(flags, own, other)
    shape = (3, 3, variables, channels)
    return (rebuilt, feat_grad, jnp.swapaxes(enc.reshape(shape), 2, 3), gen.reshape(shape))


def solution(mesh):
    lat_count, lon_count = mesh.shape["lat"], mesh.shape["lon"]
    fine = Mesh(mesh.devices.reshape(lat_count // 2, 2, 2, lon_count // 4, 2), LAT + LON)
    return jax.shard_map(
        on_device,
        mesh=fine,
        in_specs=(P(None, LAT, LON), P(), P(), P(None, LAT, LON)),
        out_specs=(P(None, LAT, LON), P(None, LAT, LON), P(), P()),
        check_vma=False,
    )
```

time: 363 us -> 94.6 us (0.26)
  waiting for transfers between devices: 259 us -> 10.4 us
  blocking collectives: 0 us -> 48 us
  matrix products: 30 us -> 0 us
  starting transfers between devices: 34 us -> 12.3 us
  Pallas kernels: 0 us -> 17.9 us
  between operations: 15 us -> 0.75 us
  other arithmetic: 10.3 us -> 0.15 us
  local copies, waits for them, and re-layouts: 14.2 us -> 4.96 us
    psum x1 -> x0, waiting for transfers between devices: 255 us -> none  [sum_grads(): summed = lax.psum((enc_part, gen_part), ('lat', 'lon'))]
    all_to_all x0 -> x2, blocking collectives: none -> 48 us  [the longest x1 28.3 us: on_device(): lax.all_to_all(half.reshape(cut), CHIPS, 0, 0, tiled=True).reshape(packed)]
    dot_general x51 -> x0, matrix products: 30 us -> none  [the longest x18 18.3 us: convolve(): jnp.dot(kernel[row_tap, col_tap], section, preferred_element_type=jnp.flo...]
    ppermute x15 -> x6, starting transfers between devices: 34 us -> 12.3 us  [the longest x2 5.63 us: swap_cores(): return lax.ppermute(value, 'core', [(0, 1), (1, 0)])]
    pallas_call x0 -> x6, Pallas kernels: none -> 17.9 us  [the longest x1 9.63 us: on_device(): call(main_kernel, (jax.ShapeDtypeStruct((ROWS, channels, LANES), BF16), j...]
    ppermute x15 -> x6, waiting for transfers between devices: 3.62 us -> 10.4 us  [the longest x1 5.31 us: on_device(): pb = lax.ppermute(pb, LAT + LON, behind)]
    slice x21 -> x0, local copies, waits for them, and re-layouts: 6.5 us -> none  [the longest x11 4.17 us: convolve(): padded[:, row_tap:row_tap + height, col_tap:col_tap + width]]
    mul x2 -> x0, other arithmetic: 3.97 us -> none  [on_device(): return (rebuilt, feat_grad, enc_sum * norm_scale, gen_sum * norm_scale)]
  transfers between devices with their start and end apart: 16 -> 6, of which waited for: 3 -> 5; matrix products, arithmetic and copies ran while one was open for 8% -> 3% of each run, Pallas kernels for 0% -> 5%
where the time goes in v1:
time: 94.6 us; the launch traced here: 94.4 us
  blocking collectives  48 us (51%)
  Pallas kernels  17.9 us (19%)
  starting transfers between devices  12.3 us (13%)
  waiting for transfers between devices  10.4 us (11%)
  local copies, waits for them, and re-layouts  4.96 us (5%)
    all_to_all x1, blocking collectives, on_device(): lax.all_to_all(half.reshape(cut), CHIPS, 0, 0, tiled=True).reshape(packed)  28.3 us
    all_to_all x1, blocking collectives, on_device(): lax.all_to_all(spread.reshape(cut), CHIPS, 0, 0, tiled=True).reshape(packed)  19.7 us
    pallas_call x1, Pallas kernels, on_device(): call(main_kernel, (jax.ShapeDtypeStruct((ROWS, channels, LANES), BF16), j...  9.63 us
    ppermute x2, starting transfers between devices, swap_cores(): return lax.ppermute(value, 'core', [(0, 1), (1, 0)])  5.63 us
    ppermute x1, waiting for transfers between devices, on_device(): pb = lax.ppermute(pb, LAT + LON, behind)  5.31 us
    unnamed x8, local copies, waits for them, and re-layouts  4.48 us
    pallas_call x1, Pallas kernels, on_device(): call(rebuilt_kernel, plane, 10 ** 9, [pltpu.VMEM((ROWS + 2, TAPS, LANES),...  4.41 us
    ppermute x1, starting transfers between devices, on_device(): pa = lax.ppermute(pa, LAT + LON, ahead)  3.29 us
  transfers between devices with their start and end apart: 6, of which 5 were waited for; matrix products, arithmetic and copies ran while one was open for 3% of the time, Pallas kernels for 5%

profile of v1, /device:TPU:1, one launch (start us, length us, event | category | flops | bytes accessed | tf_op | source)
XLA Modules:
  0.0 94.4 jit_solution(5996301115201737781)
XLA Ops:
  0.6 1.0 %copy.23 = bf16[69,16,128]{2,0,1:T(8,128)(2,1)S(1)} copy(bf16[69,16,128]{2,1,0:T(8,128)(2,1)} %param.4) | data formatting | bytes 565248 | tf_op args[0]
  1.7 1.0 %copy.22 = bf16[69,16,128]{2,0,1:T(8,128)(2,1)S(1)} copy(bf16[69,16,128]{2,1,0:T(8,128)(2,1)} %param.7) | data formatting | bytes 565248 | tf_op args[3]
  2.7 0.0 copy-start
  2.8 0.0 copy-start.1
  2.8 0.4 shard_map.75
  3.2 2.6 %collective-permute-start = (bf16[8,1280]{1,0:T(8,128)(2,1)S(1)}, bf16[8,1280]{1,0:T(8,128)(2,1)S(1)}, u32[]{:S(2)}, u32[]{:S(2)}) collective-permute-start(bf16[8,1280]{1,0:T(8,128)(2,1)S(1)} %get-tuple-element.17), channel_id=1, source_target_pairs={{0,1},{1,2},{2,3},{3,4},{4,5},{5,6},{6,7},{7,8},{8,9},{9,10},{10,1... | collective-permute-start | bytes 61448 | tf_op jit(solution)/shard_map/ppermute | solution.py:334
  5.9 0.7 collective-permute-start.1
  6.6 0.1 pad_add_fusion.flags_ref
  6.7 0.5 collective-permute-done.east_ref
  7.2 1.9 %collective-permute-done.1.west_ref = bf16[8,1280]{1,0:T(8,128)(2,1)S(1)} collective-permute-done((bf16[8,1280]{1,0:T(8,128)(2,1)S(1)}, bf16[8,1280]{1,0:T(8,128)(2,1)S(1)}, u32[]{:S(2)}, u32[]{:S(2)}) %collective-permute-start.1) | collective-permute-done | bytes 20512 | tf_op jit(solution)/shard_map/ppermute | solution.py:335
  9.1 1.1 %shard_map.76 = (bf16[16,80,128]{2,1,0:T(8,128)(2,1)S(1)}, bf16[16,80,128]{2,1,0:T(8,128)(2,1)S(1)}, bf16[6,80,128]{2,1,0:T(8,128)(2,1)S(1)}, bf16[6,80,128]{2,1,0:T(8,128)(2,1)S(1)}) custom-call(s32[4]{0:T(128)S(1)} %pad_add_fusion.flags_ref, bf16[16,80,128]{2,1,0:T(8,128)(2,1)S(1)} %pad.14.x_ref, bf16[16,80,128]{2,1,0:T(8,128)(2,1)S(1)} %pad.15.r_ref, ...), custom_call_target="tpu_custom_call" | custom-call | flops 10000000 | bytes 20000 | tf_op jit(solution)/shard_map/pallas_call | solution.py:337
  10.2 3.3 %collective-permute-start.2 = (bf16[6,80,128]{2,1,0:T(8,128)(2,1)S(1)}, bf16[6,80,128]{2,1,0:T(8,128)(2,1)S(1)}, u32[]{:S(2)}, u32[]{:S(2)}) collective-permute-start(bf16[6,80,128]{2,1,0:T(8,128)(2,1)S(1)} %get-tuple-element.21), channel_id=1, source_target_pairs={{0,16},{1,17},{2,18},{3,19},{4,20},{5,21},{6,22},{7,23},{8,0},{9,1... | collective-permute-start | bytes 368648 | tf_op jit(solution)/shard_map/ppermute | solution.py:341
  13.5 0.0 collective-permute-start.3
  13.5 0.0 copy-done
  13.5 0.0 copy-done.1
  13.6 0.2 copy.16
  13.7 0.2 copy.17.gt_ref
  13.9 1.4 %collective-permute-done.2.pa_ref = bf16[6,80,128]{2,1,0:T(8,128)(2,1)S(1)} collective-permute-done((bf16[6,80,128]{2,1,0:T(8,128)(2,1)S(1)}, bf16[6,80,128]{2,1,0:T(8,128)(2,1)S(1)}, u32[]{:S(2)}, u32[]{:S(2)}) %collective-permute-start.2) | collective-permute-done | bytes 122912 | tf_op jit(solution)/shard_map/ppermute | solution.py:341
  15.4 5.3 %collective-permute-done.3.pb_ref = bf16[6,80,128]{2,1,0:T(8,128)(2,1)S(1)} collective-permute-done((bf16[6,80,128]{2,1,0:T(8,128)(2,1)S(1)}, bf16[6,80,128]{2,1,0:T(8,128)(2,1)S(1)}, u32[]{:S(2)}, u32[]{:S(2)}) %collective-permute-start.3) | collective-permute-done | bytes 122912 | tf_op jit(solution)/shard_map/ppermute | solution.py:342
  20.7 9.6 %shard_map.77 = (bf16[16,256,128]{2,1,0:T(8,128)(2,1)S(1)}, bf16[18,256,128]{2,1,0:T(8,128)(2,1)S(1)}, bf16[256,128]{1,0:T(8,128)(2,1)S(1)}, bf16[1280,128]{1,0:T(8,128)(2,1)S(1)}, f32[1280,128]{1,0:T(8,128)S(1)}) custom-call(s32[4]{0:T(128)S(1)} %pad_add_fusion.flags_ref, bf16[16,80,128]{2,1,0:T(8,128)(2,1)S(1)} %pad.14.x_ref, ...), custom_call_target="tpu_custom_call" | custom-call | flops 3000000000 | bytes 6000000 | tf_op jit(solution)/shard_map/pallas_call | solution.py:345
  30.3 1.7 %collective-permute-start.4 = (bf16[1280,128]{1,0:T(8,128)(2,1)S(1)}, bf16[1280,128]{1,0:T(8,128)(2,1)S(1)}, u32[]{:S(2)}, u32[]{:S(2)}) collective-permute-start(bf16[1280,128]{1,0:T(8,128)(2,1)S(1)} %get-tuple-element.27), channel_id=1, source_target_pairs={{0,1},{1,0},{2,3},{3,2},{4,5},{5,4},{6,7},{7,6},{8,9},{9,8},{10,11... | collective-permute-start | bytes 983048 | tf_op jit(solution)/shard_map/ppermute | solution.py:287
  32.0 1.3 %collective-permute-done.4 = bf16[1280,128]{1,0:T(8,128)(2,1)S(1)} collective-permute-done((bf16[1280,128]{1,0:T(8,128)(2,1)S(1)}, bf16[1280,128]{1,0:T(8,128)(2,1)S(1)}, u32[]{:S(2)}, u32[]{:S(2)}) %collective-permute-start.4) | collective-permute-done | bytes 327712 | tf_op jit(solution)/shard_map/ppermute | solution.py:287
  33.3 0.1 add_convert_fusion
  33.3 28.3 %all_to_all.10 = bf16[128,5,2,128]{3,2,1,0:T(2,128)(2,1)S(1)} all-to-all(bf16[128,5,2,128]{3,2,1,0:T(2,128)(2,1)S(1)} %bitcast.36), channel_id=1, replica_groups=mesh['z'=8,'y_hi'=2,'y_lo'=2,'x'=4,'core'=2] {'z','y_hi','y_lo','x'}, dimensions={0} | all-to-all | bytes 655360 | tf_op jit(solution)/shard_map/all_to_all | solution.py:378
  61.6 0.4 shard_map.79
  62.0 19.7 %all_to_all.11 = bf16[128,5,2,128]{3,2,1,0:T(2,128)(2,1)S(1)} all-to-all(bf16[128,5,2,128]{3,2,1,0:T(2,128)(2,1)S(1)} %bitcast.32), channel_id=1, replica_groups=mesh['z'=8,'y_hi'=2,'y_lo'=2,'x'=4,'core'=2] {'z','y_hi','y_lo','x'}, dimensions={0} | all-to-all | bytes 655360 | tf_op jit(solution)/shard_map/all_to_all | solution.py:382
  81.7 3.9 %collective-permute-start.5 = (bf16[1280,128]{1,0:T(8,128)(2,1)S(1)}, bf16[1280,128]{1,0:T(8,128)(2,1)S(1)}, u32[]{:S(2)}, u32[]{:S(2)}) collective-permute-start(bf16[1280,128]{1,0:T(8,128)(2,1)S(1)} %bitcast.29), channel_id=1, source_target_pairs={{0,1},{1,0},{2,3},{3,2},{4,5},{5,4},{6,7},{7,6},{8,9},{9,8},{10,11... | collective-permute-start | bytes 983048 | tf_op jit(solution)/shard_map/ppermute | solution.py:287
  85.7 4.4 %shard_map.78 = bf16[16,80,128]{2,1,0:T(8,128)(2,1)S(1)} custom-call(bf16[18,256,128]{2,1,0:T(8,128)(2,1)S(1)} %get-tuple-element.23.hid_ref, bf16[256,128]{1,0:T(8,128)(2,1)S(1)} %get-tuple-element.24.strip_ref, bf16[720,256]{1,0:T(8,128)(2,1)S(1)} %bitcast.28), custom_call_target="tpu_custom_call" | custom-call | flops 1000000000 | bytes 2000000 | tf_op jit(solution)/shard_map/pallas_call | solution.py:367
  90.1 0.7 copy.18
  90.9 1.6 %copy.19 = bf16[256,16,128]{2,1,0:T(8,128)(2,1)} copy(bf16[256,16,128]{2,0,1:T(8,128)(2,1)S(1)} %bitcast.33) | data formatting | bytes 2097152
  92.5 0.0 collective-permute-done.5.other_ref
  92.5 1.9 %shard_map.80 = (f32[9,69,256]{2,1,0:T(8,128)}, f32[9,69,256]{2,1,0:T(8,128)}) custom-call(s32[4]{0:T(128)S(1)} %pad_add_fusion.flags_ref, bf16[1280,128]{1,0:T(8,128)(2,1)S(1)} %bitcast.30, bf16[1280,128]{1,0:T(8,128)(2,1)S(1)} %collective-permute-done.5.other_ref), custom_call_target="tpu_custom_call" | custom-call | flops 10000000 | bytes 20000 | tf_op jit(solution)/shard_map/pallas_call | solution.py:386
  (5 shorter events, 0.1 us)
Async XLA Ops:
  2.7 10.8 %copy-start = (bf16[3,3,69,256]{3,2,1,0:T(8,128)(2,1)S(1)}, bf16[3,3,69,256]{3,2,1,0:T(8,128)(2,1)}, u32[]{:S(2)}) copy-start(bf16[3,3,69,256]{3,2,1,0:T(8,128)(2,1)} %param.6) | copy-start | bytes 953860
  2.8 10.7 %copy-start.1 = (bf16[3,3,256,69]{2,3,1,0:T(8,128)(2,1)S(1)}, bf16[3,3,256,69]{2,3,1,0:T(8,128)(2,1)}, u32[]{:S(2)}) copy-start(bf16[3,3,256,69]{2,3,1,0:T(8,128)(2,1)} %param.5) | copy-start | bytes 953860
  3.2 3.9 %collective-permute-start = (bf16[8,1280]{1,0:T(8,128)(2,1)S(1)}, bf16[8,1280]{1,0:T(8,128)(2,1)S(1)}, u32[]{:S(2)}, u32[]{:S(2)}) collective-permute-start(bf16[8,1280]{1,0:T(8,128)(2,1)S(1)} %get-tuple-element.17), channel_id=1, source_target_pairs={{0,1},{1,2},{2,3},{3,4},{4,5},{5,6},{6,7},{7,8},{8,9},{9,10},{10,1... | collective-permute-start | bytes 61448 | tf_op jit(solution)/shard_map/ppermute | solution.py:334
  5.9 3.2 %collective-permute-start.1 = (bf16[8,1280]{1,0:T(8,128)(2,1)S(1)}, bf16[8,1280]{1,0:T(8,128)(2,1)S(1)}, u32[]{:S(2)}, u32[]{:S(2)}) collective-permute-start(bf16[8,1280]{1,0:T(8,128)(2,1)S(1)} %get-tuple-element.18), channel_id=1, source_target_pairs={{1,0},{2,1},{3,2},{4,3},{5,4},{6,5},{7,6},{8,7},{9,8},{10,9},{11,1... | collective-permute-start | bytes 61448 | tf_op jit(solution)/shard_map/ppermute | solution.py:335
  10.2 5.2 %collective-permute-start.2 = (bf16[6,80,128]{2,1,0:T(8,128)(2,1)S(1)}, bf16[6,80,128]{2,1,0:T(8,128)(2,1)S(1)}, u32[]{:S(2)}, u32[]{:S(2)}) collective-permute-start(bf16[6,80,128]{2,1,0:T(8,128)(2,1)S(1)} %get-tuple-element.21), channel_id=1, source_target_pairs={{0,16},{1,17},{2,18},{3,19},{4,20},{5,21},{6,22},{7,23},{8,0},{9,1... | collective-permute-start | bytes 368648 | tf_op jit(solution)/shard_map/ppermute | solution.py:341
  13.5 7.2 %collective-permute-start.3 = (bf16[6,80,128]{2,1,0:T(8,128)(2,1)S(1)}, bf16[6,80,128]{2,1,0:T(8,128)(2,1)S(1)}, u32[]{:S(2)}, u32[]{:S(2)}) collective-permute-start(bf16[6,80,128]{2,1,0:T(8,128)(2,1)S(1)} %get-tuple-element.22), channel_id=1, source_target_pairs={{16,0},{17,1},{18,2},{19,3},{20,4},{21,5},{22,6},{23,7},{0,8},{1,9... | collective-permute-start | bytes 368648 | tf_op jit(solution)/shard_map/ppermute | solution.py:342
  30.3 3.0 %collective-permute-start.4 = (bf16[1280,128]{1,0:T(8,128)(2,1)S(1)}, bf16[1280,128]{1,0:T(8,128)(2,1)S(1)}, u32[]{:S(2)}, u32[]{:S(2)}) collective-permute-start(bf16[1280,128]{1,0:T(8,128)(2,1)S(1)} %get-tuple-element.27), channel_id=1, source_target_pairs={{0,1},{1,0},{2,3},{3,2},{4,5},{5,4},{6,7},{7,6},{8,9},{9,8},{10,11... | collective-permute-start | bytes 983048 | tf_op jit(solution)/shard_map/ppermute | solution.py:287
  81.7 10.8 %collective-permute-start.5 = (bf16[1280,128]{1,0:T(8,128)(2,1)S(1)}, bf16[1280,128]{1,0:T(8,128)(2,1)S(1)}, u32[]{:S(2)}, u32[]{:S(2)}) collective-permute-start(bf16[1280,128]{1,0:T(8,128)(2,1)S(1)} %bitcast.29), channel_id=1, source_target_pairs={{0,1},{1,0},{2,3},{3,2},{4,5},{5,4},{6,7},{7,6},{8,9},{9,8},{10,11... | collective-permute-start | bytes 983048 | tf_op jit(solution)/shard_map/ppermute | solution.py:287

commit v2 on v1

--- a/solution.py
+++ b/solution.py
@@ -8,13 +8,14 @@
 from jax.sharding import Mesh
 from jax.sharding import PartitionSpec as P
 
-CHIPS = ("z", "y_hi", "y_lo", "x")
+FACE = ("y_hi", "y_lo", "x")
 LAT = ("z", "y_hi")
 LON = ("y_lo", "x", "core")
 
 LANES = 128
 ROWS = 16
 DEEP = 80
+SENT = 72
 BAND = 3 * DEEP
 TAPS = 3 * BAND
 PACK = 640
@@ -34,7 +35,7 @@
     return lax.dot_general(a, b, dims, preferred_element_type=F32)
 
 
-def call(kernel, outs, cost, scratch=(), limit=48):
+def call(kernel, outs, cost, scratch=(), limit=8):
     return functools.partial(
         pl.pallas_call,
         kernel,
@@ -58,7 +59,13 @@
     return jnp.where(hot, 1.0, 0.0).astype(BF16)
 
 
-def columns_kernel(x_ref, r_ref, east_ref, west_ref):
+def columns_kernel(fields_ref, cot_ref, x_ref, r_ref, east_ref, west_ref, raw_s):
+    for source, target in ((fields_ref, x_ref), (cot_ref, r_ref)):
+        size = source.shape[0] * ROWS
+        raw_s[:size, :] = source[...].astype(F32).reshape(size, LANES)
+        raw_s[size:, :] = jnp.zeros((raw_s.shape[0] - size, LANES), F32)
+        for row in range(ROWS):
+            target[row] = raw_s[pl.ds(row, DEEP, stride=ROWS), :].astype(BF16)
     x = x_ref[...].reshape(ROWS * DEEP, LANES)
     r = r_ref[...].reshape(ROWS * DEEP, LANES)
     east = dot(picks([(0, 126), (1, 127)]), x, NT) + dot(picks([(2, 127)]), r, NT)
@@ -75,11 +82,15 @@
     hr = dot(left, picks([(2, 127)])) + dot(right, picks([(2, 0)]))
     hx_ref[...] = hx.astype(BF16).reshape(ROWS, DEEP, LANES)
     hr_ref[...] = hr.astype(BF16).reshape(ROWS, DEEP, LANES)
-    top = (x_ref[0], x_ref[1], r_ref[0], hx_ref[0], hx_ref[1], hr_ref[0])
-    end = ROWS - 1
-    bottom = (x_ref[end], x_ref[end - 1], r_ref[end], hx_ref[end], hx_ref[end - 1], hr_ref[end])
-    for k in range(6):
-        t, b = top[k].astype(F32), bottom[k].astype(F32)
+
+    def packet(edge, inner):
+        own = [x_ref[edge].astype(F32), x_ref[inner].astype(F32), r_ref[edge].astype(F32)]
+        sides = hx_ref[edge].astype(F32) + pltpu.roll(hx_ref[inner].astype(F32), 4, 1)
+        return own + [sides + pltpu.roll(hr_ref[edge].astype(F32), 8, 1)]
+
+    top, bottom = packet(0, 1), packet(ROWS - 1, ROWS - 2)
+    for k in range(4):
+        t, b = top[k][:SENT], bottom[k][:SENT]
         a_ref[k] = jnp.where(low, b, t).astype(BF16)
         b_ref[k] = jnp.where(low, t, b).astype(BF16)
 
@@ -130,10 +141,19 @@
         return carry
 
     lax.fori_loop(0, ROWS, fill, 0)
-    pa = [pa_ref[k].astype(F32) for k in range(6)]
-    pb = [pb_ref[k].astype(F32) for k in range(6)]
-    up = [jnp.where(low, a, b) for a, b in zip(pa, pb)]
-    down = [jnp.where(low, b, a) for a, b in zip(pa, pb)]
+    blank = jnp.zeros((DEEP - SENT, LANES), F32)
+
+    def unpack(first, second):
+        cells = [
+            jnp.concatenate(
+                [jnp.where(low, first[k].astype(F32), second[k].astype(F32)), blank], axis=0
+            )
+            for k in range(4)
+        ]
+        sides = [pltpu.roll(cells[3], LANES - turn, 1) for turn in (4, 8)]
+        return cells + sides
+
+    up, down = unpack(pa_ref, pb_ref), unpack(pb_ref, pa_ref)
     put_field(1, up[0], up[3])
     put_field(0, up[1], up[4])
     put_field(ROWS + 2, down[0], down[3])
@@ -222,7 +242,7 @@
     pack(core, kept_ref)
 
 
-def rebuilt_kernel(hid_ref, strip_ref, ga_ref, out_ref, z_s, t_s):
+def rebuilt_kernel(hid_ref, strip_ref, ga_ref, out_ref, z_s, t_s, out_s):
     ga = ga_ref[...]
     zs = dot(ga, strip_ref[...])
     t0 = zs[:DEEP]
@@ -255,20 +275,27 @@
         out = out + jnp.where(lane == LANES - 1, 0.0, pltpu.roll(sums[2], LANES - 1, 1))
         side = pltpu.roll(t_s[...], LANES - 1 - 2 * row, 1)
         out = out + jnp.where((lane == 0) | (lane == LANES - 1), side, 0.0)
-        out_ref[row] = out.astype(BF16)
+        out_s[pl.ds(row, DEEP, stride=ROWS), :] = out
         return carry
 
     lax.fori_loop(0, ROWS, emit, 0)
+    size = out_ref.shape[0] * ROWS
+    out_ref[...] = out_s[:size, :].reshape(out_ref.shape).astype(BF16)
+
+
+def turn_kernel(rows_ref, out_ref, out_s):
+    for row in range(ROWS):
+        out_s[pl.ds(row, out_ref.shape[0], stride=ROWS), :] = rows_ref[row].astype(F32)
+    out_ref[...] = out_s[...].reshape(out_ref.shape).astype(BF16)
 
 
 def total_kernel(pieces_ref, out_ref):
-    count = pieces_ref.shape[0]
-    group = count // 128
-    rows = lax.broadcasted_iota(jnp.int32, (16, count), 0)
-    cells = lax.broadcasted_iota(jnp.int32, (16, count), 1)
-    hot = jnp.where(lax.rem(cells, group) == rows, 1.0, 0.0).astype(BF16)
-    total = dot(hot, pieces_ref[...]).astype(BF16)
-    out_ref[...] = dot(hot, total, TN).astype(BF16)
+    total = pieces_ref[0].astype(F32)
+    for k in range(1, pieces_ref.shape[0]):
+        total = total + pieces_ref[k].astype(F32)
+    total = total.astype(BF16)
+    for k in range(out_ref.shape[0]):
+        out_ref[k] = total
 
 
 def final_kernel(norm, flags_ref, own_ref, other_ref, enc_ref, gen_ref, pack_s):
@@ -287,10 +314,6 @@
     return lax.ppermute(value, "core", [(0, 1), (1, 0)])
 
 
-def planes(v):
-    return jnp.pad(jnp.transpose(v, (1, 0, 2)), ((0, 0), (0, DEEP - v.shape[0]), (0, 0)))
-
-
 def great_circles(lat_count, lon_count):
     pairs = []
     for la in range(lat_count):
@@ -308,7 +331,6 @@
     channels = gen_kernel.shape[3]
     lat_index, lat_count = lax.axis_index(LAT), lax.axis_size(LAT)
     lon_count = lax.axis_size(LON)
-    chips = lax.axis_size(CHIPS)
     core = lax.axis_index("core")
     low = lax.axis_index("y_lo") == 0
     flags = jnp.stack(
@@ -322,18 +344,16 @@
     pad = ((0, 0), (0, 0), (0, DEEP - variables), (0, 0))
     gen_rows = jnp.pad(gen_kernel, pad).reshape(TAPS, channels)
     enc_rows = jnp.pad(jnp.swapaxes(enc_kernel, 2, 3), pad).reshape(TAPS, channels)
-    x, r = planes(fields), planes(recon_grad)
-
     plane = jax.ShapeDtypeStruct((ROWS, DEEP, LANES), BF16)
     side = jax.ShapeDtypeStruct((8, ROWS * DEEP), BF16)
-    east, west = call(columns_kernel, (side, side), 10**7)(
-        in_specs=[FULL] * 2, out_specs=(FULL, FULL)
-    )(x, r)
+    x, r, east, west = call(
+        columns_kernel, (plane, plane, side, side), 10**7, [pltpu.VMEM((ROWS * DEEP, LANES), F32)]
+    )(in_specs=[FULL] * 2, out_specs=(FULL,) * 4)(fields, recon_grad)
     right = [(i, (i + 1) % lon_count) for i in range(lon_count)]
     left = [(b, a) for a, b in right]
     from_left = lax.ppermute(east, LON, right)
     from_right = lax.ppermute(west, LON, left)
-    packet = jax.ShapeDtypeStruct((6, DEEP, LANES), BF16)
+    packet = jax.ShapeDtypeStruct((4, SENT, LANES), BF16)
     hx, hr, pa, pb = call(rows_kernel, (plane, plane, packet, packet), 10**7)(
         in_specs=[FLAGS] + [FULL] * 4, out_specs=(FULL,) * 4
     )(flags, x, r, from_left, from_right)
@@ -361,25 +381,45 @@
             pltpu.VMEM((2, TAPS, channels), F32),
             pltpu.VMEM((PACK + 8, channels), F32),
         ],
+        24,
     )(in_specs=[FLAGS] + [FULL] * 8, out_specs=(FULL,) * 5)(
         flags, x, r, hx, hr, pa, pb, enc_rows.T, gen_rows.T
     )
-    rows = call(
+    rebuilt = call(
         rebuilt_kernel,
-        plane,
-        10**9,
-        [pltpu.VMEM((ROWS + 2, TAPS, LANES), F32), pltpu.VMEM((DEEP, LANES), F32)],
+        jax.ShapeDtypeStruct((variables, height, width), BF16),
+        4 * 10**9,
+        [
+            pltpu.VMEM((ROWS + 2, TAPS, LANES), F32),
+            pltpu.VMEM((DEEP, LANES), F32),
+            pltpu.VMEM((DEEP * ROWS, LANES), F32),
+        ],
+        12,
     )(in_specs=[FULL] * 3, out_specs=FULL)(hid, strip, gen_rows)
-    rebuilt = jnp.transpose(rows[:, :variables], (1, 0, 2))
-    feat_grad = jnp.transpose(feat, (1, 0, 2))
+    feat_grad = call(
+        turn_kernel,
+        jax.ShapeDtypeStruct((channels, height, width), BF16),
+        2 * 10**9,
+        [pltpu.VMEM((channels * ROWS, LANES), F32)],
+    )(in_specs=[FULL], out_specs=FULL)(feat)
 
     half = (kept + swap_cores(sent).astype(F32)).astype(BF16)
-    cut = (chips, 2 * PACK // chips // 2, 2, LANES)
-    pieces = lax.all_to_all(half.reshape(cut), CHIPS, 0, 0, tiled=True).reshape(packed)
-    spread = call(total_kernel, jax.ShapeDtypeStruct(packed, BF16), 10**7)(
-        in_specs=[FULL], out_specs=FULL
-    )(pieces)
-    own = lax.all_to_all(spread.reshape(cut), CHIPS, 0, 0, tiled=True).reshape(packed)
+    faces, layers = lax.axis_size(FACE), lax.axis_size("z")
+    piece = (2 * PACK // faces, LANES)
+
+    def exchange(value, axes):
+        return lax.all_to_all(value, axes, 0, 0, tiled=True)
+
+    def total(pieces, copies):
+        return call(total_kernel, jax.ShapeDtypeStruct((copies,) + piece, BF16), 10**7)(
+            in_specs=[FULL], out_specs=FULL
+        )(pieces)
+
+    pieces = exchange(half.reshape((faces,) + piece), FACE)
+    pieces, rebuilt = lax.optimization_barrier((pieces, rebuilt))
+    pieces = exchange(total(pieces, layers), "z")
+    pieces, feat_grad = lax.optimization_barrier((pieces, feat_grad))
+    own = exchange(total(pieces, faces), FACE).reshape(packed)
     other = swap_cores(own)
     norm = (height * lat_count * width * lon_count) ** -0.5
     grad = jax.ShapeDtypeStruct((9, variables, channels), F32)

time: 94.6 us -> 83.8 us (0.89)
  blocking collectives: 48 us -> 10.6 us
  starting transfers between devices: 12.3 us -> 26.7 us
  waiting for transfers between devices: 10.4 us -> 19.1 us
  Pallas kernels: 17.9 us -> 22.1 us
  local copies, waits for them, and re-layouts: 4.96 us -> 3.36 us
    all_to_all x2 -> x1, blocking collectives: 48 us -> 10.6 us  [exchange(): return lax.all_to_all(value, axes, 0, 0, tiled=True)]
    all_to_all x0 -> x2, starting transfers between devices: none -> 13.9 us  [exchange(): return lax.all_to_all(value, axes, 0, 0, tiled=True)]
    all_to_all x0 -> x2, waiting for transfers between devices: none -> 9.91 us  [exchange(): return lax.all_to_all(value, axes, 0, 0, tiled=True)]
    pallas_call x3 -> x5, Pallas kernels: 5.24 us -> 9.36 us  [the longest x1 5.34 us: on_device(): call(rebuilt_kernel, jax.ShapeDtypeStruct((variables, height, width), BF1...]
    ppermute x1, waiting for transfers between devices: 5.31 us -> 3.3 us  [on_device(): pb = lax.ppermute(pb, LAT + LON, behind)]
    unnamed x8 -> x16, local copies, waits for them, and re-layouts: 4.48 us -> 2.96 us
    ppermute x2, waiting for transfers between devices: 1.26 us -> 2.51 us  [swap_cores(): return lax.ppermute(value, 'core', [(0, 1), (1, 0)])]
  transfers between devices with their start and end apart: 6 -> 8, of which waited for: 5 -> 8; matrix products, arithmetic and copies ran while one was open for 3% -> 1% of each run, Pallas kernels for 5% -> 9%
where the time goes in v2:
time: 83.8 us; the launch traced here: 83.4 us
  starting transfers between devices  26.7 us (32%)
  Pallas kernels  22.1 us (26%)
  waiting for transfers between devices  19.1 us (23%)
  blocking collectives  10.6 us (13%)
  local copies, waits for them, and re-layouts  3.36 us (4%)
  other arithmetic  0.88 us (1%)
    all_to_all x2, starting transfers between devices, exchange(): return lax.all_to_all(value, axes, 0, 0, tiled=True)  13.9 us
    all_to_all x1, blocking collectives, exchange(): return lax.all_to_all(value, axes, 0, 0, tiled=True)  10.6 us
    all_to_all x2, waiting for transfers between devices, exchange(): return lax.all_to_all(value, axes, 0, 0, tiled=True)  9.91 us
    pallas_call x1, Pallas kernels, on_device(): call(main_kernel, (jax.ShapeDtypeStruct((ROWS, channels, LANES), BF16), j...  9.64 us
    ppermute x2, starting transfers between devices, swap_cores(): return lax.ppermute(value, 'core', [(0, 1), (1, 0)])  6.1 us
    pallas_call x1, Pallas kernels, on_device(): call(rebuilt_kernel, jax.ShapeDtypeStruct((variables, height, width), BF1...  5.34 us
    ppermute x1, waiting for transfers between devices, on_device(): pb = lax.ppermute(pb, LAT + LON, behind)  3.3 us
    ppermute x1, starting transfers between devices, on_device(): pa = lax.ppermute(pa, LAT + LON, ahead)  3.29 us
  transfers between devices with their start and end apart: 8, of which 8 were waited for; matrix products, arithmetic and copies ran while one was open for 1% of the time, Pallas kernels for 9%

profile of v2, /device:TPU:1, one launch (start us, length us, event | category | flops | bytes accessed | tf_op | source)
XLA Modules:
  0.0 83.4 jit_solution(5869019583023320876)
XLA Ops:
  0.6 0.9 %copy-done = bf16[69,16,128]{2,1,0:T(8,128)(2,1)S(1)} copy-done((bf16[69,16,128]{2,1,0:T(8,128)(2,1)S(1)}, bf16[69,16,128]{2,1,0:T(8,128)(2,1)}, u32[]{:S(2)}) %copy-start) | copy-done | bytes 282648
  1.6 1.0 %copy-done.1 = bf16[69,16,128]{2,1,0:T(8,128)(2,1)S(1)} copy-done((bf16[69,16,128]{2,1,0:T(8,128)(2,1)S(1)}, bf16[69,16,128]{2,1,0:T(8,128)(2,1)}, u32[]{:S(2)}) %copy-start.1) | copy-done | bytes 282648
  2.6 1.1 %shard_map.75 = (bf16[16,80,128]{2,1,0:T(8,128)(2,1)S(1)}, bf16[16,80,128]{2,1,0:T(8,128)(2,1)S(1)}, bf16[8,1280]{1,0:T(8,128)(2,1)S(1)}, bf16[8,1280]{1,0:T(8,128)(2,1)S(1)}) custom-call(bf16[69,16,128]{2,1,0:T(8,128)(2,1)S(1)} %copy-done, bf16[69,16,128]{2,1,0:T(8,128)(2,1)S(1)} %copy-done.1), custom_call_target="tpu_custom_call" | custom-call | flops 10000000 | bytes 20000 | tf_op jit(solution)/shard_map/pallas_call | solution.py:349
  3.7 2.7 %collective-permute-start = (bf16[8,1280]{1,0:T(8,128)(2,1)S(1)}, bf16[8,1280]{1,0:T(8,128)(2,1)S(1)}, u32[]{:S(2)}, u32[]{:S(2)}) collective-permute-start(bf16[8,1280]{1,0:T(8,128)(2,1)S(1)} %get-tuple-element.25), channel_id=1, source_target_pairs={{0,1},{1,2},{2,3},{3,4},{4,5},{5,6},{6,7},{7,8},{8,9},{9,10},{10,1... | collective-permute-start | bytes 61448 | tf_op jit(solution)/shard_map/ppermute | solution.py:354
  6.3 0.7 collective-permute-start.1
  7.1 0.1 pad_add_fusion.flags_ref
  7.1 0.5 collective-permute-done.east_ref
  7.7 1.9 %collective-permute-done.1.west_ref = bf16[8,1280]{1,0:T(8,128)(2,1)S(1)} collective-permute-done((bf16[8,1280]{1,0:T(8,128)(2,1)S(1)}, bf16[8,1280]{1,0:T(8,128)(2,1)S(1)}, u32[]{:S(2)}, u32[]{:S(2)}) %collective-permute-start.1) | collective-permute-done | bytes 20512 | tf_op jit(solution)/shard_map/ppermute | solution.py:355
  9.5 1.2 %shard_map.76 = (bf16[16,80,128]{2,1,0:T(8,128)(2,1)S(1)}, bf16[16,80,128]{2,1,0:T(8,128)(2,1)S(1)}, bf16[4,72,128]{2,1,0:T(8,128)(2,1)S(1)}, bf16[4,72,128]{2,1,0:T(8,128)(2,1)S(1)}) custom-call(s32[4]{0:T(128)S(1)} %pad_add_fusion.flags_ref, bf16[16,80,128]{2,1,0:T(8,128)(2,1)S(1)} %get-tuple-element.23.x_ref, ...), custom_call_target="tpu_custom_call" | custom-call | flops 10000000 | bytes 20000 | tf_op jit(solution)/shard_map/pallas_call | solution.py:357
  10.7 3.3 %collective-permute-start.2 = (bf16[4,72,128]{2,1,0:T(8,128)(2,1)S(1)}, bf16[4,72,128]{2,1,0:T(8,128)(2,1)S(1)}, u32[]{:S(2)}, u32[]{:S(2)}) collective-permute-start(bf16[4,72,128]{2,1,0:T(8,128)(2,1)S(1)} %get-tuple-element.29), channel_id=1, source_target_pairs={{0,16},{1,17},{2,18},{3,19},{4,20},{5,21},{6,22},{7,23},{8,0},{9,1... | collective-permute-start | bytes 221192 | tf_op jit(solution)/shard_map/ppermute | solution.py:361
  14.0 0.0 collective-permute-start.3
  14.1 0.2 copy.10
  14.3 0.2 copy.11.gt_ref
  14.5 1.0 %collective-permute-done.2.pa_ref = bf16[4,72,128]{2,1,0:T(8,128)(2,1)S(1)} collective-permute-done((bf16[4,72,128]{2,1,0:T(8,128)(2,1)S(1)}, bf16[4,72,128]{2,1,0:T(8,128)(2,1)S(1)}, u32[]{:S(2)}, u32[]{:S(2)}) %collective-permute-start.2) | collective-permute-done | bytes 73760 | tf_op jit(solution)/shard_map/ppermute | solution.py:361
  15.4 3.3 %collective-permute-done.3.pb_ref = bf16[4,72,128]{2,1,0:T(8,128)(2,1)S(1)} collective-permute-done((bf16[4,72,128]{2,1,0:T(8,128)(2,1)S(1)}, bf16[4,72,128]{2,1,0:T(8,128)(2,1)S(1)}, u32[]{:S(2)}, u32[]{:S(2)}) %collective-permute-start.3) | collective-permute-done | bytes 73760 | tf_op jit(solution)/shard_map/ppermute | solution.py:362
  18.7 9.6 %shard_map.77 = (bf16[16,256,128]{2,1,0:T(8,128)(2,1)S(1)}, bf16[18,256,128]{2,1,0:T(8,128)(2,1)S(1)}, bf16[256,128]{1,0:T(8,128)(2,1)S(1)}, bf16[1280,128]{1,0:T(8,128)(2,1)S(1)}, f32[1280,128]{1,0:T(8,128)S(1)}) custom-call(s32[4]{0:T(128)S(1)} %pad_add_fusion.flags_ref, bf16[16,80,128]{2,1,0:T(8,128)(2,1)S(1)} %get-tuple-element.23.x_ref, ...), custom_call_target="tpu_custom_call" | custom-call | flops 3000000000 | bytes 6000000 | tf_op jit(solution)/shard_map/pallas_call | solution.py:365
  28.4 1.0 %copy-done.4 = bf16[18,256,128]{2,1,0:T(8,128)(2,1)} copy-done((bf16[18,256,128]{2,1,0:T(8,128)(2,1)}, bf16[18,256,128]{2,1,0:T(8,128)(2,1)S(1)}, u32[]{:S(2)}) %copy-start.4) | copy-done | bytes 1179672
  29.4 2.2 %collective-permute-start.4 = (bf16[1280,128]{1,0:T(8,128)(2,1)S(1)}, bf16[1280,128]{1,0:T(8,128)(2,1)S(1)}, u32[]{:S(2)}, u32[]{:S(2)}) collective-permute-start(bf16[1280,128]{1,0:T(8,128)(2,1)S(1)} %get-tuple-element.32), channel_id=1, source_target_pairs={{0,1},{1,0},{2,3},{3,2},{4,5},{5,4},{6,7},{7,6},{8,9},{9,8},{10,11... | collective-permute-start | bytes 983048 | tf_op jit(solution)/shard_map/ppermute | solution.py:314
  31.6 1.3 %collective-permute-done.4 = bf16[1280,128]{1,0:T(8,128)(2,1)S(1)} collective-permute-done((bf16[1280,128]{1,0:T(8,128)(2,1)S(1)}, bf16[1280,128]{1,0:T(8,128)(2,1)S(1)}, u32[]{:S(2)}, u32[]{:S(2)}) %collective-permute-start.4) | collective-permute-done | bytes 327712 | tf_op jit(solution)/shard_map/ppermute | solution.py:314
  32.9 0.8 add_convert_fusion
  33.7 5.9 %all-to-all-start = ((bf16[16,80,128]{2,1,0:T(8,128)(2,1)}), bf16[16,80,128]{2,1,0:T(8,128)(2,1)S(1)}, u32[]{:S(2)}, u32[]{:S(2)}) async-start(bf16[16,80,128]{2,1,0:T(8,128)(2,1)} %bitcast.9), calls=%async_computation | async-start | bytes 655360 | tf_op jit(solution)/shard_map/all_to_all | solution.py:411
  39.6 0.0 copy-start.3
  39.6 5.3 %shard_map.78 = bf16[69,16,128]{2,1,0:T(8,128)(2,1)} custom-call(bf16[18,256,128]{2,1,0:T(8,128)(2,1)S(1)} %copy-done.5, bf16[256,128]{1,0:T(8,128)(2,1)S(1)} %get-tuple-element.34.strip_ref, bf16[720,256]{1,0:T(8,128)(2,1)S(1)} %bitcast.17), custom_call_target="tpu_custom_call" | custom-call | flops 4000000000 | bytes 8000000 | tf_op jit(solution)/shard_map/pallas_call | solution.py:388
  45.0 3.7 %all-to-all-done.pieces_ref = bf16[16,80,128]{2,1,0:T(8,128)(2,1)S(1)} async-done(((bf16[16,80,128]{2,1,0:T(8,128)(2,1)}), bf16[16,80,128]{2,1,0:T(8,128)(2,1)S(1)}, u32[]{:S(2)}, u32[]{:S(2)}) %all-to-all-start) | async-done | bytes 327712 | tf_op jit(solution)/shard_map/all_to_all | solution.py:411
  48.7 0.7 shard_map.79
  49.4 8.0 %all-to-all-start.1 = ((bf16[8,80,128]{2,1,0:T(8,128)(2,1)}), bf16[8,80,128]{2,1,0:T(8,128)(2,1)S(1)}, u32[]{:S(2)}, u32[]{:S(2)}) async-start(bf16[8,80,128]{2,1,0:T(8,128)(2,1)} %shard_map.79), calls=%async_computation.1 | async-start | bytes 327680 | tf_op jit(solution)/shard_map/all_to_all | solution.py:411
  57.4 2.2 %shard_map.80 = bf16[256,16,128]{2,1,0:T(8,128)(2,1)} custom-call(bf16[16,256,128]{2,1,0:T(8,128)(2,1)S(1)} %copy-done.3), custom_call_target="tpu_custom_call" | custom-call | flops 2000000000 | bytes 4000000 | tf_op jit(solution)/shard_map/pallas_call | solution.py:399
  59.6 6.2 %all-to-all-done.1.pieces_ref = bf16[8,80,128]{2,1,0:T(8,128)(2,1)S(1)} async-done(((bf16[8,80,128]{2,1,0:T(8,128)(2,1)}), bf16[8,80,128]{2,1,0:T(8,128)(2,1)S(1)}, u32[]{:S(2)}, u32[]{:S(2)}) %all-to-all-start.1) | async-done | bytes 163872 | tf_op jit(solution)/shard_map/all_to_all | solution.py:411
  65.8 10.6 %all_to_all.15 = bf16[16,80,128]{2,1,0:T(8,128)(2,1)S(1)} all-to-all(bf16[16,80,128]{2,1,0:T(8,128)(2,1)S(1)} %shard_map.81), channel_id=1, replica_groups=mesh['z'=8,'y_hi'=2,'y_lo'=2,'x'=4,'core'=2] {'y_hi','y_lo','x'}, dimensions={0} | all-to-all | bytes 655360 | tf_op jit(solution)/shard_map/all_to_all | solution.py:411
  76.4 3.9 %collective-permute-start.5 = (bf16[1280,128]{1,0:T(8,128)(2,1)S(1)}, bf16[1280,128]{1,0:T(8,128)(2,1)S(1)}, u32[]{:S(2)}, u32[]{:S(2)}) collective-permute-start(bf16[1280,128]{1,0:T(8,128)(2,1)S(1)} %bitcast.18), channel_id=1, source_target_pairs={{0,1},{1,0},{2,3},{3,2},{4,5},{5,4},{6,7},{7,6},{8,9},{9,8},{10,11... | collective-permute-start | bytes 983048 | tf_op jit(solution)/shard_map/ppermute | solution.py:314
  80.3 1.3 %collective-permute-done.5.other_ref = bf16[1280,128]{1,0:T(8,128)(2,1)S(1)} collective-permute-done((bf16[1280,128]{1,0:T(8,128)(2,1)S(1)}, bf16[1280,128]{1,0:T(8,128)(2,1)S(1)}, u32[]{:S(2)}, u32[]{:S(2)}) %collective-permute-start.5) | collective-permute-done | bytes 327712 | tf_op jit(solution)/shard_map/ppermute | solution.py:314
  81.6 1.9 %shard_map.82 = (f32[9,69,256]{2,1,0:T(8,128)}, f32[9,69,256]{2,1,0:T(8,128)}) custom-call(s32[4]{0:T(128)S(1)} %pad_add_fusion.flags_ref, bf16[1280,128]{1,0:T(8,128)(2,1)S(1)} %bitcast.19, bf16[1280,128]{1,0:T(8,128)(2,1)S(1)} %collective-permute-done.5.other_ref), custom_call_target="tpu_custom_call" | custom-call | flops 10000000 | bytes 20000 | tf_op jit(solution)/shard_map/pallas_call | solution.py:426
  (15 shorter events, 0.1 us)
Async XLA Ops:
  0.6 1.0 %copy-start = (bf16[69,16,128]{2,1,0:T(8,128)(2,1)S(1)}, bf16[69,16,128]{2,1,0:T(8,128)(2,1)}, u32[]{:S(2)}) copy-start(bf16[69,16,128]{2,1,0:T(8,128)(2,1)} %fields_ref.1) | copy-start | bytes 847876
  1.6 1.0 %copy-start.1 = (bf16[69,16,128]{2,1,0:T(8,128)(2,1)S(1)}, bf16[69,16,128]{2,1,0:T(8,128)(2,1)}, u32[]{:S(2)}) copy-start(bf16[69,16,128]{2,1,0:T(8,128)(2,1)} %cot_ref.1) | copy-start | bytes 847876
  2.5 11.5 %copy-start.6 = (bf16[3,3,69,256]{3,2,1,0:T(8,128)(2,1)S(1)}, bf16[3,3,69,256]{3,2,1,0:T(8,128)(2,1)}, u32[]{:S(2)}) copy-start(bf16[3,3,69,256]{3,2,1,0:T(8,128)(2,1)} %param.6) | copy-start | bytes 953860
  2.5 11.5 %copy-start.7 = (bf16[3,3,256,69]{2,3,1,0:T(8,128)(2,1)S(1)}, bf16[3,3,256,69]{2,3,1,0:T(8,128)(2,1)}, u32[]{:S(2)}) copy-start(bf16[3,3,256,69]{2,3,1,0:T(8,128)(2,1)} %param.5) | copy-start | bytes 953860
  3.7 4.0 %collective-permute-start = (bf16[8,1280]{1,0:T(8,128)(2,1)S(1)}, bf16[8,1280]{1,0:T(8,128)(2,1)S(1)}, u32[]{:S(2)}, u32[]{:S(2)}) collective-permute-start(bf16[8,1280]{1,0:T(8,128)(2,1)S(1)} %get-tuple-element.25), channel_id=1, source_target_pairs={{0,1},{1,2},{2,3},{3,4},{4,5},{5,6},{6,7},{7,8},{8,9},{9,10},{10,1... | collective-permute-start | bytes 61448 | tf_op jit(solution)/shard_map/ppermute | solution.py:354
  6.3 3.2 %collective-permute-start.1 = (bf16[8,1280]{1,0:T(8,128)(2,1)S(1)}, bf16[8,1280]{1,0:T(8,128)(2,1)S(1)}, u32[]{:S(2)}, u32[]{:S(2)}) collective-permute-start(bf16[8,1280]{1,0:T(8,128)(2,1)S(1)} %get-tuple-element.26), channel_id=1, source_target_pairs={{1,0},{2,1},{3,2},{4,3},{5,4},{6,5},{7,6},{8,7},{9,8},{10,9},{11,1... | collective-permute-start | bytes 61448 | tf_op jit(solution)/shard_map/ppermute | solution.py:355
  10.7 4.7 %collective-permute-start.2 = (bf16[4,72,128]{2,1,0:T(8,128)(2,1)S(1)}, bf16[4,72,128]{2,1,0:T(8,128)(2,1)S(1)}, u32[]{:S(2)}, u32[]{:S(2)}) collective-permute-start(bf16[4,72,128]{2,1,0:T(8,128)(2,1)S(1)} %get-tuple-element.29), channel_id=1, source_target_pairs={{0,16},{1,17},{2,18},{3,19},{4,20},{5,21},{6,22},{7,23},{8,0},{9,1... | collective-permute-start | bytes 221192 | tf_op jit(solution)/shard_map/ppermute | solution.py:361
  14.0 4.7 %collective-permute-start.3 = (bf16[4,72,128]{2,1,0:T(8,128)(2,1)S(1)}, bf16[4,72,128]{2,1,0:T(8,128)(2,1)S(1)}, u32[]{:S(2)}, u32[]{:S(2)}) collective-permute-start(bf16[4,72,128]{2,1,0:T(8,128)(2,1)S(1)} %get-tuple-element.30), channel_id=1, source_target_pairs={{16,0},{17,1},{18,2},{19,3},{20,4},{21,5},{22,6},{23,7},{0,8},{1,9... | collective-permute-start | bytes 221192 | tf_op jit(solution)/shard_map/ppermute | solution.py:362
  28.4 1.0 %copy-start.4 = (bf16[18,256,128]{2,1,0:T(8,128)(2,1)}, bf16[18,256,128]{2,1,0:T(8,128)(2,1)S(1)}, u32[]{:S(2)}) copy-start(bf16[18,256,128]{2,1,0:T(8,128)(2,1)S(1)} %get-tuple-element.33.hid_ref) | copy-start | bytes 3538948
  29.4 4.3 %copy-start.2 = (bf16[16,256,128]{2,1,0:T(8,128)(2,1)}, bf16[16,256,128]{2,1,0:T(8,128)(2,1)S(1)}, u32[]{:S(2)}) copy-start(bf16[16,256,128]{2,1,0:T(8,128)(2,1)S(1)} %get-tuple-element.37.rows_ref) | copy-start | bytes 3145732
  29.4 10.2 %copy-start.5 = (bf16[18,256,128]{2,1,0:T(8,128)(2,1)S(1)}, bf16[18,256,128]{2,1,0:T(8,128)(2,1)}, u32[]{:S(2)}) copy-start(bf16[18,256,128]{2,1,0:T(8,128)(2,1)} %copy-done.4) | copy-start | bytes 3538948
  29.4 3.5 %collective-permute-start.4 = (bf16[1280,128]{1,0:T(8,128)(2,1)S(1)}, bf16[1280,128]{1,0:T(8,128)(2,1)S(1)}, u32[]{:S(2)}, u32[]{:S(2)}) collective-permute-start(bf16[1280,128]{1,0:T(8,128)(2,1)S(1)} %get-tuple-element.32), channel_id=1, source_target_pairs={{0,1},{1,0},{2,3},{3,2},{4,5},{5,4},{6,7},{7,6},{8,9},{9,8},{10,11... | collective-permute-start | bytes 983048 | tf_op jit(solution)/shard_map/ppermute | solution.py:314
  33.7 15.0 %all-to-all-start = ((bf16[16,80,128]{2,1,0:T(8,128)(2,1)}), bf16[16,80,128]{2,1,0:T(8,128)(2,1)S(1)}, u32[]{:S(2)}, u32[]{:S(2)}) async-start(bf16[16,80,128]{2,1,0:T(8,128)(2,1)} %bitcast.9), calls=%async_computation | async-start | bytes 655360 | tf_op jit(solution)/shard_map/all_to_all | solution.py:411
  39.6 17.8 %copy-start.3 = (bf16[16,256,128]{2,1,0:T(8,128)(2,1)S(1)}, bf16[16,256,128]{2,1,0:T(8,128)(2,1)}, u32[]{:S(2)}) copy-start(bf16[16,256,128]{2,1,0:T(8,128)(2,1)} %copy-done.2) | copy-start | bytes 3145732
  49.4 16.4 %all-to-all-start.1 = ((bf16[8,80,128]{2,1,0:T(8,128)(2,1)}), bf16[8,80,128]{2,1,0:T(8,128)(2,1)S(1)}, u32[]{:S(2)}, u32[]{:S(2)}) async-start(bf16[8,80,128]{2,1,0:T(8,128)(2,1)} %shard_map.79), calls=%async_computation.1 | async-start | bytes 327680 | tf_op jit(solution)/shard_map/all_to_all | solution.py:411
  76.4 5.2 %collective-permute-start.5 = (bf16[1280,128]{1,0:T(8,128)(2,1)S(1)}, bf16[1280,128]{1,0:T(8,128)(2,1)S(1)}, u32[]{:S(2)}, u32[]{:S(2)}) collective-permute-start(bf16[1280,128]{1,0:T(8,128)(2,1)S(1)} %bitcast.18), channel_id=1, source_target_pairs={{0,1},{1,0},{2,3},{3,2},{4,5},{5,4},{6,7},{7,6},{8,9},{9,8},{10,11... | collective-permute-start | bytes 983048 | tf_op jit(solution)/shard_map/ppermute | solution.py:314

commit v3 on v2

v3 whole, which is shorter than its diff:
```python
import functools

import jax
import jax.numpy as jnp
from jax import lax
from jax.experimental import pallas as pl
from jax.experimental.pallas import tpu as pltpu
from jax.sharding import Mesh
from jax.sharding import PartitionSpec as P

FACE = ("y_hi", "y_lo", "x")
LAT = ("z", "y_hi")
LON = ("y_lo", "x", "core")

LANES = 128
ROWS = 16
DEEP = 80
SENT = 72
SIDES = 16
MID = ROWS - 2
BAND = 3 * DEEP
TAPS = 3 * BAND
PACK = 640
F32 = jnp.float32
BF16 = jnp.bfloat16
NT = (((1,), (1,)), ((), ()))
TN = (((0,), (0,)), ((), ()))
FULL = pl.BlockSpec(memory_space=pltpu.VMEM)
FLAGS = pl.BlockSpec(memory_space=pltpu.SMEM)
FAR = pl.BlockSpec(memory_space=pltpu.HBM)


def lane_of(shape):
    return lax.broadcasted_iota(jnp.int32, shape, len(shape) - 1)


def dot(a, b, dims=(((1,), (0,)), ((), ()))):
    return lax.dot_general(a, b, dims, preferred_element_type=F32)


def call(kernel, outs, cost, scratch=(), limit=8):
    return functools.partial(
        pl.pallas_call,
        kernel,
        out_shape=outs,
        scratch_shapes=list(scratch),
        compiler_params=pltpu.CompilerParams(vmem_limit_bytes=limit << 20),
        cost_estimate=pl.CostEstimate(flops=cost, bytes_accessed=cost // 500, transcendentals=0),
    )


def picks(count, pairs):
    rows = lax.broadcasted_iota(jnp.int32, (SIDES, count), 0)
    lanes = lax.broadcasted_iota(jnp.int32, (SIDES, count), 1)
    hot = (rows == pairs[0][0]) & (lanes == pairs[0][1])
    for row, lane in pairs[1:]:
        hot = hot | ((rows == row) & (lanes == lane))
    return jnp.where(hot, 1.0, 0.0).astype(BF16)


def columns_kernel(
    fields_ref, cot_ref, x_ref, r_ref, east_ref, west_ref, in_x, in_r, raw_s, sems
):
    loads = [
        pltpu.make_async_copy(fields_ref, in_x, sems.at[0]),
        pltpu.make_async_copy(cot_ref, in_r, sems.at[1]),
    ]
    for load in loads:
        load.start()
    size = in_x.shape[0] * ROWS
    sides = None
    for load, source, target, chosen in (
        (loads[0], in_x, x_ref, [(0, 126), (1, 127), (8, 0), (9, 1)]),
        (loads[1], in_r, r_ref, [(2, 127), (10, 0)]),
    ):
        load.wait()
        raw_s[:size, :] = source[...].astype(F32).reshape(size, LANES)
        raw_s[size:, :] = jnp.zeros((raw_s.shape[0] - size, LANES), F32)
        for row in range(ROWS):
            target[row] = raw_s[pl.ds(row, DEEP, stride=ROWS), :].astype(BF16)
        some = dot(picks(LANES, chosen), target[...].reshape(ROWS * DEEP, LANES), NT)
        sides = some if sides is None else sides + some
    east_ref[...] = sides[: SIDES // 2].astype(BF16)
    west_ref[...] = sides[SIDES // 2 :].astype(BF16)


def side_columns(east_ref, west_ref, rows):
    first, last = rows[0] * DEEP, (rows[-1] + 1) * DEEP
    east, west = east_ref[:, first:last].astype(F32), west_ref[:, first:last].astype(F32)
    return jnp.concatenate([east, west], axis=0).T.astype(BF16)


OWN = [(0, 126), (1, 127), (8, 0), (9, 1)]


def side_planes(columns):
    return dot(columns, picks(2 * LANES, OWN + [(2, LANES + 127), (10, LANES)]))


def rows_kernel(flags_ref, x_ref, r_ref, east_ref, west_ref, a_ref, b_ref):
    low = flags_ref[3] == 1
    edge_picks = picks(LANES, OWN + [(2, 7), (10, 8)])
    inner_picks = picks(LANES, [(0, 2), (1, 3), (8, 4), (9, 5)])

    def packet(edge, inner):
        both = side_columns(east_ref, west_ref, sorted((edge, inner)))
        outer, other = (both[:DEEP], both[DEEP:]) if edge < inner else (both[DEEP:], both[:DEEP])
        sides = dot(outer, edge_picks) + dot(other, inner_picks)
        return [x_ref[edge].astype(F32), x_ref[inner].astype(F32), r_ref[edge].astype(F32), sides]

    top, bottom = packet(0, 1), packet(ROWS - 1, ROWS - 2)
    for k in range(4):
        t, b = top[k][:SENT], bottom[k][:SENT]
        a_ref[k] = jnp.where(low, b, t).astype(BF16)
        b_ref[k] = jnp.where(low, t, b).astype(BF16)


def shifts(x, h):
    lane = lane_of(x.shape)
    left = pltpu.roll(jnp.where(lane == LANES - 1, h, x), 1, 1)
    right = pltpu.roll(jnp.where(lane == 0, h, x), LANES - 1, 1)
    return left, right


def put_field(ref, slot, x, h):
    left, right = shifts(x, h)
    ref[slot, :DEEP, :] = left.astype(BF16)
    ref[slot, DEEP : 2 * DEEP, :] = x.astype(BF16)
    ref[slot, 2 * DEEP :, :] = right.astype(BF16)


def put_cot(ref, slot, x, h):
    left, right = shifts(x, h)
    ref[slot, :DEEP, :] = right.astype(BF16)
    ref[slot, DEEP : 2 * DEEP, :] = x.astype(BF16)
    ref[slot, 2 * DEEP :, :] = left.astype(BF16)


def put_strip(ref, slot, x, h):
    lane = lane_of((DEEP, LANES))
    spot = 2 * slot
    hit = (lane == spot) | (lane == spot + 1)
    sides = (
        (jnp.where(lane == LANES - 1, x, h), spot + 2),
        (h, spot + 1),
        (jnp.where(lane == 0, x, h), spot),
    )
    for tap, (plane, turn) in enumerate(sides):
        rows = pl.ds(tap * DEEP, DEEP)
        ref[rows, :] = jnp.where(hit, pltpu.roll(plane, turn, 1), ref[rows, :])


def wide(ref, slots):
    return jnp.concatenate([ref[slot] for slot in slots], axis=1)


def stacks(ref, starts):
    return jnp.concatenate([ref[k : k + 3].reshape(TAPS, LANES) for k in starts], axis=1)


def inner_kernel(
    x_ref, r_ref, east_ref, west_ref, we_ref, gt_ref, feat_ref, hid_ref, acc_ref, f_s, r_s, back_s
):
    planes = side_planes(side_columns(east_ref, west_ref, range(ROWS)))
    for row in range(ROWS):
        side = planes[row * DEEP : (row + 1) * DEEP]
        put_field(f_s, row, x_ref[row].astype(F32), side[:, :LANES])
        put_cot(r_s, ROWS - 1 - row, r_ref[row].astype(F32), side[:, LANES:])
    for k in range(0, MID, 2):
        pre = dot(we_ref[...], stacks(f_s, (k, k + 1)))
        gate = 1.0 / (1.0 + jnp.exp(-pre))
        hid = (pre * gate).astype(BF16)
        feat = dot(gt_ref[...], stacks(r_s, (MID - 1 - k, MID - 2 - k))).astype(BF16)
        back = (feat.astype(F32) * gate * (1.0 + pre * (1.0 - gate))).astype(BF16)
        for ref, value in ((feat_ref, feat), (hid_ref, hid), (back_s, back)):
            ref[k] = value[:, :LANES]
            ref[k + 1] = value[:, LANES:]
    rows = range(MID)
    acc_ref[0] = dot(stacks(r_s, [MID - 1 - k for k in rows]), wide(hid_ref, rows), NT)
    acc_ref[1] = dot(stacks(f_s, rows), wide(back_s, rows), NT)


def unpack(low, first_ref, second_ref):
    blank = jnp.zeros((DEEP - SENT, LANES), F32)
    cells = [
        jnp.concatenate(
            [jnp.where(low, first_ref[k].astype(F32), second_ref[k].astype(F32)), blank], axis=0
        )
        for k in range(4)
    ]
    return cells + [pltpu.roll(cells[3], LANES - turn, 1) for turn in (4, 8)]


def edge_kernel(
    flags_ref, x_ref, r_ref, east_ref, west_ref, pa_ref, pb_ref, we_ref, gt_ref, acc_ref,
    feat_ref, hid_ref, sent_ref, kept_ref, f_s, r_s, pole_s, sum_s, pack_s,
):
    north, south = flags_ref[0] == 1, flags_ref[1] == 1
    core, low = flags_ref[2], flags_ref[3] == 1
    up, down = unpack(low, pa_ref, pb_ref), unpack(low, pb_ref, pa_ref)
    near = [side_planes(side_columns(east_ref, west_ref, rows)) for rows in ((0, 1), (14, 15))]
    slots = {0: (0, 0), 1: (0, DEEP), ROWS - 2: (1, 0), ROWS - 1: (1, DEEP)}
    for row, slot, back in ((0, 1, 1), (1, 2, 0), (ROWS - 2, 3, 5), (ROWS - 1, 4, 4)):
        which, start = slots[row]
        planes = near[which][start : start + DEEP]
        put_field(f_s, slot, x_ref[row].astype(F32), planes[:, :LANES])
        put_cot(r_s, back, r_ref[row].astype(F32), planes[:, LANES:])
    put_field(f_s, 0, up[0], up[3])
    put_field(f_s, 5, down[0], down[3])
    put_cot(r_s, 2, jnp.where(north, 0.0, up[2]), jnp.where(north, 0.0, up[5]))
    put_cot(r_s, 3, jnp.where(south, 0.0, down[2]), jnp.where(south, 0.0, down[5]))
    put_cot(pole_s, 0, jnp.where(north, up[2], 0.0), jnp.where(north, up[5], 0.0))
    put_cot(pole_s, 1, jnp.where(south, down[2], 0.0), jnp.where(south, down[5], 0.0))
    f2, r2 = stacks(f_s, (0, 3)), stacks(r_s, (0, 3))
    pre = dot(we_ref[...], f2)
    gate = 1.0 / (1.0 + jnp.exp(-pre))
    hid = (pre * gate).astype(BF16)
    hid_ref[0], hid_ref[1] = hid[:, :LANES], hid[:, LANES:]
    extra = jnp.concatenate(
        [dot(gt_ref[:, :BAND], pole_s[0]), dot(gt_ref[:, 2 * BAND :], pole_s[1])], axis=1
    )
    feat = (dot(gt_ref[...], r2) + extra).astype(BF16)
    feat_ref[0], feat_ref[1] = feat[:, :LANES], feat[:, LANES:]
    back = (feat.astype(F32) * gate * (1.0 + pre * (1.0 - gate))).astype(BF16)
    sum_s[0] = acc_ref[0] + dot(r2, hid, NT)
    sum_s[1] = acc_ref[1] + dot(f2, back, NT)
    sum_s[0, :BAND, :] += dot(pole_s[0], hid_ref[0], NT)
    sum_s[0, 2 * BAND :, :] += dot(pole_s[1], hid_ref[1], NT)

    def pack(which, out_ref):
        for tap in range(9):
            pack_s[69 * tap : 69 * tap + 69, :] = sum_s[which, DEEP * tap : DEEP * tap + 69, :]
        pack_s[621:, :] = jnp.zeros((pack_s.shape[0] - 621, pack_s.shape[1]), F32)
        out_ref[:PACK, :] = pack_s[:PACK, :LANES].astype(out_ref.dtype)
        out_ref[PACK:, :] = pack_s[:PACK, LANES:].astype(out_ref.dtype)

    pack(1 - core, sent_ref)
    pack(core, kept_ref)


def beyond_kernel(
    flags_ref, x_ref, east_ref, west_ref, pa_ref, pb_ref, we_ref, halo_ref, strip_ref, f_s, u_s
):
    north, south, low = flags_ref[0] == 1, flags_ref[1] == 1, flags_ref[3] == 1
    up, down = unpack(low, pa_ref, pb_ref), unpack(low, pb_ref, pa_ref)
    planes = side_planes(side_columns(east_ref, west_ref, range(ROWS)))
    u_s[...] = jnp.zeros_like(u_s)
    kept = {0: 2, 1: 3, ROWS - 2: 4, ROWS - 1: 5}
    for row in range(ROWS):
        x, h = x_ref[row].astype(F32), planes[row * DEEP : (row + 1) * DEEP, :LANES]
        put_strip(u_s, row + 2, x, h)
        if row in kept:
            put_field(f_s, kept[row], x, h)
    for slot, place, x, h in (
        (0, 0, up[1], up[4]),
        (1, 1, up[0], up[3]),
        (6, ROWS + 2, down[0], down[3]),
        (7, ROWS + 3, down[1], down[4]),
    ):
        put_field(f_s, slot, x, h)
        put_strip(u_s, place, x, h)

    def rows(flag, first, middle, last):
        a, c = f_s[first].astype(F32), f_s[last].astype(F32)
        ends = jnp.where(flag, c, a).astype(BF16), jnp.where(flag, a, c).astype(BF16)
        return jnp.concatenate([ends[0], f_s[middle], ends[1]], axis=0)

    def silu(v):
        return (v * (1.0 / (1.0 + jnp.exp(-v)))).astype(BF16)

    ring = jnp.concatenate([rows(north, 0, 1, 2), rows(south, 5, 6, 7)], axis=1)
    halo = silu(dot(we_ref[...], ring))
    halo_ref[0], halo_ref[1] = halo[:, :LANES], halo[:, LANES:]
    u = u_s[...]
    u2 = pltpu.roll(u, LANES - 2, 1)
    u4 = pltpu.roll(u, LANES - 4, 1)
    lane = lane_of(u.shape)
    last = 2 * (ROWS + 1)
    flip = (north & (lane < 2)) | (south & ((lane == last) | (lane == last + 1)))
    strip = jnp.concatenate(
        [jnp.where(flip, u4, u).astype(BF16), u2.astype(BF16), jnp.where(flip, u, u4).astype(BF16)],
        axis=0,
    )
    strip_ref[...] = silu(dot(we_ref[...], strip))


def rebuilt_kernel(mid_ref, edge_ref, halo_ref, strip_ref, ga_ref, out_ref, z_s, t_s, out_s):
    ga = ga_ref[...]
    zs = dot(ga, strip_ref[...])
    t0 = zs[:DEEP]
    t2 = zs[2 * DEEP : BAND]
    for a in (1, 2):
        t0 = t0 + pltpu.roll(zs[a * BAND : a * BAND + DEEP], LANES - 2 * a, 1)
        t2 = t2 + pltpu.roll(zs[a * BAND + 2 * DEEP : (a + 1) * BAND], LANES - 2 * a, 1)
    lane = lane_of((DEEP, LANES))
    even = lax.rem(lane, 2) == 0
    t_s[...] = jnp.where(even, pltpu.roll(t2, LANES - 1, 1), pltpu.roll(t0, 1, 1))

    def put(slot, first, second):
        z = dot(ga_ref[...], jnp.concatenate([first, second], axis=1))
        z_s[slot] = z[:, :LANES]
        z_s[slot + 1] = z[:, LANES:]

    put(0, halo_ref[0], edge_ref[0])
    for k in range(0, MID, 2):
        put(k + 2, mid_ref[k], mid_ref[k + 1])
    put(ROWS, edge_ref[1], halo_ref[1])

    for row in range(ROWS):
        sums = []
        for b in range(3):
            total = z_s[row, b * DEEP : (b + 1) * DEEP, :]
            for a in (1, 2):
                start = a * BAND + b * DEEP
                total = total + z_s[row + a, start : start + DEEP, :]
            sums.append(total)
        out = sums[1]
        out = out + jnp.where(lane == 0, 0.0, pltpu.roll(sums[0], 1, 1))
        out = out + jnp.where(lane == LANES - 1, 0.0, pltpu.roll(sums[2], LANES - 1, 1))
        side = pltpu.roll(t_s[...], LANES - 1 - 2 * row, 1)
        out = out + jnp.where((lane == 0) | (lane == LANES - 1), side, 0.0)
        out_s[pl.ds(row, DEEP, stride=ROWS), :] = out
    size = out_ref.shape[0] * ROWS
    out_ref[...] = out_s[:size, :].reshape(out_ref.shape).astype(BF16)


def turn_kernel(mid_ref, edge_ref, out_ref, out_s):
    rows = [edge_ref.at[0]] + [mid_ref.at[row] for row in range(MID)] + [edge_ref.at[1]]
    for row in range(ROWS):
        out_s[pl.ds(row, out_ref.shape[0], stride=ROWS), :] = rows[row][...].astype(F32)
    out_ref[...] = out_s[...].reshape(out_ref.shape).astype(BF16)


def total_kernel(pieces_ref, out_ref):
    total = pieces_ref[0].astype(F32)
    for k in range(1, pieces_ref.shape[0]):
        total = total + pieces_ref[k].astype(F32)
    total = total.astype(BF16)
    for k in range(out_ref.shape[0]):
        out_ref[k] = total


def final_kernel(norm, flags_ref, own_ref, other_ref, enc_ref, gen_ref, pack_s):
    first = flags_ref[2] == 0
    own, other = own_ref[...].astype(F32), other_ref[...].astype(F32)
    gen = jnp.where(first, own, other) * norm
    enc = jnp.where(first, other, own) * norm
    for value, out in ((gen, gen_ref), (enc, enc_ref)):
        pack_s[...] = value
        for tap in range(9):
            out[tap, :, :LANES] = pack_s[69 * tap : 69 * tap + 69, :]
            out[tap, :, LANES:] = pack_s[PACK + 69 * tap : PACK + 69 * tap + 69, :]


def swap_cores(value):
    return lax.ppermute(value, "core", [(0, 1), (1, 0)])


def great_circles(lat_count, lon_count):
    pairs = []
    for la in range(lat_count):
        for lo in range(lon_count):
            if lo < lon_count // 2:
                to = (la + 1, lo) if la < lat_count - 1 else (la, lo + lon_count // 2)
            else:
                to = (la - 1, lo) if la > 0 else (la, lo - lon_count // 2)
            pairs.append((la * lon_count + lo, to[0] * lon_count + to[1]))
    return pairs, [(b, a) for a, b in pairs]


def on_device(fields, enc_kernel, gen_kernel, recon_grad):
    variables, height, width = fields.shape
    channels = gen_kernel.shape[3]
    lat_index, lat_count = lax.axis_index(LAT), lax.axis_size(LAT)
    lon_count = lax.axis_size(LON)
    core = lax.axis_index("core")
    low = lax.axis_index("y_lo") == 0
    flags = jnp.stack(
        [
            (lat_index == 0).astype(jnp.int32),
            (lat_index == lat_count - 1).astype(jnp.int32),
            core.astype(jnp.int32),
            low.astype(jnp.int32),
        ]
    )
    pad = ((0, 0), (0, 0), (0, DEEP - variables), (0, 0))
    gen_rows = jnp.pad(gen_kernel, pad).reshape(TAPS, channels)
    enc_rows = jnp.pad(jnp.swapaxes(enc_kernel, 2, 3), pad).reshape(TAPS, channels)
    def shaped(*shape, dtype=BF16):
        return jax.ShapeDtypeStruct(shape, dtype)

    plane, side = shaped(ROWS, DEEP, LANES), shaped(SIDES // 2, ROWS * DEEP)
    x, r, east, west = call(
        columns_kernel,
        (plane, plane, side, side),
        10**7,
        [
            pltpu.VMEM(fields.shape, BF16),
            pltpu.VMEM(fields.shape, BF16),
            pltpu.VMEM((ROWS * DEEP, LANES), F32),
            pltpu.SemaphoreType.DMA((2,)),
        ],
    )(in_specs=[FAR] * 2, out_specs=(FULL,) * 4)(
        *(pltpu.with_memory_space_constraint(v, pltpu.HBM) for v in (fields, recon_grad))
    )
    right = [(i, (i + 1) % lon_count) for i in range(lon_count)]
    left = [(b, a) for a, b in right]
    east = lax.ppermute(east, LON, right)
    west = lax.ppermute(west, LON, left)
    packet = shaped(4, SENT, LANES)
    pa, pb = call(rows_kernel, (packet, packet), 10**7)(
        in_specs=[FLAGS] + [FULL] * 4, out_specs=(FULL,) * 2
    )(flags, x, r, east, west)
    ahead, behind = great_circles(lat_count, lon_count)
    pa = lax.ppermute(pa, LAT + LON, ahead)
    pb = lax.ppermute(pb, LAT + LON, behind)
    we, gt = enc_rows.T, gen_rows.T
    sums, packed = (2, TAPS, channels), (2 * PACK, LANES)
    feat_mid, hid_mid, acc = call(
        inner_kernel,
        (shaped(MID, channels, LANES), shaped(MID, channels, LANES), shaped(*sums, dtype=F32)),
        9 * 10**9,
        [
            pltpu.VMEM((ROWS, BAND, LANES), BF16),
            pltpu.VMEM((ROWS, BAND, LANES), BF16),
            pltpu.VMEM((MID, channels, LANES), BF16),
        ],
        16,
    )(in_specs=[FULL] * 6, out_specs=(FULL,) * 3)(x, r, east, west, we, gt)
    feat_edge, hid_edge, sent, kept = call(
        edge_kernel,
        (
            shaped(2, channels, LANES),
            shaped(2, channels, LANES),
            shaped(*packed),
            shaped(*packed, dtype=F32),
        ),
        10**9,
        [
            pltpu.VMEM((6, BAND, LANES), BF16),
            pltpu.VMEM((6, BAND, LANES), BF16),
            pltpu.VMEM((2, BAND, LANES), BF16),
            pltpu.VMEM(sums, F32),
            pltpu.VMEM((PACK + 8, channels), F32),
        ],
        16,
    )(in_specs=[FLAGS] + [FULL] * 9, out_specs=(FULL,) * 4)(
        flags, x, r, east, west, pa, pb, we, gt, acc
    )
    halo, strip = call(
        beyond_kernel,
        (shaped(2, channels, LANES), shaped(channels, LANES)),
        10**9,
        [pltpu.VMEM((8, BAND, LANES), BF16), pltpu.VMEM((BAND, LANES), F32)],
    )(in_specs=[FLAGS] + [FULL] * 6, out_specs=(FULL,) * 2)(flags, x, east, west, pa, pb, we)
    feat_grad = call(
        turn_kernel,
        shaped(channels, height, width),
        2 * 10**9,
        [pltpu.VMEM((channels * ROWS, LANES), F32)],
    )(in_specs=[FULL] * 2, out_specs=FULL)(feat_mid, feat_edge)

    half = (kept + swap_cores(sent).astype(F32)).astype(BF16)
    faces, layers = lax.axis_size(FACE), lax.axis_size("z")
    piece = (2 * PACK // faces, LANES)

    def exchange(value, axes):
        return lax.all_to_all(value, axes, 0, 0, tiled=True)

    def total(pieces, copies):
        return call(total_kernel, jax.ShapeDtypeStruct((copies,) + piece, BF16), 10**7)(
            in_specs=[FULL], out_specs=FULL
        )(pieces)

    pieces = exchange(half.reshape((faces,) + piece), FACE)
    pieces, feat_grad, halo, strip = lax.optimization_barrier((pieces, feat_grad, halo, strip))
    pieces = exchange(total(pieces, layers), "z")
    rebuilt = call(
        rebuilt_kernel,
        shaped(variables, height, width),
        4 * 10**9,
        [
            pltpu.VMEM((ROWS + 2, TAPS, LANES), F32),
            pltpu.VMEM((DEEP, LANES), F32),
            pltpu.VMEM((DEEP * ROWS, LANES), F32),
        ],
        12,
    )(in_specs=[FULL] * 5, out_specs=FULL)(hid_mid, hid_edge, halo, strip, gen_rows)
    pieces, rebuilt = lax.optimization_barrier((pieces, rebuilt))
    own = exchange(total(pieces, faces), FACE).reshape(packed)
    other = swap_cores(own)
    norm = (height * lat_count * width * lon_count) ** -0.5
    grad = jax.ShapeDtypeStruct((9, variables, channels), F32)
    enc, gen = call(
        functools.partial(final_kernel, norm), (grad, grad), 10**7, [pltpu.VMEM(packed, F32)]
    )(in_specs=[FLAGS, FULL, FULL], out_specs=(FULL, FULL))(flags, own, other)
    shape = (3, 3, variables, channels)
    return (rebuilt, feat_grad, jnp.swapaxes(enc.reshape(shape), 2, 3), gen.reshape(shape))


def solution(mesh):
    lat_count, lon_count = mesh.shape["lat"], mesh.shape["lon"]
    fine = Mesh(mesh.devices.reshape(lat_count // 2, 2, 2, lon_count // 4, 2), LAT + LON)
    return jax.shard_map(
        on_device,
        mesh=fine,
        in_specs=(P(None, LAT, LON), P(), P(), P(None, LAT, LON)),
        out_specs=(P(None, LAT, LON), P(None, LAT, LON), P(), P()),
        check_vma=False,
    )
```

time: 83.8 us -> 73.8 us (0.88)
  Pallas kernels: 22.1 us -> 16.8 us
  waiting for transfers between devices: 19.1 us -> 14.9 us
    pallas_call x5 -> x7, Pallas kernels: 19.4 us -> 14.2 us  [the longest x1 3.64 us: on_device(): call(inner_kernel, (shaped(MID, channels, LANES), shaped(MID, channels, L...]
    ppermute x1, waiting for transfers between devices: 3.3 us -> 1.05 us  [on_device(): pb = lax.ppermute(pb, LAT + LON, behind)]
    unnamed x16 -> x6, local copies, waits for them, and re-layouts: 2.96 us -> 1.18 us
    ppermute x2, waiting for transfers between devices: 2.4 us -> 0.99 us  [the longest x1 0.98 us: on_device(): west = lax.ppermute(west, LON, left)]
    pad x1, local copies, waits for them, and re-layouts: 0.03 us -> 1 us  [on_device(): jnp.pad(jnp.swapaxes(enc_kernel, 2, 3), pad).reshape(TAPS, channels)]
    ppermute x1, waiting for transfers between devices: 0.97 us -> 0.01 us  [on_device(): pa = lax.ppermute(pa, LAT + LON, ahead)]
  transfers between devices with their start and end apart: 8 -> 8, of which waited for: 8 -> 6; matrix products, arithmetic and copies ran while one was open for 1% -> 2% of each run, Pallas kernels for 9% -> 13%
where the time goes in v3:
time: 73.8 us; the launch traced here: 73.3 us
  starting transfers between devices  26.8 us (36%)
  Pallas kernels  16.8 us (23%)
  waiting for transfers between devices  14.9 us (20%)
  blocking collectives  10.6 us (14%)
  local copies, waits for them, and re-layouts  2.55 us (3%)
  other arithmetic  0.89 us (1%)
  between operations  0.76 us (1%)
    all_to_all x2, starting transfers between devices, exchange(): return lax.all_to_all(value, axes, 0, 0, tiled=True)  13.9 us
    all_to_all x1, blocking collectives, exchange(): return lax.all_to_all(value, axes, 0, 0, tiled=True)  10.6 us
    all_to_all x2, waiting for transfers between devices, exchange(): return lax.all_to_all(value, axes, 0, 0, tiled=True)  10.4 us
    ppermute x2, starting transfers between devices, swap_cores(): return lax.ppermute(value, 'core', [(0, 1), (1, 0)])  6.17 us
    pallas_call x1, Pallas kernels, on_device(): call(inner_kernel, (shaped(MID, channels, LANES), shaped(MID, channels, L...  3.64 us
    ppermute x1, starting transfers between devices, on_device(): pa = lax.ppermute(pa, LAT + LON, ahead)  3.29 us
    ppermute x1, starting transfers between devices, on_device(): east = lax.ppermute(east, LON, right)  2.68 us
    ppermute x2, waiting for transfers between devices, swap_cores(): return lax.ppermute(value, 'core', [(0, 1), (1, 0)])  2.51 us
  transfers between devices with their start and end apart: 8, of which 6 were waited for; matrix products, arithmetic and copies ran while one was open for 2% of the time, Pallas kernels for 13%

profile of v3, /device:TPU:1, one launch (start us, length us, event | category | flops | bytes accessed | tf_op | source)
XLA Modules:
  0.0 73.3 jit_solution(11516894197404684871)
XLA Ops:
  0.6 1.8 %shard_map.75 = (bf16[16,80,128]{2,1,0:T(8,128)(2,1)S(1)}, bf16[16,80,128]{2,1,0:T(8,128)(2,1)S(1)}, bf16[8,1280]{1,0:T(8,128)(2,1)S(1)}, bf16[8,1280]{1,0:T(8,128)(2,1)S(1)}) custom-call(bf16[69,16,128]{2,1,0:T(8,128)(2,1)} %fields_ref.1, bf16[69,16,128]{2,1,0:T(8,128)(2,1)} %cot_ref.1), custom_call_target="tpu_custom_call" | custom-call | flops 10000000 | bytes 20000 | tf_op jit(solution)/shard_map/pallas_call | solution.py:393
  2.4 2.7 %collective-permute-start = (bf16[8,1280]{1,0:T(8,128)(2,1)S(1)}, bf16[8,1280]{1,0:T(8,128)(2,1)S(1)}, u32[]{:S(2)}, u32[]{:S(2)}) collective-permute-start(bf16[8,1280]{1,0:T(8,128)(2,1)S(1)} %get-tuple-element.29), channel_id=1, source_target_pairs={{0,1},{1,2},{2,3},{3,4},{4,5},{5,6},{6,7},{7,8},{8,9},{9,10},{10,1... | collective-permute-start | bytes 61448 | tf_op jit(solution)/shard_map/ppermute | solution.py:408
  5.1 0.7 collective-permute-start.1
  5.9 0.1 pad_add_fusion.flags_ref
  5.9 1.0 %pad.7 = bf16[3,3,80,256]{3,2,1,0:T(8,128)(2,1)S(1)} pad(bf16[3,3,69,256]{3,2,1,0:T(8,128)(2,1)} %bitcast.24, bf16[]{:T(256)} %constant.24.clone.1), padding=0_0x0_0x0_11x0_0 | pad | bytes 686594 | tf_op jit(solution)/shard_map/jit(_pad)/pad | solution.py:388
  6.9 0.2 copy.11
  7.2 0.2 copy.13.gt_ref
  7.3 0.0 collective-permute-done.east_ref
  7.3 1.0 %collective-permute-done.1.west_ref = bf16[8,1280]{1,0:T(8,128)(2,1)S(1)} collective-permute-done((bf16[8,1280]{1,0:T(8,128)(2,1)S(1)}, bf16[8,1280]{1,0:T(8,128)(2,1)S(1)}, u32[]{:S(2)}, u32[]{:S(2)}) %collective-permute-start.1) | collective-permute-done | bytes 20512 | tf_op jit(solution)/shard_map/ppermute | solution.py:409
  8.3 0.9 %shard_map.76 = (bf16[4,72,128]{2,1,0:T(8,128)(2,1)S(1)}, bf16[4,72,128]{2,1,0:T(8,128)(2,1)S(1)}) custom-call(s32[4]{0:T(128)S(1)} %pad_add_fusion.flags_ref, bf16[16,80,128]{2,1,0:T(8,128)(2,1)S(1)} %get-tuple-element.27.x_ref, bf16[16,80,128]{2,1,0:T(8,128)(2,1)S(1)} %get-tuple-element.28.r_ref, bf16[8,1280]{1,0:T(8,128)(2,1)S(1)} %collective-permute-done.east_ref, ...), custom_call_target="tpu_custom_call" | custom-call | flops 10000000 | bytes 20000 | tf_op jit(solution)/shard_map/pallas_call | solution.py:411
  9.2 3.3 %collective-permute-start.2 = (bf16[4,72,128]{2,1,0:T(8,128)(2,1)S(1)}, bf16[4,72,128]{2,1,0:T(8,128)(2,1)S(1)}, u32[]{:S(2)}, u32[]{:S(2)}) collective-permute-start(bf16[4,72,128]{2,1,0:T(8,128)(2,1)S(1)} %get-tuple-element.31), channel_id=1, source_target_pairs={{0,16},{1,17},{2,18},{3,19},{4,20},{5,21},{6,22},{7,23},{8,0},{9,1... | collective-permute-start | bytes 221192 | tf_op jit(solution)/shard_map/ppermute | solution.py:415
  12.5 0.0 collective-permute-start.3
  12.5 3.6 %shard_map.77 = (bf16[14,256,128]{2,1,0:T(8,128)(2,1)S(1)}, bf16[14,256,128]{2,1,0:T(8,128)(2,1)S(1)}, f32[2,720,256]{2,1,0:T(8,128)S(1)}) custom-call(bf16[16,80,128]{2,1,0:T(8,128)(2,1)S(1)} %get-tuple-element.27.x_ref, bf16[16,80,128]{2,1,0:T(8,128)(2,1)S(1)} %get-tuple-element.28.r_ref, bf16[8,1280]{1,0:T(8,128)(2,1)S(1)} %collective-permute-done.east_ref, ...), custom_call_target="tpu_custom_call" | custom-call | flops 8999999488 | bytes 18000000 | tf_op jit(solution)/shard_map/pallas_call | solution.py:419
  16.1 0.0 collective-permute-done.2.pa_ref
  16.1 1.0 %collective-permute-done.3.pb_ref = bf16[4,72,128]{2,1,0:T(8,128)(2,1)S(1)} collective-permute-done((bf16[4,72,128]{2,1,0:T(8,128)(2,1)S(1)}, bf16[4,72,128]{2,1,0:T(8,128)(2,1)S(1)}, u32[]{:S(2)}, u32[]{:S(2)}) %collective-permute-start.3) | collective-permute-done | bytes 73760 | tf_op jit(solution)/shard_map/ppermute | solution.py:416
  17.2 2.0 %shard_map.78 = (bf16[2,256,128]{2,1,0:T(8,128)(2,1)S(1)}, bf16[2,256,128]{2,1,0:T(8,128)(2,1)S(1)}, bf16[1280,128]{1,0:T(8,128)(2,1)S(1)}, f32[1280,128]{1,0:T(8,128)S(1)}) custom-call(s32[4]{0:T(128)S(1)} %pad_add_fusion.flags_ref, bf16[16,80,128]{2,1,0:T(8,128)(2,1)S(1)} %get-tuple-element.27.x_ref, bf16[16,80,128]{2,1,0:T(8,128)(2,1)S(1)} %get-tuple-element.28.r_ref, ...), custom_call_target="tpu_custom_call" | custom-call | flops 1000000000 | bytes 2000000 | tf_op jit(solution)/shard_map/pallas_call | solution.py:430
  19.2 2.3 %collective-permute-start.4 = (bf16[1280,128]{1,0:T(8,128)(2,1)S(1)}, bf16[1280,128]{1,0:T(8,128)(2,1)S(1)}, u32[]{:S(2)}, u32[]{:S(2)}) collective-permute-start(bf16[1280,128]{1,0:T(8,128)(2,1)S(1)} %get-tuple-element.35), channel_id=1, source_target_pairs={{0,1},{1,0},{2,3},{3,2},{4,5},{5,4},{6,7},{7,6},{8,9},{9,8},{10,11... | collective-permute-start | bytes 983048 | tf_op jit(solution)/shard_map/ppermute | solution.py:356
  21.5 1.3 %collective-permute-done.4 = bf16[1280,128]{1,0:T(8,128)(2,1)S(1)} collective-permute-done((bf16[1280,128]{1,0:T(8,128)(2,1)S(1)}, bf16[1280,128]{1,0:T(8,128)(2,1)S(1)}, u32[]{:S(2)}, u32[]{:S(2)}) %collective-permute-start.4) | collective-permute-done | bytes 327712 | tf_op jit(solution)/shard_map/ppermute | solution.py:356
  22.8 0.8 %add_convert_fusion = bf16[1280,128]{1,0:T(8,128)(2,1)} fusion(f32[1280,128]{1,0:T(8,128)S(1)} %get-tuple-element.34, bf16[1280,128]{1,0:T(8,128)(2,1)S(1)} %collective-permute-done.4), kind=kLoop, calls=%fused_computation | loop fusion | flops 491520 | bytes 1310720 | tf_op jit(solution)/shard_map/convert_element_type | solution.py:463
  23.6 5.9 %all-to-all-start = ((bf16[16,80,128]{2,1,0:T(8,128)(2,1)}), bf16[16,80,128]{2,1,0:T(8,128)(2,1)S(1)}, u32[]{:S(2)}, u32[]{:S(2)}) async-start(bf16[16,80,128]{2,1,0:T(8,128)(2,1)} %bitcast.9), calls=%async_computation | async-start | bytes 655360 | tf_op jit(solution)/shard_map/all_to_all | solution.py:468
  29.5 1.7 %shard_map.80 = (bf16[2,256,128]{2,1,0:T(8,128)(2,1)S(1)}, bf16[256,128]{1,0:T(8,128)(2,1)S(1)}) custom-call(s32[4]{0:T(128)S(1)} %pad_add_fusion.flags_ref, bf16[16,80,128]{2,1,0:T(8,128)(2,1)S(1)} %get-tuple-element.27.x_ref, bf16[8,1280]{1,0:T(8,128)(2,1)S(1)} %collective-permute-done.east_ref, bf16[8,1280]{1,0:T(8,128)(2,1)S(1)} %collective-permute-done.1.west_ref, ...), custom_call_target="tpu_custom_call" | custom-call | flops 1000000000 | bytes 2000000 | tf_op jit(solution)/shard_map/pallas_call | solution.py:450
  31.2 2.2 %shard_map.79 = bf16[256,16,128]{2,1,0:T(8,128)(2,1)} custom-call(bf16[14,256,128]{2,1,0:T(8,128)(2,1)S(1)} %get-tuple-element.36.mid_ref, bf16[2,256,128]{2,1,0:T(8,128)(2,1)S(1)} %get-tuple-element.37.edge_ref), custom_call_target="tpu_custom_call" | custom-call | flops 2000000000 | bytes 4000000 | tf_op jit(solution)/shard_map/pallas_call | solution.py:456
  33.3 5.2 %all-to-all-done.pieces_ref = bf16[16,80,128]{2,1,0:T(8,128)(2,1)S(1)} async-done(((bf16[16,80,128]{2,1,0:T(8,128)(2,1)}), bf16[16,80,128]{2,1,0:T(8,128)(2,1)S(1)}, u32[]{:S(2)}, u32[]{:S(2)}) %all-to-all-start) | async-done | bytes 327712 | tf_op jit(solution)/shard_map/all_to_all | solution.py:468
  38.5 0.7 shard_map.81
  39.3 8.0 %all-to-all-start.1 = ((bf16[8,80,128]{2,1,0:T(8,128)(2,1)}), bf16[8,80,128]{2,1,0:T(8,128)(2,1)S(1)}, u32[]{:S(2)}, u32[]{:S(2)}) async-start(bf16[8,80,128]{2,1,0:T(8,128)(2,1)} %shard_map.81), calls=%async_computation.1 | async-start | bytes 327680 | tf_op jit(solution)/shard_map/all_to_all | solution.py:468
  47.3 1.2 %copy-done.1 = bf16[14,256,128]{2,1,0:T(8,128)(2,1)S(1)} copy-done((bf16[14,256,128]{2,1,0:T(8,128)(2,1)S(1)}, bf16[14,256,128]{2,1,0:T(8,128)(2,1)}, u32[]{:S(2)}) %copy-start.1) | copy-done | bytes 917528
  48.5 2.1 %shard_map.82 = bf16[69,16,128]{2,1,0:T(8,128)(2,1)} custom-call(bf16[14,256,128]{2,1,0:T(8,128)(2,1)S(1)} %copy-done.1, bf16[2,256,128]{2,1,0:T(8,128)(2,1)S(1)} %get-tuple-element.42.edge_ref, bf16[2,256,128]{2,1,0:T(8,128)(2,1)S(1)} %get-tuple-element.43.halo_ref, bf16[256,128]{1,0:T(8,128)(2,1)S(1)} %get-tuple-element.44.strip_ref, ...), custom_call_target="tpu_custom_call" | custom-call | flops 4000000000 | bytes 8000000 | tf_op jit(solution)/shard_map/pallas_call | solution.py:478
  50.5 5.1 %all-to-all-done.1.pieces_ref = bf16[8,80,128]{2,1,0:T(8,128)(2,1)S(1)} async-done(((bf16[8,80,128]{2,1,0:T(8,128)(2,1)}), bf16[8,80,128]{2,1,0:T(8,128)(2,1)S(1)}, u32[]{:S(2)}, u32[]{:S(2)}) %all-to-all-start.1) | async-done | bytes 163872 | tf_op jit(solution)/shard_map/all_to_all | solution.py:468
  55.7 10.6 %all_to_all.15 = bf16[16,80,128]{2,1,0:T(8,128)(2,1)S(1)} all-to-all(bf16[16,80,128]{2,1,0:T(8,128)(2,1)S(1)} %shard_map.83), channel_id=1, replica_groups=mesh['z'=8,'y_hi'=2,'y_lo'=2,'x'=4,'core'=2] {'y_hi','y_lo','x'}, dimensions={0} | all-to-all | bytes 655360 | tf_op jit(solution)/shard_map/all_to_all | solution.py:468
  66.3 3.9 %collective-permute-start.5 = (bf16[1280,128]{1,0:T(8,128)(2,1)S(1)}, bf16[1280,128]{1,0:T(8,128)(2,1)S(1)}, u32[]{:S(2)}, u32[]{:S(2)}) collective-permute-start(bf16[1280,128]{1,0:T(8,128)(2,1)S(1)} %bitcast.18), channel_id=1, source_target_pairs={{0,1},{1,0},{2,3},{3,2},{4,5},{5,4},{6,7},{7,6},{8,9},{9,8},{10,11... | collective-permute-start | bytes 983048 | tf_op jit(solution)/shard_map/ppermute | solution.py:356
  70.2 1.3 %collective-permute-done.5.other_ref = bf16[1280,128]{1,0:T(8,128)(2,1)S(1)} collective-permute-done((bf16[1280,128]{1,0:T(8,128)(2,1)S(1)}, bf16[1280,128]{1,0:T(8,128)(2,1)S(1)}, u32[]{:S(2)}, u32[]{:S(2)}) %collective-permute-start.5) | collective-permute-done | bytes 327712 | tf_op jit(solution)/shard_map/ppermute | solution.py:356
  71.5 1.9 %shard_map.84 = (f32[9,69,256]{2,1,0:T(8,128)}, f32[9,69,256]{2,1,0:T(8,128)}) custom-call(s32[4]{0:T(128)S(1)} %pad_add_fusion.flags_ref, bf16[1280,128]{1,0:T(8,128)(2,1)S(1)} %bitcast.19, bf16[1280,128]{1,0:T(8,128)(2,1)S(1)} %collective-permute-done.5.other_ref), custom_call_target="tpu_custom_call" | custom-call | flops 10000000 | bytes 20000 | tf_op jit(solution)/shard_map/pallas_call | solution.py:494
  (7 shorter events, 0.1 us)
Async XLA Ops:
  0.6 6.5 %copy-start.2 = (bf16[3,3,69,256]{3,2,1,0:T(8,128)(2,1)S(1)}, bf16[3,3,69,256]{3,2,1,0:T(8,128)(2,1)}, u32[]{:S(2)}) copy-start(bf16[3,3,69,256]{3,2,1,0:T(8,128)(2,1)} %param.6) | copy-start | bytes 953860
  2.4 4.9 %collective-permute-start = (bf16[8,1280]{1,0:T(8,128)(2,1)S(1)}, bf16[8,1280]{1,0:T(8,128)(2,1)S(1)}, u32[]{:S(2)}, u32[]{:S(2)}) collective-permute-start(bf16[8,1280]{1,0:T(8,128)(2,1)S(1)} %get-tuple-element.29), channel_id=1, source_target_pairs={{0,1},{1,2},{2,3},{3,4},{4,5},{5,6},{6,7},{7,8},{8,9},{9,10},{10,1... | collective-permute-start | bytes 61448 | tf_op jit(solution)/shard_map/ppermute | solution.py:408
  5.1 3.2 %collective-permute-start.1 = (bf16[8,1280]{1,0:T(8,128)(2,1)S(1)}, bf16[8,1280]{1,0:T(8,128)(2,1)S(1)}, u32[]{:S(2)}, u32[]{:S(2)}) collective-permute-start(bf16[8,1280]{1,0:T(8,128)(2,1)S(1)} %get-tuple-element.30), channel_id=1, source_target_pairs={{1,0},{2,1},{3,2},{4,3},{5,4},{6,5},{7,6},{8,7},{9,8},{10,9},{11,1... | collective-permute-start | bytes 61448 | tf_op jit(solution)/shard_map/ppermute | solution.py:409
  9.2 6.9 %collective-permute-start.2 = (bf16[4,72,128]{2,1,0:T(8,128)(2,1)S(1)}, bf16[4,72,128]{2,1,0:T(8,128)(2,1)S(1)}, u32[]{:S(2)}, u32[]{:S(2)}) collective-permute-start(bf16[4,72,128]{2,1,0:T(8,128)(2,1)S(1)} %get-tuple-element.31), channel_id=1, source_target_pairs={{0,16},{1,17},{2,18},{3,19},{4,20},{5,21},{6,22},{7,23},{8,0},{9,1... | collective-permute-start | bytes 221192 | tf_op jit(solution)/shard_map/ppermute | solution.py:415
  12.5 4.7 %collective-permute-start.3 = (bf16[4,72,128]{2,1,0:T(8,128)(2,1)S(1)}, bf16[4,72,128]{2,1,0:T(8,128)(2,1)S(1)}, u32[]{:S(2)}, u32[]{:S(2)}) collective-permute-start(bf16[4,72,128]{2,1,0:T(8,128)(2,1)S(1)} %get-tuple-element.32), channel_id=1, source_target_pairs={{16,0},{17,1},{18,2},{19,3},{20,4},{21,5},{22,6},{23,7},{0,8},{1,9... | collective-permute-start | bytes 221192 | tf_op jit(solution)/shard_map/ppermute | solution.py:416
  16.1 3.1 %copy-start = (bf16[14,256,128]{2,1,0:T(8,128)(2,1)}, bf16[14,256,128]{2,1,0:T(8,128)(2,1)S(1)}, u32[]{:S(2)}) copy-start(bf16[14,256,128]{2,1,0:T(8,128)(2,1)S(1)} %get-tuple-element.41.mid_ref) | copy-start | bytes 2752516
  19.2 3.5 %collective-permute-start.4 = (bf16[1280,128]{1,0:T(8,128)(2,1)S(1)}, bf16[1280,128]{1,0:T(8,128)(2,1)S(1)}, u32[]{:S(2)}, u32[]{:S(2)}) collective-permute-start(bf16[1280,128]{1,0:T(8,128)(2,1)S(1)} %get-tuple-element.35), channel_id=1, source_target_pairs={{0,1},{1,0},{2,3},{3,2},{4,5},{5,4},{6,7},{7,6},{8,9},{9,8},{10,11... | collective-permute-start | bytes 983048 | tf_op jit(solution)/shard_map/ppermute | solution.py:356
  23.6 15.0 %all-to-all-start = ((bf16[16,80,128]{2,1,0:T(8,128)(2,1)}), bf16[16,80,128]{2,1,0:T(8,128)(2,1)S(1)}, u32[]{:S(2)}, u32[]{:S(2)}) async-start(bf16[16,80,128]{2,1,0:T(8,128)(2,1)} %bitcast.9), calls=%async_computation | async-start | bytes 655360 | tf_op jit(solution)/shard_map/all_to_all | solution.py:468
  39.3 16.4 %all-to-all-start.1 = ((bf16[8,80,128]{2,1,0:T(8,128)(2,1)}), bf16[8,80,128]{2,1,0:T(8,128)(2,1)S(1)}, u32[]{:S(2)}, u32[]{:S(2)}) async-start(bf16[8,80,128]{2,1,0:T(8,128)(2,1)} %shard_map.81), calls=%async_computation.1 | async-start | bytes 327680 | tf_op jit(solution)/shard_map/all_to_all | solution.py:468
  47.3 1.2 %copy-start.1 = (bf16[14,256,128]{2,1,0:T(8,128)(2,1)S(1)}, bf16[14,256,128]{2,1,0:T(8,128)(2,1)}, u32[]{:S(2)}) copy-start(bf16[14,256,128]{2,1,0:T(8,128)(2,1)} %copy-done) | copy-start | bytes 2752516
  66.3 5.2 %collective-permute-start.5 = (bf16[1280,128]{1,0:T(8,128)(2,1)S(1)}, bf16[1280,128]{1,0:T(8,128)(2,1)S(1)}, u32[]{:S(2)}, u32[]{:S(2)}) collective-permute-start(bf16[1280,128]{1,0:T(8,128)(2,1)S(1)} %bitcast.18), channel_id=1, source_target_pairs={{0,1},{1,0},{2,3},{3,2},{4,5},{5,4},{6,7},{7,6},{8,9},{9,8},{10,11... | collective-permute-start | bytes 983048 | tf_op jit(solution)/shard_map/ppermute | solution.py:356

commit v4 on v3

--- a/solution.py
+++ b/solution.py
@@ -18,6 +18,7 @@
 SENT = 72
 SIDES = 16
 MID = ROWS - 2
+EDGES = (0, 1, ROWS - 2, ROWS - 1)
 BAND = 3 * DEEP
 TAPS = 3 * BAND
 PACK = 640
@@ -159,13 +160,17 @@
 
 
 def inner_kernel(
-    x_ref, r_ref, east_ref, west_ref, we_ref, gt_ref, feat_ref, hid_ref, acc_ref, f_s, r_s, back_s
+    x_ref, r_ref, east_ref, west_ref, we_ref, gt_ref,
+    feat_ref, hid_ref, acc_ref, fe_ref, re_ref, f_s, r_s, back_s,
 ):
     planes = side_planes(side_columns(east_ref, west_ref, range(ROWS)))
     for row in range(ROWS):
         side = planes[row * DEEP : (row + 1) * DEEP]
         put_field(f_s, row, x_ref[row].astype(F32), side[:, :LANES])
         put_cot(r_s, ROWS - 1 - row, r_ref[row].astype(F32), side[:, LANES:])
+    for k, row in enumerate(EDGES):
+        fe_ref[k] = f_s[row]
+        re_ref[k] = r_s[ROWS - 1 - row]
     for k in range(0, MID, 2):
         pre = dot(we_ref[...], stacks(f_s, (k, k + 1)))
         gate = 1.0 / (1.0 + jnp.exp(-pre))
@@ -191,51 +196,58 @@
     return cells + [pltpu.roll(cells[3], LANES - turn, 1) for turn in (4, 8)]
 
 
+def gradient(which, acc_ref, lhs_ref, rhs_ref, pole_ref, sum_s, pack_s, out_ref):
+    sum_s[...] = acc_ref[which] + dot(lhs_ref[which], rhs_ref[which], NT)
+    for k, start in ((0, 0), (1, 2 * BAND)):
+        pole = jnp.where(which == 0, pole_ref[k].astype(F32), 0.0).astype(BF16)
+        hid = rhs_ref[0, :, k * LANES : (k + 1) * LANES]
+        sum_s[start : start + BAND, :] += dot(pole, hid, NT)
+    for tap in range(9):
+        pack_s[69 * tap : 69 * tap + 69, :] = sum_s[DEEP * tap : DEEP * tap + 69, :]
+    pack_s[621:, :] = jnp.zeros((pack_s.shape[0] - 621, pack_s.shape[1]), F32)
+    out_ref[:PACK, :] = pack_s[:PACK, :LANES].astype(out_ref.dtype)
+    out_ref[PACK:, :] = pack_s[:PACK, LANES:].astype(out_ref.dtype)
+
+
 def edge_kernel(
-    flags_ref, x_ref, r_ref, east_ref, west_ref, pa_ref, pb_ref, we_ref, gt_ref, acc_ref,
-    feat_ref, hid_ref, sent_ref, kept_ref, f_s, r_s, pole_s, sum_s, pack_s,
+    flags_ref, fe_ref, re_ref, pa_ref, pb_ref, we_ref, gt_ref, acc_ref,
+    feat_ref, hid_ref, sent_ref, lhs_ref, rhs_ref, pole_ref, out_s, cot_s, sum_s, pack_s,
 ):
     north, south = flags_ref[0] == 1, flags_ref[1] == 1
     core, low = flags_ref[2], flags_ref[3] == 1
     up, down = unpack(low, pa_ref, pb_ref), unpack(low, pb_ref, pa_ref)
-    near = [side_planes(side_columns(east_ref, west_ref, rows)) for rows in ((0, 1), (14, 15))]
-    slots = {0: (0, 0), 1: (0, DEEP), ROWS - 2: (1, 0), ROWS - 1: (1, DEEP)}
-    for row, slot, back in ((0, 1, 1), (1, 2, 0), (ROWS - 2, 3, 5), (ROWS - 1, 4, 4)):
-        which, start = slots[row]
-        planes = near[which][start : start + DEEP]
-        put_field(f_s, slot, x_ref[row].astype(F32), planes[:, :LANES])
-        put_cot(r_s, back, r_ref[row].astype(F32), planes[:, LANES:])
-    put_field(f_s, 0, up[0], up[3])
-    put_field(f_s, 5, down[0], down[3])
-    put_cot(r_s, 2, jnp.where(north, 0.0, up[2]), jnp.where(north, 0.0, up[5]))
-    put_cot(r_s, 3, jnp.where(south, 0.0, down[2]), jnp.where(south, 0.0, down[5]))
-    put_cot(pole_s, 0, jnp.where(north, up[2], 0.0), jnp.where(north, up[5], 0.0))
-    put_cot(pole_s, 1, jnp.where(south, down[2], 0.0), jnp.where(south, down[5], 0.0))
-    f2, r2 = stacks(f_s, (0, 3)), stacks(r_s, (0, 3))
-    pre = dot(we_ref[...], f2)
+    put_field(out_s, 0, up[0], up[3])
+    put_field(out_s, 1, down[0], down[3])
+    put_cot(cot_s, 0, jnp.where(north, 0.0, up[2]), jnp.where(north, 0.0, up[5]))
+    put_cot(cot_s, 1, jnp.where(south, 0.0, down[2]), jnp.where(south, 0.0, down[5]))
+    put_cot(pole_ref, 0, jnp.where(north, up[2], 0.0), jnp.where(north, up[5], 0.0))
+    put_cot(pole_ref, 1, jnp.where(south, down[2], 0.0), jnp.where(south, down[5], 0.0))
+
+    def beside(first, second):
+        return jnp.concatenate(
+            [jnp.concatenate(first, axis=0), jnp.concatenate(second, axis=0)], axis=1
+        )
+
+    lhs_ref[0] = beside(
+        (re_ref[1], re_ref[0], cot_s[0]), (cot_s[1], re_ref[3], re_ref[2])
+    )
+    lhs_ref[1] = beside((out_s[0], fe_ref[0], fe_ref[1]), (fe_ref[2], fe_ref[3], out_s[1]))
+    pre = dot(we_ref[...], lhs_ref[1])
     gate = 1.0 / (1.0 + jnp.exp(-pre))
     hid = (pre * gate).astype(BF16)
+    extra = jnp.concatenate(
+        [dot(gt_ref[:, :BAND], pole_ref[0]), dot(gt_ref[:, 2 * BAND :], pole_ref[1])], axis=1
+    )
+    feat = (dot(gt_ref[...], lhs_ref[0]) + extra).astype(BF16)
+    back = (feat.astype(F32) * gate * (1.0 + pre * (1.0 - gate))).astype(BF16)
     hid_ref[0], hid_ref[1] = hid[:, :LANES], hid[:, LANES:]
-    extra = jnp.concatenate(
-        [dot(gt_ref[:, :BAND], pole_s[0]), dot(gt_ref[:, 2 * BAND :], pole_s[1])], axis=1
-    )
-    feat = (dot(gt_ref[...], r2) + extra).astype(BF16)
     feat_ref[0], feat_ref[1] = feat[:, :LANES], feat[:, LANES:]
-    back = (feat.astype(F32) * gate * (1.0 + pre * (1.0 - gate))).astype(BF16)
-    sum_s[0] = acc_ref[0] + dot(r2, hid, NT)
-    sum_s[1] = acc_ref[1] + dot(f2, back, NT)
-    sum_s[0, :BAND, :] += dot(pole_s[0], hid_ref[0], NT)
-    sum_s[0, 2 * BAND :, :] += dot(pole_s[1], hid_ref[1], NT)
-
-    def pack(which, out_ref):
-        for tap in range(9):
-            pack_s[69 * tap : 69 * tap + 69, :] = sum_s[which, DEEP * tap : DEEP * tap + 69, :]
-        pack_s[621:, :] = jnp.zeros((pack_s.shape[0] - 621, pack_s.shape[1]), F32)
-        out_ref[:PACK, :] = pack_s[:PACK, :LANES].astype(out_ref.dtype)
-        out_ref[PACK:, :] = pack_s[:PACK, LANES:].astype(out_ref.dtype)
-
-    pack(1 - core, sent_ref)
-    pack(core, kept_ref)
+    rhs_ref[0], rhs_ref[1] = hid, back
+    gradient(1 - core, acc_ref, lhs_ref, rhs_ref, pole_ref, sum_s, pack_s, sent_ref)
+
+
+def kept_kernel(flags_ref, acc_ref, lhs_ref, rhs_ref, pole_ref, kept_ref, sum_s, pack_s):
+    gradient(flags_ref[2], acc_ref, lhs_ref, rhs_ref, pole_ref, sum_s, pack_s, kept_ref)
 
 
 def beyond_kernel(
@@ -340,16 +352,24 @@
         out_ref[k] = total
 
 
-def final_kernel(norm, flags_ref, own_ref, other_ref, enc_ref, gen_ref, pack_s):
+def final_kernel(norm, flags_ref, own_ref, other_ref, enc_ref, gen_ref, pack_s, out_s, sems):
     first = flags_ref[2] == 0
     own, other = own_ref[...].astype(F32), other_ref[...].astype(F32)
-    gen = jnp.where(first, own, other) * norm
-    enc = jnp.where(first, other, own) * norm
-    for value, out in ((gen, gen_ref), (enc, enc_ref)):
-        pack_s[...] = value
-        for tap in range(9):
-            out[tap, :, :LANES] = pack_s[69 * tap : 69 * tap + 69, :]
-            out[tap, :, LANES:] = pack_s[PACK + 69 * tap : PACK + 69 * tap + 69, :]
+    pack_s[0] = jnp.where(first, own, other) * norm
+    pack_s[1] = jnp.where(first, other, own) * norm
+    copies = []
+    for k, out in enumerate((gen_ref, enc_ref)):
+        for group in range(3):
+            for tap in range(3 * group, 3 * group + 3):
+                out_s[k, tap, :, :LANES] = pack_s[k, 69 * tap : 69 * tap + 69, :]
+                out_s[k, tap, :, LANES:] = pack_s[k, PACK + 69 * tap : PACK + 69 * tap + 69, :]
+            taps = pl.ds(3 * group, 3)
+            copies.append(
+                pltpu.make_async_copy(out_s.at[k, taps], out.at[taps], sems.at[3 * k + group])
+            )
+            copies[-1].start()
+    for copy in copies:
+        copy.wait()
 
 
 def swap_cores(value):
@@ -416,9 +436,16 @@
     pb = lax.ppermute(pb, LAT + LON, behind)
     we, gt = enc_rows.T, gen_rows.T
     sums, packed = (2, TAPS, channels), (2 * PACK, LANES)
-    feat_mid, hid_mid, acc = call(
+    few = shaped(4, BAND, LANES)
+    feat_mid, hid_mid, acc, fe, re = call(
         inner_kernel,
-        (shaped(MID, channels, LANES), shaped(MID, channels, LANES), shaped(*sums, dtype=F32)),
+        (
+            shaped(MID, channels, LANES),
+            shaped(MID, channels, LANES),
+            shaped(*sums, dtype=F32),
+            few,
+            few,
+        ),
         9 * 10**9,
         [
             pltpu.VMEM((ROWS, BAND, LANES), BF16),
@@ -426,55 +453,36 @@
             pltpu.VMEM((MID, channels, LANES), BF16),
         ],
         16,
-    )(in_specs=[FULL] * 6, out_specs=(FULL,) * 3)(x, r, east, west, we, gt)
-    feat_edge, hid_edge, sent, kept = call(
+    )(in_specs=[FULL] * 6, out_specs=(FULL,) * 5)(x, r, east, west, we, gt)
+    pair = shaped(2, channels, LANES)
+    work = [pltpu.VMEM(sums[1:], F32), pltpu.VMEM((PACK + 8, channels), F32)]
+    feat_edge, hid_edge, sent, lhs, rhs, poles = call(
         edge_kernel,
         (
-            shaped(2, channels, LANES),
-            shaped(2, channels, LANES),
+            pair,
+            pair,
             shaped(*packed),
-            shaped(*packed, dtype=F32),
+            shaped(2, TAPS, 2 * LANES),
+            shaped(2, channels, 2 * LANES),
+            shaped(2, BAND, LANES),
         ),
         10**9,
-        [
-            pltpu.VMEM((6, BAND, LANES), BF16),
-            pltpu.VMEM((6, BAND, LANES), BF16),
-            pltpu.VMEM((2, BAND, LANES), BF16),
-            pltpu.VMEM(sums, F32),
-            pltpu.VMEM((PACK + 8, channels), F32),
-        ],
+        [pltpu.VMEM((2, BAND, LANES), BF16), pltpu.VMEM((2, BAND, LANES), BF16)] + work,
         16,
-    )(in_specs=[FLAGS] + [FULL] * 9, out_specs=(FULL,) * 4)(
-        flags, x, r, east, west, pa, pb, we, gt, acc
-    )
+    )(in_specs=[FLAGS] + [FULL] * 7, out_specs=(FULL,) * 6)(
+        flags, fe, re, pa, pb, we, gt, acc
+    )
+    kept = call(kept_kernel, shaped(*packed, dtype=F32), 10**9, work)(
+        in_specs=[FLAGS] + [FULL] * 4, out_specs=FULL
+    )(flags, acc, lhs, rhs, poles)
+    half = (kept + swap_cores(sent).astype(F32)).astype(BF16)
+    half, feat_edge, pa = lax.optimization_barrier((half, feat_edge, pa))
     halo, strip = call(
         beyond_kernel,
         (shaped(2, channels, LANES), shaped(channels, LANES)),
         10**9,
         [pltpu.VMEM((8, BAND, LANES), BF16), pltpu.VMEM((BAND, LANES), F32)],
     )(in_specs=[FLAGS] + [FULL] * 6, out_specs=(FULL,) * 2)(flags, x, east, west, pa, pb, we)
-    feat_grad = call(
-        turn_kernel,
-        shaped(channels, height, width),
-        2 * 10**9,
-        [pltpu.VMEM((channels * ROWS, LANES), F32)],
-    )(in_specs=[FULL] * 2, out_specs=FULL)(feat_mid, feat_edge)
-
-    half = (kept + swap_cores(sent).astype(F32)).astype(BF16)
-    faces, layers = lax.axis_size(FACE), lax.axis_size("z")
-    piece = (2 * PACK // faces, LANES)
-
-    def exchange(value, axes):
-        return lax.all_to_all(value, axes, 0, 0, tiled=True)
-
-    def total(pieces, copies):
-        return call(total_kernel, jax.ShapeDtypeStruct((copies,) + piece, BF16), 10**7)(
-            in_specs=[FULL], out_specs=FULL
-        )(pieces)
-
-    pieces = exchange(half.reshape((faces,) + piece), FACE)
-    pieces, feat_grad, halo, strip = lax.optimization_barrier((pieces, feat_grad, halo, strip))
-    pieces = exchange(total(pieces, layers), "z")
     rebuilt = call(
         rebuilt_kernel,
         shaped(variables, height, width),
@@ -486,14 +494,41 @@
         ],
         12,
     )(in_specs=[FULL] * 5, out_specs=FULL)(hid_mid, hid_edge, halo, strip, gen_rows)
-    pieces, rebuilt = lax.optimization_barrier((pieces, rebuilt))
+    feat_grad = call(
+        turn_kernel,
+        shaped(channels, height, width),
+        2 * 10**9,
+        [pltpu.VMEM((channels * ROWS, LANES), F32)],
+    )(in_specs=[FULL] * 2, out_specs=FULL)(feat_mid, feat_edge)
+
+    faces, layers = lax.axis_size(FACE), lax.axis_size("z")
+    piece = (2 * PACK // faces, LANES)
+
+    def exchange(value, axes):
+        return lax.all_to_all(value, axes, 0, 0, tiled=True)
+
+    def total(pieces, copies):
+        return call(total_kernel, jax.ShapeDtypeStruct((copies,) + piece, BF16), 10**7)(
+            in_specs=[FULL], out_specs=FULL
+        )(pieces)
+
+    pieces = exchange(half.reshape((faces,) + piece), FACE)
+    pieces, feat_grad, rebuilt = lax.optimization_barrier((pieces, feat_grad, rebuilt))
+    pieces = exchange(total(pieces, layers), "z")
     own = exchange(total(pieces, faces), FACE).reshape(packed)
     other = swap_cores(own)
     norm = (height * lat_count * width * lon_count) ** -0.5
     grad = jax.ShapeDtypeStruct((9, variables, channels), F32)
     enc, gen = call(
-        functools.partial(final_kernel, norm), (grad, grad), 10**7, [pltpu.VMEM(packed, F32)]
-    )(in_specs=[FLAGS, FULL, FULL], out_specs=(FULL, FULL))(flags, own, other)
+        functools.partial(final_kernel, norm),
+        (grad, grad),
+        10**7,
+        [
+            pltpu.VMEM((2,) + packed, F32),
+            pltpu.VMEM((2, 9, variables, channels), F32),
+            pltpu.SemaphoreType.DMA((6,)),
+        ],
+    )(in_specs=[FLAGS, FULL, FULL], out_specs=(FAR, FAR))(flags, own, other)
     shape = (3, 3, variables, channels)
     return (rebuilt, feat_grad, jnp.swapaxes(enc.reshape(shape), 2, 3), gen.reshape(shape))
 

time: 73.8 us -> 72.9 us (0.988)
  blocking collectives: 10.6 us -> 27.3 us
  waiting for transfers between devices: 14.9 us -> 6.66 us
  starting transfers between devices: 26.8 us -> 18.8 us
  local copies, waits for them, and re-layouts: 2.55 us -> 1.38 us
    all_to_all x1 -> x2, blocking collectives: 10.6 us -> 27.3 us  [exchange(): return lax.all_to_all(value, axes, 0, 0, tiled=True)]
    all_to_all x2 -> x1, starting transfers between devices: 13.9 us -> 5.88 us  [exchange(): return lax.all_to_all(value, axes, 0, 0, tiled=True)]
    all_to_all x2 -> x1, waiting for transfers between devices: 10.4 us -> 3.13 us  [exchange(): return lax.all_to_all(value, axes, 0, 0, tiled=True)]
    unnamed x6, local copies, waits for them, and re-layouts: 1.18 us -> 0.01 us
    pad x1, local copies, waits for them, and re-layouts: 0.03 us -> 1 us  [on_device(): gen_rows = jnp.pad(gen_kernel, pad).reshape(TAPS, channels)]
    pad x1, local copies, waits for them, and re-layouts: 1 us -> 0.03 us  [on_device(): jnp.pad(jnp.swapaxes(enc_kernel, 2, 3), pad).reshape(TAPS, channels)]
    ppermute x2, waiting for transfers between devices: 2.51 us -> 1.58 us  [swap_cores(): return lax.ppermute(value, 'core', [(0, 1), (1, 0)])]
    pallas_call x1 -> x2, Pallas kernels: 2.03 us -> 2.55 us  [the longest x1 1.61 us: on_device(): call(edge_kernel, (pair, pair, shaped(*packed), shaped(2, TAPS, 2 * LANES...]
  transfers between devices with their start and end apart: 8 -> 7, of which waited for: 6 -> 5; matrix products, arithmetic and copies ran while one was open for 2% -> 2% of each run, Pallas kernels for 13% -> 15%
where the time goes in v4:
time: 72.9 us; the launch traced here: 72.6 us
  blocking collectives  27.3 us (37%)
  starting transfers between devices  18.8 us (26%)
  Pallas kernels  16.7 us (23%)
  waiting for transfers between devices  6.66 us (9%)
  local copies, waits for them, and re-layouts  1.38 us (2%)
  between operations  0.92 us (1%)
  other arithmetic  0.87 us (1%)
    all_to_all x2, blocking collectives, exchange(): return lax.all_to_all(value, axes, 0, 0, tiled=True)  27.3 us
    ppermute x2, starting transfers between devices, swap_cores(): return lax.ppermute(value, 'core', [(0, 1), (1, 0)])  6.19 us
    all_to_all x1, starting transfers between devices, exchange(): return lax.all_to_all(value, axes, 0, 0, tiled=True)  5.88 us
    pallas_call x1, Pallas kernels, on_device(): call(inner_kernel, (shaped(MID, channels, LANES), shaped(MID, channels, L...  3.71 us
    ppermute x1, starting transfers between devices, on_device(): pa = lax.ppermute(pa, LAT + LON, ahead)  3.29 us
    all_to_all x1, waiting for transfers between devices, exchange(): return lax.all_to_all(value, axes, 0, 0, tiled=True)  3.13 us
    ppermute x1, starting transfers between devices, on_device(): east = lax.ppermute(east, LON, right)  2.68 us
    pallas_call x1, Pallas kernels, on_device(): call(turn_kernel, shaped(channels, height, width), 2 * 10 ** 9, [pltpu.VM...  2.16 us
  transfers between devices with their start and end apart: 7, of which 5 were waited for; matrix products, arithmetic and copies ran while one was open for 2% of the time, Pallas kernels for 15%

profile of v4, /device:TPU:1, one launch (start us, length us, event | category | flops | bytes accessed | tf_op | source)
XLA Modules:
  0.0 72.6 jit_solution(14970230001075161056)
XLA Ops:
  0.6 1.8 %shard_map.75 = (bf16[16,80,128]{2,1,0:T(8,128)(2,1)S(1)}, bf16[16,80,128]{2,1,0:T(8,128)(2,1)S(1)}, bf16[8,1280]{1,0:T(8,128)(2,1)S(1)}, bf16[8,1280]{1,0:T(8,128)(2,1)S(1)}) custom-call(bf16[69,16,128]{2,1,0:T(8,128)(2,1)} %fields_ref.1, bf16[69,16,128]{2,1,0:T(8,128)(2,1)} %cot_ref.1), custom_call_target="tpu_custom_call" | custom-call | flops 10000000 | bytes 20000 | tf_op jit(solution)/shard_map/pallas_call | solution.py:413
  2.4 2.7 %collective-permute-start = (bf16[8,1280]{1,0:T(8,128)(2,1)S(1)}, bf16[8,1280]{1,0:T(8,128)(2,1)S(1)}, u32[]{:S(2)}, u32[]{:S(2)}) collective-permute-start(bf16[8,1280]{1,0:T(8,128)(2,1)S(1)} %get-tuple-element.33), channel_id=1, source_target_pairs={{0,1},{1,2},{2,3},{3,4},{4,5},{5,6},{6,7},{7,8},{8,9},{9,10},{10,1... | collective-permute-start | bytes 61448 | tf_op jit(solution)/shard_map/ppermute | solution.py:428
  5.1 0.7 %collective-permute-start.1 = (bf16[8,1280]{1,0:T(8,128)(2,1)S(1)}, bf16[8,1280]{1,0:T(8,128)(2,1)S(1)}, u32[]{:S(2)}, u32[]{:S(2)}) collective-permute-start(bf16[8,1280]{1,0:T(8,128)(2,1)S(1)} %get-tuple-element.34), channel_id=1, source_target_pairs={{1,0},{2,1},{3,2},{4,3},{5,4},{6,5},{7,6},{8,7},{9,8},{10,9},{11,1... | collective-permute-start | bytes 61448 | tf_op jit(solution)/shard_map/ppermute | solution.py:429
  5.9 0.1 pad_add_fusion.flags_ref
  5.9 1.0 %pad.8 = bf16[3,3,80,256]{3,2,1,0:T(8,128)(2,1)S(1)} pad(bf16[3,3,69,256]{3,2,1,0:T(8,128)(2,1)} %param.6, bf16[]{:T(256)} %constant.24.clone.1), padding=0_0x0_0x0_11x0_0 | pad | bytes 686594 | tf_op jit(solution)/shard_map/jit(_pad)/pad | solution.py:407
  6.9 0.0 copy-done.2
  7.0 0.2 copy.11
  7.2 0.2 copy.12.gt_ref
  7.3 0.0 collective-permute-done.east_ref
  7.4 1.0 %collective-permute-done.1.west_ref = bf16[8,1280]{1,0:T(8,128)(2,1)S(1)} collective-permute-done((bf16[8,1280]{1,0:T(8,128)(2,1)S(1)}, bf16[8,1280]{1,0:T(8,128)(2,1)S(1)}, u32[]{:S(2)}, u32[]{:S(2)}) %collective-permute-start.1) | collective-permute-done | bytes 20512 | tf_op jit(solution)/shard_map/ppermute | solution.py:429
  8.3 0.9 %shard_map.77 = (bf16[4,72,128]{2,1,0:T(8,128)(2,1)S(1)}, bf16[4,72,128]{2,1,0:T(8,128)(2,1)S(1)}) custom-call(s32[4]{0:T(128)S(1)} %pad_add_fusion.flags_ref, bf16[16,80,128]{2,1,0:T(8,128)(2,1)S(1)} %get-tuple-element.31.x_ref, bf16[16,80,128]{2,1,0:T(8,128)(2,1)S(1)} %get-tuple-element.32.r_ref, bf16[8,1280]{1,0:T(8,128)(2,1)S(1)} %collective-permute-done.east_ref, ...), custom_call_target="tpu_custom_call" | custom-call | flops 10000000 | bytes 20000 | tf_op jit(solution)/shard_map/pallas_call | solution.py:431
  9.2 3.3 %collective-permute-start.2 = (bf16[4,72,128]{2,1,0:T(8,128)(2,1)S(1)}, bf16[4,72,128]{2,1,0:T(8,128)(2,1)S(1)}, u32[]{:S(2)}, u32[]{:S(2)}) collective-permute-start(bf16[4,72,128]{2,1,0:T(8,128)(2,1)S(1)} %get-tuple-element.38), channel_id=1, source_target_pairs={{0,16},{1,17},{2,18},{3,19},{4,20},{5,21},{6,22},{7,23},{8,0},{9,1... | collective-permute-start | bytes 221192 | tf_op jit(solution)/shard_map/ppermute | solution.py:435
  12.5 0.0 collective-permute-start.3
  12.5 3.7 %shard_map.76 = (bf16[14,256,128]{2,1,0:T(8,128)(2,1)S(1)}, bf16[14,256,128]{2,1,0:T(8,128)(2,1)S(1)}, f32[2,720,256]{2,1,0:T(8,128)S(1)}, bf16[4,240,128]{2,1,0:T(8,128)(2,1)S(1)}, bf16[4,240,128]{2,1,0:T(8,128)(2,1)S(1)}) custom-call(bf16[16,80,128]{2,1,0:T(8,128)(2,1)S(1)} %get-tuple-element.31.x_ref, bf16[16,80,128]{2,1,0:T(8,128)(2,1)S(1)} %get-tuple-element.32.r_ref, ...), custom_call_target="tpu_custom_call" | custom-call | flops 8999999488 | bytes 18000000 | tf_op jit(solution)/shard_map/pallas_call | solution.py:440
  16.2 0.0 collective-permute-done.2.pa_ref
  16.2 1.0 %collective-permute-done.3.pb_ref = bf16[4,72,128]{2,1,0:T(8,128)(2,1)S(1)} collective-permute-done((bf16[4,72,128]{2,1,0:T(8,128)(2,1)S(1)}, bf16[4,72,128]{2,1,0:T(8,128)(2,1)S(1)}, u32[]{:S(2)}, u32[]{:S(2)}) %collective-permute-start.3) | collective-permute-done | bytes 73760 | tf_op jit(solution)/shard_map/ppermute | solution.py:436
  17.2 1.6 %shard_map.78 = (bf16[2,256,128]{2,1,0:T(8,128)(2,1)S(1)}, bf16[2,256,128]{2,1,0:T(8,128)(2,1)S(1)}, bf16[1280,128]{1,0:T(8,128)(2,1)S(1)}, bf16[2,720,256]{2,1,...) custom-call(s32[4]{0:T(128)S(1)} %pad_add_fusion.flags_ref, ...), custom_call_target="tpu_custom_call" | custom-call | flops 1000000000 | bytes 2000000 | tf_op jit(solution)/shard_map/pallas_call | solution.py:459
  18.8 2.3 %collective-permute-start.4 = (bf16[1280,128]{1,0:T(8,128)(2,1)S(1)}, bf16[1280,128]{1,0:T(8,128)(2,1)S(1)}, u32[]{:S(2)}, u32[]{:S(2)}) collective-permute-start(bf16[1280,128]{1,0:T(8,128)(2,1)S(1)} %get-tuple-element.43), channel_id=1, source_target_pairs={{0,1},{1,0},{2,3},{3,2},{4,5},{5,4},{6,7},{7,6},{8,9},{9,8},{10,11... | collective-permute-start | bytes 983048 | tf_op jit(solution)/shard_map/ppermute | solution.py:376
  21.1 0.9 %shard_map.79 = f32[1280,128]{1,0:T(8,128)S(1)} custom-call(s32[4]{0:T(128)S(1)} %pad_add_fusion.flags_ref, f32[2,720,256]{2,1,0:T(8,128)S(1)} %get-tuple-element.35.acc_ref, bf16[2,720,256]{2,1,0:T(8,128)(2,1)S(1)} %get-tuple-element.40.lhs_ref, bf16[2,256,256]{2,1,0:T(8,128)(2,1)S(1)} %get-tuple-element.41.rhs_ref, ...), custom_call_target="tpu_custom_call" | custom-call | flops 1000000000 | bytes 2000000 | tf_op jit(solution)/shard_map/pallas_call | solution.py:475
  22.0 0.3 collective-permute-done.4
  22.4 0.8 %add_convert_fusion = bf16[1280,128]{1,0:T(8,128)(2,1)} fusion(f32[1280,128]{1,0:T(8,128)S(1)} %shard_map.79, bf16[1280,128]{1,0:T(8,128)(2,1)S(1)} %collective-permute-done.4), kind=kLoop, calls=%fused_computation | loop fusion | flops 491520 | bytes 1310720 | tf_op jit(solution)/shard_map/convert_element_type | solution.py:478
  23.2 5.9 %all-to-all-start = ((bf16[16,80,128]{2,1,0:T(8,128)(2,1)}), bf16[16,80,128]{2,1,0:T(8,128)(2,1)S(1)}, u32[]{:S(2)}, u32[]{:S(2)}) async-start(bf16[16,80,128]{2,1,0:T(8,128)(2,1)} %bitcast.9), calls=%async_computation | async-start | bytes 655360 | tf_op jit(solution)/shard_map/all_to_all | solution.py:508
  29.0 2.2 %shard_map.80 = bf16[256,16,128]{2,1,0:T(8,128)(2,1)} custom-call(bf16[14,256,128]{2,1,0:T(8,128)(2,1)S(1)} %get-tuple-element.46.mid_ref, bf16[2,256,128]{2,1,0:T(8,128)(2,1)S(1)} %get-tuple-element.47.edge_ref), custom_call_target="tpu_custom_call" | custom-call | flops 2000000000 | bytes 4000000 | tf_op jit(solution)/shard_map/pallas_call | solution.py:497
  31.2 1.7 %shard_map.81 = (bf16[2,256,128]{2,1,0:T(8,128)(2,1)S(1)}, bf16[256,128]{1,0:T(8,128)(2,1)S(1)}) custom-call(s32[4]{0:T(128)S(1)} %pad_add_fusion.flags_ref, bf16[16,80,128]{2,1,0:T(8,128)(2,1)S(1)} %get-tuple-element.31.x_ref, bf16[8,1280]{1,0:T(8,128)(2,1)S(1)} %collective-permute-done.east_ref, bf16[8,1280]{1,0:T(8,128)(2,1)S(1)} %collective-permute-done.1.west_ref, ...), custom_call_target="tpu_custom_call" | custom-call | flops 1000000000 | bytes 2000000 | tf_op jit(solution)/shard_map/pallas_call | solution.py:480
  32.9 2.1 %shard_map.82 = bf16[69,16,128]{2,1,0:T(8,128)(2,1)} custom-call(bf16[14,256,128]{2,1,0:T(8,128)(2,1)S(1)} %copy-done.1, bf16[2,256,128]{2,1,0:T(8,128)(2,1)S(1)} %get-tuple-element.49.edge_ref, bf16[2,256,128]{2,1,0:T(8,128)(2,1)S(1)} %get-tuple-element.51.halo_ref, bf16[256,128]{1,0:T(8,128)(2,1)S(1)} %get-tuple-element.52.strip_ref, ...), custom_call_target="tpu_custom_call" | custom-call | flops 4000000000 | bytes 8000000 | tf_op jit(solution)/shard_map/pallas_call | solution.py:486
  35.0 3.1 %all-to-all-done.pieces_ref = bf16[16,80,128]{2,1,0:T(8,128)(2,1)S(1)} async-done(((bf16[16,80,128]{2,1,0:T(8,128)(2,1)}), bf16[16,80,128]{2,1,0:T(8,128)(2,1)S(1)}, u32[]{:S(2)}, u32[]{:S(2)}) %all-to-all-start) | async-done | bytes 327712 | tf_op jit(solution)/shard_map/all_to_all | solution.py:508
  38.1 0.1 shard_map.83
  38.2 16.2 %all_to_all.15.pieces_ref = bf16[8,80,128]{2,1,0:T(8,128)(2,1)S(1)} all-to-all(bf16[8,80,128]{2,1,0:T(8,128)(2,1)S(1)} %shard_map.83), channel_id=1, replica_groups=mesh['z'=8,'y_hi'=2,'y_lo'=2,'x'=4,'core'=2] {'z'}, dimensions={0} | all-to-all | bytes 327680 | tf_op jit(solution)/shard_map/all_to_all | solution.py:508
  54.4 11.1 %all_to_all.16 = bf16[16,80,128]{2,1,0:T(8,128)(2,1)S(1)} all-to-all(bf16[16,80,128]{2,1,0:T(8,128)(2,1)S(1)} %shard_map.84), channel_id=1, replica_groups=mesh['z'=8,'y_hi'=2,'y_lo'=2,'x'=4,'core'=2] {'y_hi','y_lo','x'}, dimensions={0} | all-to-all | bytes 655360 | tf_op jit(solution)/shard_map/all_to_all | solution.py:508
  65.5 3.9 %collective-permute-start.5 = (bf16[1280,128]{1,0:T(8,128)(2,1)S(1)}, bf16[1280,128]{1,0:T(8,128)(2,1)S(1)}, u32[]{:S(2)}, u32[]{:S(2)}) collective-permute-start(bf16[1280,128]{1,0:T(8,128)(2,1)S(1)} %bitcast.18), channel_id=1, source_target_pairs={{0,1},{1,0},{2,3},{3,2},{4,5},{5,4},{6,7},{7,6},{8,9},{9,8},{10,11... | collective-permute-start | bytes 983048 | tf_op jit(solution)/shard_map/ppermute | solution.py:376
  69.4 1.3 %collective-permute-done.5.other_ref = bf16[1280,128]{1,0:T(8,128)(2,1)S(1)} collective-permute-done((bf16[1280,128]{1,0:T(8,128)(2,1)S(1)}, bf16[1280,128]{1,0:T(8,128)(2,1)S(1)}, u32[]{:S(2)}, u32[]{:S(2)}) %collective-permute-start.5) | collective-permute-done | bytes 327712 | tf_op jit(solution)/shard_map/ppermute | solution.py:376
  70.7 1.8 %shard_map.85 = (f32[9,69,256]{2,1,0:T(8,128)}, f32[9,69,256]{2,1,0:T(8,128)}) custom-call(s32[4]{0:T(128)S(1)} %pad_add_fusion.flags_ref, bf16[1280,128]{1,0:T(8,128)(2,1)S(1)} %bitcast.19, bf16[1280,128]{1,0:T(8,128)(2,1)S(1)} %collective-permute-done.5.other_ref), custom_call_target="tpu_custom_call" | custom-call | flops 10000000 | bytes 20000 | tf_op jit(solution)/shard_map/pallas_call | solution.py:522
  (7 shorter events, 0.1 us)
Async XLA Ops:
  0.6 6.3 %copy-start.2 = (bf16[3,3,256,69]{2,3,1,0:T(8,128)(2,1)S(1)}, bf16[3,3,256,69]{2,3,1,0:T(8,128)(2,1)}, u32[]{:S(2)}) copy-start(bf16[3,3,256,69]{2,3,1,0:T(8,128)(2,1)} %param.5) | copy-start | bytes 953860
  2.4 4.9 %collective-permute-start = (bf16[8,1280]{1,0:T(8,128)(2,1)S(1)}, bf16[8,1280]{1,0:T(8,128)(2,1)S(1)}, u32[]{:S(2)}, u32[]{:S(2)}) collective-permute-start(bf16[8,1280]{1,0:T(8,128)(2,1)S(1)} %get-tuple-element.33), channel_id=1, source_target_pairs={{0,1},{1,2},{2,3},{3,4},{4,5},{5,6},{6,7},{7,8},{8,9},{9,10},{10,1... | collective-permute-start | bytes 61448 | tf_op jit(solution)/shard_map/ppermute | solution.py:428
  5.1 3.2 %collective-permute-start.1 = (bf16[8,1280]{1,0:T(8,128)(2,1)S(1)}, bf16[8,1280]{1,0:T(8,128)(2,1)S(1)}, u32[]{:S(2)}, u32[]{:S(2)}) collective-permute-start(bf16[8,1280]{1,0:T(8,128)(2,1)S(1)} %get-tuple-element.34), channel_id=1, source_target_pairs={{1,0},{2,1},{3,2},{4,3},{5,4},{6,5},{7,6},{8,7},{9,8},{10,9},{11,1... | collective-permute-start | bytes 61448 | tf_op jit(solution)/shard_map/ppermute | solution.py:429
  9.2 7.0 %collective-permute-start.2 = (bf16[4,72,128]{2,1,0:T(8,128)(2,1)S(1)}, bf16[4,72,128]{2,1,0:T(8,128)(2,1)S(1)}, u32[]{:S(2)}, u32[]{:S(2)}) collective-permute-start(bf16[4,72,128]{2,1,0:T(8,128)(2,1)S(1)} %get-tuple-element.38), channel_id=1, source_target_pairs={{0,16},{1,17},{2,18},{3,19},{4,20},{5,21},{6,22},{7,23},{8,0},{9,1... | collective-permute-start | bytes 221192 | tf_op jit(solution)/shard_map/ppermute | solution.py:435
  12.5 4.7 %collective-permute-start.3 = (bf16[4,72,128]{2,1,0:T(8,128)(2,1)S(1)}, bf16[4,72,128]{2,1,0:T(8,128)(2,1)S(1)}, u32[]{:S(2)}, u32[]{:S(2)}) collective-permute-start(bf16[4,72,128]{2,1,0:T(8,128)(2,1)S(1)} %get-tuple-element.39), channel_id=1, source_target_pairs={{16,0},{17,1},{18,2},{19,3},{20,4},{21,5},{22,6},{23,7},{0,8},{1,9... | collective-permute-start | bytes 221192 | tf_op jit(solution)/shard_map/ppermute | solution.py:436
  16.2 2.6 %copy-start = (bf16[14,256,128]{2,1,0:T(8,128)(2,1)}, bf16[14,256,128]{2,1,0:T(8,128)(2,1)S(1)}, u32[]{:S(2)}) copy-start(bf16[14,256,128]{2,1,0:T(8,128)(2,1)S(1)} %get-tuple-element.48.mid_ref) | copy-start | bytes 2752516
  18.8 3.5 %collective-permute-start.4 = (bf16[1280,128]{1,0:T(8,128)(2,1)S(1)}, bf16[1280,128]{1,0:T(8,128)(2,1)S(1)}, u32[]{:S(2)}, u32[]{:S(2)}) collective-permute-start(bf16[1280,128]{1,0:T(8,128)(2,1)S(1)} %get-tuple-element.43), channel_id=1, source_target_pairs={{0,1},{1,0},{2,3},{3,2},{4,5},{5,4},{6,7},{7,6},{8,9},{9,8},{10,11... | collective-permute-start | bytes 983048 | tf_op jit(solution)/shard_map/ppermute | solution.py:376
  23.2 14.9 %all-to-all-start = ((bf16[16,80,128]{2,1,0:T(8,128)(2,1)}), bf16[16,80,128]{2,1,0:T(8,128)(2,1)S(1)}, u32[]{:S(2)}, u32[]{:S(2)}) async-start(bf16[16,80,128]{2,1,0:T(8,128)(2,1)} %bitcast.9), calls=%async_computation | async-start | bytes 655360 | tf_op jit(solution)/shard_map/all_to_all | solution.py:508
  31.2 1.7 %copy-start.1 = (bf16[14,256,128]{2,1,0:T(8,128)(2,1)S(1)}, bf16[14,256,128]{2,1,0:T(8,128)(2,1)}, u32[]{:S(2)}) copy-start(bf16[14,256,128]{2,1,0:T(8,128)(2,1)} %copy-done) | copy-start | bytes 2752516
  65.5 5.2 %collective-permute-start.5 = (bf16[1280,128]{1,0:T(8,128)(2,1)S(1)}, bf16[1280,128]{1,0:T(8,128)(2,1)S(1)}, u32[]{:S(2)}, u32[]{:S(2)}) collective-permute-start(bf16[1280,128]{1,0:T(8,128)(2,1)S(1)} %bitcast.18), channel_id=1, source_target_pairs={{0,1},{1,0},{2,3},{3,2},{4,5},{5,4},{6,7},{7,6},{8,9},{9,8},{10,11... | collective-permute-start | bytes 983048 | tf_op jit(solution)/shard_map/ppermute | solution.py:376

commit v5 on v4

--- a/solution.py
+++ b/solution.py
@@ -60,11 +60,14 @@
 
 
 def columns_kernel(
-    fields_ref, cot_ref, x_ref, r_ref, east_ref, west_ref, in_x, in_r, raw_s, sems
+    fields_ref, cot_ref, enc_ref, gen_ref, x_ref, r_ref, east_ref, west_ref, er_ref, gr_ref,
+    in_x, in_r, in_e, in_g, raw_s, sems,
 ):
     loads = [
-        pltpu.make_async_copy(fields_ref, in_x, sems.at[0]),
-        pltpu.make_async_copy(cot_ref, in_r, sems.at[1]),
+        pltpu.make_async_copy(source, target, sems.at[k])
+        for k, (source, target) in enumerate(
+            ((fields_ref, in_x), (cot_ref, in_r), (enc_ref, in_e), (gen_ref, in_g))
+        )
     ]
     for load in loads:
         load.start()
@@ -81,6 +84,11 @@
             target[row] = raw_s[pl.ds(row, DEEP, stride=ROWS), :].astype(BF16)
         some = dot(picks(LANES, chosen), target[...].reshape(ROWS * DEEP, LANES), NT)
         sides = some if sides is None else sides + some
+    for load, source, target in ((loads[2], in_e, er_ref), (loads[3], in_g, gr_ref)):
+        load.wait()
+        for tap in range(9):
+            target[tap, 64:, :] = jnp.zeros((DEEP - 64, target.shape[2]), BF16)
+            target[tap, : source.shape[1], :] = source[tap]
     east_ref[...] = sides[: SIDES // 2].astype(BF16)
     west_ref[...] = sides[SIDES // 2 :].astype(BF16)
 
@@ -336,11 +344,17 @@
     out_ref[...] = out_s[:size, :].reshape(out_ref.shape).astype(BF16)
 
 
-def turn_kernel(mid_ref, edge_ref, out_ref, out_s):
-    rows = [edge_ref.at[0]] + [mid_ref.at[row] for row in range(MID)] + [edge_ref.at[1]]
+def turn_kernel(part, mid_ref, edge_ref, *refs):
+    into_ref, out_s, turned_s, sem = refs[-4:]
+    count = turned_s.shape[0]
+    chosen = pl.ds(part * count, count)
     for row in range(ROWS):
-        out_s[pl.ds(row, out_ref.shape[0], stride=ROWS), :] = rows[row][...].astype(F32)
-    out_ref[...] = out_s[...].reshape(out_ref.shape).astype(BF16)
+        source = mid_ref.at[row - 1] if 0 < row <= MID else edge_ref.at[min(row, 1)]
+        out_s[pl.ds(row, count, stride=ROWS), :] = source[chosen, :].astype(F32)
+    turned_s[...] = out_s[...].reshape(turned_s.shape).astype(BF16)
+    copy = pltpu.make_async_copy(turned_s, into_ref.at[chosen], sem)
+    copy.start()
+    copy.wait()
 
 
 def total_kernel(pieces_ref, out_ref):
@@ -355,10 +369,9 @@
 def final_kernel(norm, flags_ref, own_ref, other_ref, enc_ref, gen_ref, pack_s, out_s, sems):
     first = flags_ref[2] == 0
     own, other = own_ref[...].astype(F32), other_ref[...].astype(F32)
-    pack_s[0] = jnp.where(first, own, other) * norm
-    pack_s[1] = jnp.where(first, other, own) * norm
     copies = []
     for k, out in enumerate((gen_ref, enc_ref)):
+        pack_s[k] = (jnp.where(first, other, own) if k else jnp.where(first, own, other)) * norm
         for group in range(3):
             for tap in range(3 * group, 3 * group + 3):
                 out_s[k, tap, :, :LANES] = pack_s[k, 69 * tap : 69 * tap + 69, :]
@@ -403,26 +416,36 @@
             low.astype(jnp.int32),
         ]
     )
-    pad = ((0, 0), (0, 0), (0, DEEP - variables), (0, 0))
-    gen_rows = jnp.pad(gen_kernel, pad).reshape(TAPS, channels)
-    enc_rows = jnp.pad(jnp.swapaxes(enc_kernel, 2, 3), pad).reshape(TAPS, channels)
     def shaped(*shape, dtype=BF16):
         return jax.ShapeDtypeStruct(shape, dtype)
 
     plane, side = shaped(ROWS, DEEP, LANES), shaped(SIDES // 2, ROWS * DEEP)
-    x, r, east, west = call(
+    weights = shaped(9, DEEP, channels)
+    taps = (9, variables, channels)
+    x, r, east, west, enc_rows, gen_rows = call(
         columns_kernel,
-        (plane, plane, side, side),
+        (plane, plane, side, side, weights, weights),
         10**7,
         [
             pltpu.VMEM(fields.shape, BF16),
             pltpu.VMEM(fields.shape, BF16),
+            pltpu.VMEM(taps, BF16),
+            pltpu.VMEM(taps, BF16),
             pltpu.VMEM((ROWS * DEEP, LANES), F32),
-            pltpu.SemaphoreType.DMA((2,)),
+            pltpu.SemaphoreType.DMA((4,)),
         ],
-    )(in_specs=[FAR] * 2, out_specs=(FULL,) * 4)(
-        *(pltpu.with_memory_space_constraint(v, pltpu.HBM) for v in (fields, recon_grad))
-    )
+    )(in_specs=[FAR] * 4, out_specs=(FULL,) * 6)(
+        *(
+            pltpu.with_memory_space_constraint(v, pltpu.HBM)
+            for v in (
+                fields,
+                recon_grad,
+                jnp.swapaxes(enc_kernel, 2, 3).reshape(taps),
+                gen_kernel.reshape(taps),
+            )
+        )
+    )
+    enc_rows, gen_rows = (v.reshape(TAPS, channels) for v in (enc_rows, gen_rows))
     right = [(i, (i + 1) % lon_count) for i in range(lon_count)]
     left = [(b, a) for a, b in right]
     east = lax.ppermute(east, LON, right)
@@ -494,13 +517,25 @@
         ],
         12,
     )(in_specs=[FULL] * 5, out_specs=FULL)(hid_mid, hid_edge, halo, strip, gen_rows)
-    feat_grad = call(
-        turn_kernel,
-        shaped(channels, height, width),
-        2 * 10**9,
-        [pltpu.VMEM((channels * ROWS, LANES), F32)],
-    )(in_specs=[FULL] * 2, out_specs=FULL)(feat_mid, feat_edge)
-
+
+    def turn(part, *earlier):
+        half_channels = channels // 2
+        return pl.pallas_call(
+            functools.partial(turn_kernel, part),
+            out_shape=shaped(channels, height, width),
+            in_specs=[FULL] * 2 + [FAR] * len(earlier),
+            out_specs=FAR,
+            scratch_shapes=[
+                pltpu.VMEM((half_channels * ROWS, LANES), F32),
+                pltpu.VMEM((half_channels, height, width), BF16),
+                pltpu.SemaphoreType.DMA,
+            ],
+            input_output_aliases={2: 0} if earlier else {},
+            compiler_params=pltpu.CompilerParams(vmem_limit_bytes=8 << 20),
+            cost_estimate=pl.CostEstimate(flops=10**9, bytes_accessed=10**6, transcendentals=0),
+        )(feat_mid, feat_edge, *earlier)
+
+    feat_grad = turn(0)
     faces, layers = lax.axis_size(FACE), lax.axis_size("z")
     piece = (2 * PACK // faces, LANES)
 
@@ -516,7 +551,11 @@
     pieces, feat_grad, rebuilt = lax.optimization_barrier((pieces, feat_grad, rebuilt))
     pieces = exchange(total(pieces, layers), "z")
     own = exchange(total(pieces, faces), FACE).reshape(packed)
+    own, feat_mid, feat_edge, feat_grad = lax.optimization_barrier(
+        (own, feat_mid, feat_edge, feat_grad)
+    )
     other = swap_cores(own)
+    feat_grad = turn(1, feat_grad)
     norm = (height * lat_count * width * lon_count) ** -0.5
     grad = jax.ShapeDtypeStruct((9, variables, channels), F32)
     enc, gen = call(

time: 72.9 us -> 72.4 us (level)
  local copies, waits for them, and re-layouts: 1.38 us -> 0.35 us
  waiting for transfers between devices: 6.66 us -> 7.5 us
    ppermute x2, waiting for transfers between devices: 1.58 us -> 0.33 us  [swap_cores(): return lax.ppermute(value, 'core', [(0, 1), (1, 0)])]
    pad x2 -> x0, local copies, waits for them, and re-layouts: 1.03 us -> none  [the longest x1 1 us: on_device(): gen_rows = jnp.pad(gen_kernel, pad).reshape(TAPS, channels)]
    ppermute x1, waiting for transfers between devices: 0.98 us -> 1.88 us  [on_device(): west = lax.ppermute(west, LON, left)]
    all_to_all x1, waiting for transfers between devices: 3.13 us -> 3.93 us  [exchange(): return lax.all_to_all(value, axes, 0, 0, tiled=True)]
    pallas_call x2 -> x3, Pallas kernels: 3.96 us -> 4.6 us  [the longest x2 2.77 us: turn(): pl.pallas_call(functools.partial(turn_kernel, part), out_shape=shaped(cha...]
  transfers between devices with their start and end apart: 7 -> 7, of which waited for: 5 -> 5; matrix products, arithmetic and copies ran while one was open for 2% -> 1% of each run, Pallas kernels for 15% -> 15%
where the time goes in v5:
time: 72.4 us; the launch traced here: 72.1 us
  blocking collectives  26.8 us (37%)
  starting transfers between devices  18.8 us (26%)
  Pallas kernels  17.1 us (24%)
  waiting for transfers between devices  7.5 us (10%)
  other arithmetic  0.87 us (1%)
  between operations  0.75 us (1%)
    all_to_all x2, blocking collectives, exchange(): return lax.all_to_all(value, axes, 0, 0, tiled=True)  26.8 us
    ppermute x2, starting transfers between devices, swap_cores(): return lax.ppermute(value, 'core', [(0, 1), (1, 0)])  6.16 us
    all_to_all x1, starting transfers between devices, exchange(): return lax.all_to_all(value, axes, 0, 0, tiled=True)  5.9 us
    all_to_all x1, waiting for transfers between devices, exchange(): return lax.all_to_all(value, axes, 0, 0, tiled=True)  3.93 us
    pallas_call x1, Pallas kernels, on_device(): call(inner_kernel, (shaped(MID, channels, LANES), shaped(MID, channels, L...  3.49 us
    ppermute x1, starting transfers between devices, on_device(): pa = lax.ppermute(pa, LAT + LON, ahead)  3.29 us
    pallas_call x2, Pallas kernels, turn(): pl.pallas_call(functools.partial(turn_kernel, part), out_shape=shaped(cha...  2.77 us
    ppermute x1, starting transfers between devices, on_device(): east = lax.ppermute(east, LON, right)  2.68 us
  transfers between devices with their start and end apart: 7, of which 5 were waited for; matrix products, arithmetic and copies ran while one was open for 1% of the time, Pallas kernels for 15%

profile of v5, /device:TPU:1, one launch (start us, length us, event | category | flops | bytes accessed | tf_op | source)
XLA Modules:
  0.0 72.1 jit_solution(466181019782777069)
XLA Ops:
  0.6 1.8 %shard_map.75 = (bf16[16,80,128]{2,1,0:T(8,128)(2,1)S(1)}, bf16[16,80,128]{2,1,0:T(8,128)(2,1)S(1)}, bf16[8,1280]{1,0:T(8,128)(2,1)S(1)}, bf16[8,1280]{1,0:T(8,1...) custom-call(bf16[69,16,128]{2,1,0:T(8,128)(2,1)} %fields_ref.1, ...), custom_call_target="tpu_custom_call" | custom-call | flops 10000000 | bytes 20000 | tf_op jit(solution)/shard_map/pallas_call | solution.py:425
  2.5 2.7 %collective-permute-start = (bf16[8,1280]{1,0:T(8,128)(2,1)S(1)}, bf16[8,1280]{1,0:T(8,128)(2,1)S(1)}, u32[]{:S(2)}, u32[]{:S(2)}) collective-permute-start(bf16[8,1280]{1,0:T(8,128)(2,1)S(1)} %get-tuple-element.39), channel_id=1, source_target_pairs={{0,1},{1,2},{2,3},{3,4},{4,5},{5,6},{6,7},{7,8},{8,9},{9,10},{10,1... | collective-permute-start | bytes 61448 | tf_op jit(solution)/shard_map/ppermute | solution.py:451
  5.1 0.7 %collective-permute-start.1 = (bf16[8,1280]{1,0:T(8,128)(2,1)S(1)}, bf16[8,1280]{1,0:T(8,128)(2,1)S(1)}, u32[]{:S(2)}, u32[]{:S(2)}) collective-permute-start(bf16[8,1280]{1,0:T(8,128)(2,1)S(1)} %get-tuple-element.40), channel_id=1, source_target_pairs={{1,0},{2,1},{3,2},{4,3},{5,4},{6,5},{7,6},{8,7},{9,8},{10,9},{11,1... | collective-permute-start | bytes 61448 | tf_op jit(solution)/shard_map/ppermute | solution.py:452
  5.9 0.1 pad_add_fusion.flags_ref
  6.0 0.2 copy.13.gt_ref
  6.1 0.2 copy.12
  6.3 0.2 collective-permute-done.east_ref
  6.5 1.9 %collective-permute-done.1.west_ref = bf16[8,1280]{1,0:T(8,128)(2,1)S(1)} collective-permute-done((bf16[8,1280]{1,0:T(8,128)(2,1)S(1)}, bf16[8,1280]{1,0:T(8,128)(2,1)S(1)}, u32[]{:S(2)}, u32[]{:S(2)}) %collective-permute-start.1) | collective-permute-done | bytes 20512 | tf_op jit(solution)/shard_map/ppermute | solution.py:452
  8.4 0.9 %shard_map.77 = (bf16[4,72,128]{2,1,0:T(8,128)(2,1)S(1)}, bf16[4,72,128]{2,1,0:T(8,128)(2,1)S(1)}) custom-call(s32[4]{0:T(128)S(1)} %pad_add_fusion.flags_ref, bf16[16,80,128]{2,1,0:T(8,128)(2,1)S(1)} %get-tuple-element.37.x_ref, bf16[16,80,128]{2,1,0:T(8,128)(2,1)S(1)} %get-tuple-element.38.r_ref, bf16[8,1280]{1,0:T(8,128)(2,1)S(1)} %collective-permute-done.east_ref, ...), custom_call_target="tpu_custom_call" | custom-call | flops 10000000 | bytes 20000 | tf_op jit(solution)/shard_map/pallas_call | solution.py:454
  9.2 3.3 %collective-permute-start.2 = (bf16[4,72,128]{2,1,0:T(8,128)(2,1)S(1)}, bf16[4,72,128]{2,1,0:T(8,128)(2,1)S(1)}, u32[]{:S(2)}, u32[]{:S(2)}) collective-permute-start(bf16[4,72,128]{2,1,0:T(8,128)(2,1)S(1)} %get-tuple-element.46), channel_id=1, source_target_pairs={{0,16},{1,17},{2,18},{3,19},{4,20},{5,21},{6,22},{7,23},{8,0},{9,1... | collective-permute-start | bytes 221192 | tf_op jit(solution)/shard_map/ppermute | solution.py:458
  12.5 0.0 collective-permute-start.3
  12.5 3.5 %shard_map.76 = (bf16[14,256,128]{2,1,0:T(8,128)(2,1)S(1)}, bf16[14,256,128]{2,1,0:T(8,128)(2,1)S(1)}, f32[2,720,256]{2,1,0:T(8,128)S(1)}, bf16[4,240,128]{2,1,0:T(8,128)(2,1)S(1)}, bf16[4,240,128]{2,1,0:T(8,128)(2,1)S(1)}) custom-call(bf16[16,80,128]{2,1,0:T(8,128)(2,1)S(1)} %get-tuple-element.37.x_ref, bf16[16,80,128]{2,1,0:T(8,128)(2,1)S(1)} %get-tuple-element.38.r_ref, ...), custom_call_target="tpu_custom_call" | custom-call | flops 8999999488 | bytes 18000000 | tf_op jit(solution)/shard_map/pallas_call | solution.py:463
  16.0 0.0 copy-start
  16.0 0.0 collective-permute-done.2.pa_ref
  16.0 1.2 %collective-permute-done.3.pb_ref = bf16[4,72,128]{2,1,0:T(8,128)(2,1)S(1)} collective-permute-done((bf16[4,72,128]{2,1,0:T(8,128)(2,1)S(1)}, bf16[4,72,128]{2,1,0:T(8,128)(2,1)S(1)}, u32[]{:S(2)}, u32[]{:S(2)}) %collective-permute-start.3) | collective-permute-done | bytes 73760 | tf_op jit(solution)/shard_map/ppermute | solution.py:459
  17.2 1.6 %shard_map.78 = (bf16[2,256,128]{2,1,0:T(8,128)(2,1)S(1)}, bf16[2,256,128]{2,1,0:T(8,128)(2,1)S(1)}, bf16[1280,128]{1,0:T(8,128)(2,1)S(1)}, bf16[2,720,256]{2,1,...) custom-call(s32[4]{0:T(128)S(1)} %pad_add_fusion.flags_ref, ...), custom_call_target="tpu_custom_call" | custom-call | flops 1000000000 | bytes 2000000 | tf_op jit(solution)/shard_map/pallas_call | solution.py:482
  18.8 2.3 %collective-permute-start.4 = (bf16[1280,128]{1,0:T(8,128)(2,1)S(1)}, bf16[1280,128]{1,0:T(8,128)(2,1)S(1)}, u32[]{:S(2)}, u32[]{:S(2)}) collective-permute-start(bf16[1280,128]{1,0:T(8,128)(2,1)S(1)} %get-tuple-element.51), channel_id=1, source_target_pairs={{0,1},{1,0},{2,3},{3,2},{4,5},{5,4},{6,7},{7,6},{8,9},{9,8},{10,11... | collective-permute-start | bytes 983048 | tf_op jit(solution)/shard_map/ppermute | solution.py:389
  21.1 0.9 %shard_map.79 = f32[1280,128]{1,0:T(8,128)S(1)} custom-call(s32[4]{0:T(128)S(1)} %pad_add_fusion.flags_ref, f32[2,720,256]{2,1,0:T(8,128)S(1)} %get-tuple-element.43.acc_ref, bf16[2,720,256]{2,1,0:T(8,128)(2,1)S(1)} %get-tuple-element.48.lhs_ref, bf16[2,256,256]{2,1,0:T(8,128)(2,1)S(1)} %get-tuple-element.49.rhs_ref, ...), custom_call_target="tpu_custom_call" | custom-call | flops 1000000000 | bytes 2000000 | tf_op jit(solution)/shard_map/pallas_call | solution.py:498
  22.0 0.3 collective-permute-done.4
  22.3 0.8 %add_convert_fusion = bf16[1280,128]{1,0:T(8,128)(2,1)} fusion(f32[1280,128]{1,0:T(8,128)S(1)} %shard_map.79, bf16[1280,128]{1,0:T(8,128)(2,1)S(1)} %collective-permute-done.4), kind=kLoop, calls=%fused_computation | loop fusion | flops 491520 | bytes 1310720 | tf_op jit(solution)/shard_map/convert_element_type | solution.py:501
  23.1 5.9 %all-to-all-start = ((bf16[16,80,128]{2,1,0:T(8,128)(2,1)}), bf16[16,80,128]{2,1,0:T(8,128)(2,1)S(1)}, u32[]{:S(2)}, u32[]{:S(2)}) async-start(bf16[16,80,128]{2,1,0:T(8,128)(2,1)} %bitcast.11), calls=%async_computation | async-start | bytes 655360 | tf_op jit(solution)/shard_map/all_to_all | solution.py:543
  29.0 1.4 %shard_map.80.refs_0_ = bf16[256,16,128]{2,1,0:T(8,128)(2,1)} custom-call(bf16[14,256,128]{2,1,0:T(8,128)(2,1)S(1)} %get-tuple-element.64.mid_ref, bf16[2,256,128]{2,1,0:T(8,128)(2,1)S(1)} %get-tuple-element.65.edge_ref), custom_call_target="tpu_custom_call" | custom-call | flops 1000000000 | bytes 1000000 | tf_op jit(solution)/shard_map/pallas_call | solution.py:523
  30.4 1.7 %shard_map.81 = (bf16[2,256,128]{2,1,0:T(8,128)(2,1)S(1)}, bf16[256,128]{1,0:T(8,128)(2,1)S(1)}) custom-call(s32[4]{0:T(128)S(1)} %pad_add_fusion.flags_ref, bf16[16,80,128]{2,1,0:T(8,128)(2,1)S(1)} %get-tuple-element.37.x_ref, bf16[8,1280]{1,0:T(8,128)(2,1)S(1)} %collective-permute-done.east_ref, bf16[8,1280]{1,0:T(8,128)(2,1)S(1)} %collective-permute-done.1.west_ref, ...), custom_call_target="tpu_custom_call" | custom-call | flops 1000000000 | bytes 2000000 | tf_op jit(solution)/shard_map/pallas_call | solution.py:503
  32.1 2.1 %shard_map.82 = bf16[69,16,128]{2,1,0:T(8,128)(2,1)} custom-call(bf16[14,256,128]{2,1,0:T(8,128)(2,1)S(1)} %copy-done.1, bf16[2,256,128]{2,1,0:T(8,128)(2,1)S(1)} %get-tuple-element.57.edge_ref, bf16[2,256,128]{2,1,0:T(8,128)(2,1)S(1)} %get-tuple-element.59.halo_ref, bf16[256,128]{1,0:T(8,128)(2,1)S(1)} %get-tuple-element.60.strip_ref, ...), custom_call_target="tpu_custom_call" | custom-call | flops 4000000000 | bytes 8000000 | tf_op jit(solution)/shard_map/pallas_call | solution.py:509
  34.2 3.9 %all-to-all-done.pieces_ref = bf16[16,80,128]{2,1,0:T(8,128)(2,1)S(1)} async-done(((bf16[16,80,128]{2,1,0:T(8,128)(2,1)}), bf16[16,80,128]{2,1,0:T(8,128)(2,1)S(1)}, u32[]{:S(2)}, u32[]{:S(2)}) %all-to-all-start) | async-done | bytes 327712 | tf_op jit(solution)/shard_map/all_to_all | solution.py:543
  38.1 0.1 shard_map.83
  38.1 16.2 %all_to_all.15.pieces_ref = bf16[8,80,128]{2,1,0:T(8,128)(2,1)S(1)} all-to-all(bf16[8,80,128]{2,1,0:T(8,128)(2,1)S(1)} %shard_map.83), channel_id=1, replica_groups=mesh['z'=8,'y_hi'=2,'y_lo'=2,'x'=4,'core'=2] {'z'}, dimensions={0} | all-to-all | bytes 327680 | tf_op jit(solution)/shard_map/all_to_all | solution.py:543
  54.4 10.6 %all_to_all.16 = bf16[16,80,128]{2,1,0:T(8,128)(2,1)S(1)} all-to-all(bf16[16,80,128]{2,1,0:T(8,128)(2,1)S(1)} %shard_map.84), channel_id=1, replica_groups=mesh['z'=8,'y_hi'=2,'y_lo'=2,'x'=4,'core'=2] {'y_hi','y_lo','x'}, dimensions={0} | all-to-all | bytes 655360 | tf_op jit(solution)/shard_map/all_to_all | solution.py:543
  65.0 3.9 %collective-permute-start.5 = (bf16[1280,128]{1,0:T(8,128)(2,1)S(1)}, bf16[1280,128]{1,0:T(8,128)(2,1)S(1)}, u32[]{:S(2)}, u32[]{:S(2)}) collective-permute-start(bf16[1280,128]{1,0:T(8,128)(2,1)S(1)} %bitcast.19), channel_id=1, source_target_pairs={{0,1},{1,0},{2,3},{3,2},{4,5},{5,4},{6,7},{7,6},{8,9},{9,8},{10,11... | collective-permute-start | bytes 983048 | tf_op jit(solution)/shard_map/ppermute | solution.py:389
  68.9 1.4 %shard_map.85 = bf16[256,16,128]{2,1,0:T(8,128)(2,1)} custom-call(bf16[14,256,128]{2,1,0:T(8,128)(2,1)S(1)} %get-tuple-element.64.mid_ref, bf16[2,256,128]{2,1,0:T(8,128)(2,1)S(1)} %get-tuple-element.65.edge_ref, bf16[256,16,128]{2,1,0:T(8,128)(2,1)} %shard_map.80.refs_0_), custom_call_target="tpu_custom_call", output_to_operand_aliasing={{}: (2, {})} | custom-call | flops 1000000000 | bytes 1000000 | tf_op jit(solution)/shard_map/pallas_call | solution.py:523
  70.3 0.0 collective-permute-done.5.other_ref
  70.3 1.8 %shard_map.86 = (f32[9,69,256]{2,1,0:T(8,128)}, f32[9,69,256]{2,1,0:T(8,128)}) custom-call(s32[4]{0:T(128)S(1)} %pad_add_fusion.flags_ref, bf16[1280,128]{1,0:T(8,128)(2,1)S(1)} %bitcast.20, bf16[1280,128]{1,0:T(8,128)(2,1)S(1)} %collective-permute-done.5.other_ref), custom_call_target="tpu_custom_call" | custom-call | flops 10000000 | bytes 20000 | tf_op jit(solution)/shard_map/pallas_call | solution.py:561
  (4 shorter events, 0.0 us)
Async XLA Ops:
  2.5 4.0 %collective-permute-start = (bf16[8,1280]{1,0:T(8,128)(2,1)S(1)}, bf16[8,1280]{1,0:T(8,128)(2,1)S(1)}, u32[]{:S(2)}, u32[]{:S(2)}) collective-permute-start(bf16[8,1280]{1,0:T(8,128)(2,1)S(1)} %get-tuple-element.39), channel_id=1, source_target_pairs={{0,1},{1,2},{2,3},{3,4},{4,5},{5,6},{6,7},{7,8},{8,9},{9,10},{10,1... | collective-permute-start | bytes 61448 | tf_op jit(solution)/shard_map/ppermute | solution.py:451
  5.1 3.2 %collective-permute-start.1 = (bf16[8,1280]{1,0:T(8,128)(2,1)S(1)}, bf16[8,1280]{1,0:T(8,128)(2,1)S(1)}, u32[]{:S(2)}, u32[]{:S(2)}) collective-permute-start(bf16[8,1280]{1,0:T(8,128)(2,1)S(1)} %get-tuple-element.40), channel_id=1, source_target_pairs={{1,0},{2,1},{3,2},{4,3},{5,4},{6,5},{7,6},{8,7},{9,8},{10,9},{11,1... | collective-permute-start | bytes 61448 | tf_op jit(solution)/shard_map/ppermute | solution.py:452
  9.2 6.8 %collective-permute-start.2 = (bf16[4,72,128]{2,1,0:T(8,128)(2,1)S(1)}, bf16[4,72,128]{2,1,0:T(8,128)(2,1)S(1)}, u32[]{:S(2)}, u32[]{:S(2)}) collective-permute-start(bf16[4,72,128]{2,1,0:T(8,128)(2,1)S(1)} %get-tuple-element.46), channel_id=1, source_target_pairs={{0,16},{1,17},{2,18},{3,19},{4,20},{5,21},{6,22},{7,23},{8,0},{9,1... | collective-permute-start | bytes 221192 | tf_op jit(solution)/shard_map/ppermute | solution.py:458
  12.5 4.7 %collective-permute-start.3 = (bf16[4,72,128]{2,1,0:T(8,128)(2,1)S(1)}, bf16[4,72,128]{2,1,0:T(8,128)(2,1)S(1)}, u32[]{:S(2)}, u32[]{:S(2)}) collective-permute-start(bf16[4,72,128]{2,1,0:T(8,128)(2,1)S(1)} %get-tuple-element.47), channel_id=1, source_target_pairs={{16,0},{17,1},{18,2},{19,3},{20,4},{21,5},{22,6},{23,7},{0,8},{1,9... | collective-permute-start | bytes 221192 | tf_op jit(solution)/shard_map/ppermute | solution.py:459
  16.0 2.8 %copy-start = (bf16[14,256,128]{2,1,0:T(8,128)(2,1)}, bf16[14,256,128]{2,1,0:T(8,128)(2,1)S(1)}, u32[]{:S(2)}) copy-start(bf16[14,256,128]{2,1,0:T(8,128)(2,1)S(1)} %get-tuple-element.56.mid_ref) | copy-start | bytes 2752516
  18.8 3.5 %collective-permute-start.4 = (bf16[1280,128]{1,0:T(8,128)(2,1)S(1)}, bf16[1280,128]{1,0:T(8,128)(2,1)S(1)}, u32[]{:S(2)}, u32[]{:S(2)}) collective-permute-start(bf16[1280,128]{1,0:T(8,128)(2,1)S(1)} %get-tuple-element.51), channel_id=1, source_target_pairs={{0,1},{1,0},{2,3},{3,2},{4,5},{5,4},{6,7},{7,6},{8,9},{9,8},{10,11... | collective-permute-start | bytes 983048 | tf_op jit(solution)/shard_map/ppermute | solution.py:389
  23.1 15.0 %all-to-all-start = ((bf16[16,80,128]{2,1,0:T(8,128)(2,1)}), bf16[16,80,128]{2,1,0:T(8,128)(2,1)S(1)}, u32[]{:S(2)}, u32[]{:S(2)}) async-start(bf16[16,80,128]{2,1,0:T(8,128)(2,1)} %bitcast.11), calls=%async_computation | async-start | bytes 655360 | tf_op jit(solution)/shard_map/all_to_all | solution.py:543
  30.4 1.7 %copy-start.1 = (bf16[14,256,128]{2,1,0:T(8,128)(2,1)S(1)}, bf16[14,256,128]{2,1,0:T(8,128)(2,1)}, u32[]{:S(2)}) copy-start(bf16[14,256,128]{2,1,0:T(8,128)(2,1)} %copy-done) | copy-start | bytes 2752516
  65.0 5.3 %collective-permute-start.5 = (bf16[1280,128]{1,0:T(8,128)(2,1)S(1)}, bf16[1280,128]{1,0:T(8,128)(2,1)S(1)}, u32[]{:S(2)}, u32[]{:S(2)}) collective-permute-start(bf16[1280,128]{1,0:T(8,128)(2,1)S(1)} %bitcast.19), channel_id=1, source_target_pairs={{0,1},{1,0},{2,3},{3,2},{4,5},{5,4},{6,7},{7,6},{8,9},{9,8},{10,11... | collective-permute-start | bytes 983048 | tf_op jit(solution)/shard_map/ppermute | solution.py:389

commit v6 on v5

--- a/solution.py
+++ b/solution.py
@@ -60,43 +60,56 @@
 
 
 def columns_kernel(
-    fields_ref, cot_ref, enc_ref, gen_ref, x_ref, r_ref, east_ref, west_ref, er_ref, gr_ref,
-    in_x, in_r, in_e, in_g, raw_s, sems,
+    fields_ref, cot_ref, enc_ref, gen_ref, x_ref, r_ref, we_ref, wg_ref, east_ref, west_ref, sems
 ):
     loads = [
         pltpu.make_async_copy(source, target, sems.at[k])
         for k, (source, target) in enumerate(
-            ((fields_ref, in_x), (cot_ref, in_r), (enc_ref, in_e), (gen_ref, in_g))
+            ((fields_ref, x_ref), (cot_ref, r_ref), (enc_ref, we_ref), (gen_ref, wg_ref))
         )
     ]
     for load in loads:
         load.start()
-    size = in_x.shape[0] * ROWS
     sides = None
-    for load, source, target, chosen in (
-        (loads[0], in_x, x_ref, [(0, 126), (1, 127), (8, 0), (9, 1)]),
-        (loads[1], in_r, r_ref, [(2, 127), (10, 0)]),
+    for load, source, chosen in (
+        (loads[0], x_ref, [(0, 126), (1, 127), (8, 0), (9, 1)]),
+        (loads[1], r_ref, [(2, 127), (10, 0)]),
     ):
         load.wait()
+        cells = source[...].reshape(source.shape[0] * ROWS, LANES)
+        some = dot(picks(LANES, chosen), cells, NT)
+        sides = some if sides is None else sides + some
+    east_ref[...] = sides[: SIDES // 2].astype(BF16)
+    west_ref[...] = sides[SIDES // 2 :].astype(BF16)
+    loads[2].wait()
+    loads[3].wait()
+
+
+def planes_kernel(fields_ref, cot_ref, enc_ref, gen_ref, x_ref, r_ref, er_ref, gr_ref, raw_s):
+    size = fields_ref.shape[0] * ROWS
+    raw_s[size:, :] = jnp.zeros((raw_s.shape[0] - size, LANES), F32)
+    for source, target in ((fields_ref, x_ref), (cot_ref, r_ref)):
         raw_s[:size, :] = source[...].astype(F32).reshape(size, LANES)
-        raw_s[size:, :] = jnp.zeros((raw_s.shape[0] - size, LANES), F32)
         for row in range(ROWS):
             target[row] = raw_s[pl.ds(row, DEEP, stride=ROWS), :].astype(BF16)
-        some = dot(picks(LANES, chosen), target[...].reshape(ROWS * DEEP, LANES), NT)
-        sides = some if sides is None else sides + some
-    for load, source, target in ((loads[2], in_e, er_ref), (loads[3], in_g, gr_ref)):
-        load.wait()
+    for source, target in ((enc_ref, er_ref), (gen_ref, gr_ref)):
         for tap in range(9):
             target[tap, 64:, :] = jnp.zeros((DEEP - 64, target.shape[2]), BF16)
             target[tap, : source.shape[1], :] = source[tap]
-    east_ref[...] = sides[: SIDES // 2].astype(BF16)
-    west_ref[...] = sides[SIDES // 2 :].astype(BF16)
-
-
-def side_columns(east_ref, west_ref, rows):
-    first, last = rows[0] * DEEP, (rows[-1] + 1) * DEEP
-    east, west = east_ref[:, first:last].astype(F32), west_ref[:, first:last].astype(F32)
-    return jnp.concatenate([east, west], axis=0).T.astype(BF16)
+
+
+def side_columns(east_ref, west_ref, turn_s):
+    size = east_ref.shape[1]
+    both = jnp.concatenate([east_ref[...].astype(F32), west_ref[...].astype(F32)], axis=0)
+    turn_s[:size, :] = both.T
+    turn_s[size:, :] = jnp.zeros((turn_s.shape[0] - size, SIDES), F32)
+
+    def of(rows):
+        return jnp.concatenate(
+            [turn_s[pl.ds(row, DEEP, stride=ROWS), :] for row in rows], axis=0
+        ).astype(BF16)
+
+    return of
 
 
 OWN = [(0, 126), (1, 127), (8, 0), (9, 1)]
@@ -106,15 +119,14 @@
     return dot(columns, picks(2 * LANES, OWN + [(2, LANES + 127), (10, LANES)]))
 
 
-def rows_kernel(flags_ref, x_ref, r_ref, east_ref, west_ref, a_ref, b_ref):
+def rows_kernel(flags_ref, x_ref, r_ref, east_ref, west_ref, a_ref, b_ref, turn_s):
+    columns = side_columns(east_ref, west_ref, turn_s)
     low = flags_ref[3] == 1
     edge_picks = picks(LANES, OWN + [(2, 7), (10, 8)])
     inner_picks = picks(LANES, [(0, 2), (1, 3), (8, 4), (9, 5)])
 
     def packet(edge, inner):
-        both = side_columns(east_ref, west_ref, sorted((edge, inner)))
-        outer, other = (both[:DEEP], both[DEEP:]) if edge < inner else (both[DEEP:], both[:DEEP])
-        sides = dot(outer, edge_picks) + dot(other, inner_picks)
+        sides = dot(columns([edge]), edge_picks) + dot(columns([inner]), inner_picks)
         return [x_ref[edge].astype(F32), x_ref[inner].astype(F32), r_ref[edge].astype(F32), sides]
 
     top, bottom = packet(0, 1), packet(ROWS - 1, ROWS - 2)
@@ -169,9 +181,9 @@
 
 def inner_kernel(
     x_ref, r_ref, east_ref, west_ref, we_ref, gt_ref,
-    feat_ref, hid_ref, acc_ref, fe_ref, re_ref, f_s, r_s, back_s,
+    feat_ref, hid_ref, acc_ref, fe_ref, re_ref, f_s, r_s, back_s, turn_s,
 ):
-    planes = side_planes(side_columns(east_ref, west_ref, range(ROWS)))
+    planes = side_planes(side_columns(east_ref, west_ref, turn_s)(range(ROWS)))
     for row in range(ROWS):
         side = planes[row * DEEP : (row + 1) * DEEP]
         put_field(f_s, row, x_ref[row].astype(F32), side[:, :LANES])
@@ -259,11 +271,12 @@
 
 
 def beyond_kernel(
-    flags_ref, x_ref, east_ref, west_ref, pa_ref, pb_ref, we_ref, halo_ref, strip_ref, f_s, u_s
+    flags_ref, x_ref, east_ref, west_ref, pa_ref, pb_ref, we_ref,
+    halo_ref, strip_ref, f_s, u_s, turn_s,
 ):
     north, south, low = flags_ref[0] == 1, flags_ref[1] == 1, flags_ref[3] == 1
     up, down = unpack(low, pa_ref, pb_ref), unpack(low, pb_ref, pa_ref)
-    planes = side_planes(side_columns(east_ref, west_ref, range(ROWS)))
+    planes = side_planes(side_columns(east_ref, west_ref, turn_s)(range(ROWS)))
     u_s[...] = jnp.zeros_like(u_s)
     kept = {0: 2, 1: 3, ROWS - 2: 4, ROWS - 1: 5}
     for row in range(ROWS):
@@ -419,39 +432,36 @@
     def shaped(*shape, dtype=BF16):
         return jax.ShapeDtypeStruct(shape, dtype)
 
-    plane, side = shaped(ROWS, DEEP, LANES), shaped(SIDES // 2, ROWS * DEEP)
-    weights = shaped(9, DEEP, channels)
-    taps = (9, variables, channels)
-    x, r, east, west, enc_rows, gen_rows = call(
+    plane, side = shaped(ROWS, DEEP, LANES), shaped(SIDES // 2, variables * ROWS)
+    weights, taps = shaped(9, DEEP, channels), (9, variables, channels)
+    raw = (
+        fields,
+        recon_grad,
+        jnp.swapaxes(enc_kernel, 2, 3).reshape(taps),
+        gen_kernel.reshape(taps),
+    )
+    *raw, east, west = call(
         columns_kernel,
-        (plane, plane, side, side, weights, weights),
+        tuple(shaped(*v.shape) for v in raw) + (side, side),
         10**7,
-        [
-            pltpu.VMEM(fields.shape, BF16),
-            pltpu.VMEM(fields.shape, BF16),
-            pltpu.VMEM(taps, BF16),
-            pltpu.VMEM(taps, BF16),
-            pltpu.VMEM((ROWS * DEEP, LANES), F32),
-            pltpu.SemaphoreType.DMA((4,)),
-        ],
+        [pltpu.SemaphoreType.DMA((4,))],
     )(in_specs=[FAR] * 4, out_specs=(FULL,) * 6)(
-        *(
-            pltpu.with_memory_space_constraint(v, pltpu.HBM)
-            for v in (
-                fields,
-                recon_grad,
-                jnp.swapaxes(enc_kernel, 2, 3).reshape(taps),
-                gen_kernel.reshape(taps),
-            )
-        )
-    )
-    enc_rows, gen_rows = (v.reshape(TAPS, channels) for v in (enc_rows, gen_rows))
+        *(pltpu.with_memory_space_constraint(v, pltpu.HBM) for v in raw)
+    )
+    turned = pltpu.VMEM((ROWS * DEEP, SIDES), F32)
     right = [(i, (i + 1) % lon_count) for i in range(lon_count)]
     left = [(b, a) for a, b in right]
     east = lax.ppermute(east, LON, right)
     west = lax.ppermute(west, LON, left)
+    x, r, enc_rows, gen_rows = call(
+        planes_kernel,
+        (plane, plane, weights, weights),
+        10**9,
+        [pltpu.VMEM((ROWS * DEEP, LANES), F32)],
+    )(in_specs=[FULL] * 4, out_specs=(FULL,) * 4)(*raw)
+    enc_rows, gen_rows = (v.reshape(TAPS, channels) for v in (enc_rows, gen_rows))
     packet = shaped(4, SENT, LANES)
-    pa, pb = call(rows_kernel, (packet, packet), 10**7)(
+    pa, pb = call(rows_kernel, (packet, packet), 10**7, [turned])(
         in_specs=[FLAGS] + [FULL] * 4, out_specs=(FULL,) * 2
     )(flags, x, r, east, west)
     ahead, behind = great_circles(lat_count, lon_count)
@@ -474,6 +484,7 @@
             pltpu.VMEM((ROWS, BAND, LANES), BF16),
             pltpu.VMEM((ROWS, BAND, LANES), BF16),
             pltpu.VMEM((MID, channels, LANES), BF16),
+            turned,
         ],
         16,
     )(in_specs=[FULL] * 6, out_specs=(FULL,) * 5)(x, r, east, west, we, gt)
@@ -504,7 +515,7 @@
         beyond_kernel,
         (shaped(2, channels, LANES), shaped(channels, LANES)),
         10**9,
-        [pltpu.VMEM((8, BAND, LANES), BF16), pltpu.VMEM((BAND, LANES), F32)],
+        [pltpu.VMEM((8, BAND, LANES), BF16), pltpu.VMEM((BAND, LANES), F32), turned],
     )(in_specs=[FLAGS] + [FULL] * 6, out_specs=(FULL,) * 2)(flags, x, east, west, pa, pb, we)
     rebuilt = call(
         rebuilt_kernel,

time: 72.4 us -> 72.1 us (level)
  waiting for transfers between devices: 7.5 us -> 6.66 us
    pallas_call x2 -> x3, Pallas kernels: 2.68 us -> 2.75 us  [the longest x1 1.36 us: on_device(): call(columns_kernel, tuple((shaped(*v.shape) for v in raw)) + (side, side...]
  transfers between devices with their start and end apart: 7 -> 7, of which waited for: 5 -> 4; matrix products, arithmetic and copies ran while one was open for 1% -> 1% of each run, Pallas kernels for 15% -> 16%
where the time goes in v6:
time: 72.1 us; the launch traced here: 71.8 us
  blocking collectives  26.8 us (37%)
  starting transfers between devices  18.8 us (26%)
  Pallas kernels  17.4 us (24%)
  waiting for transfers between devices  6.66 us (9%)
  between operations  0.93 us (1%)
  other arithmetic  0.87 us (1%)
    all_to_all x2, blocking collectives, exchange(): return lax.all_to_all(value, axes, 0, 0, tiled=True)  26.8 us
    ppermute x2, starting transfers between devices, swap_cores(): return lax.ppermute(value, 'core', [(0, 1), (1, 0)])  6.16 us
    all_to_all x1, starting transfers between devices, exchange(): return lax.all_to_all(value, axes, 0, 0, tiled=True)  5.91 us
    all_to_all x1, waiting for transfers between devices, exchange(): return lax.all_to_all(value, axes, 0, 0, tiled=True)  3.83 us
    pallas_call x1, Pallas kernels, on_device(): call(inner_kernel, (shaped(MID, channels, LANES), shaped(MID, channels, L...  3.68 us
    ppermute x1, starting transfers between devices, on_device(): pa = lax.ppermute(pa, LAT + LON, ahead)  3.29 us
    pallas_call x2, Pallas kernels, turn(): pl.pallas_call(functools.partial(turn_kernel, part), out_shape=shaped(cha...  2.77 us
    ppermute x1, starting transfers between devices, on_device(): east = lax.ppermute(east, LON, right)  2.68 us
  transfers between devices with their start and end apart: 7, of which 4 were waited for; matrix products, arithmetic and copies ran while one was open for 1% of the time, Pallas kernels for 16%

profile of v6, /device:TPU:1, one launch (start us, length us, event | category | flops | bytes accessed | tf_op | source)
XLA Modules:
  0.0 71.8 jit_solution(8157582568195798563)
XLA Ops:
  0.6 1.4 %shard_map.75 = (bf16[69,16,128]{2,1,0:T(8,128)(2,1)S(1)}, bf16[69,16,128]{2,1,0:T(8,128)(2,1)S(1)}, bf16[9,69,256]{2,1,0:T(8,128)(2,1)S(1)}, bf16[9,69,256]{2,1...) custom-call(bf16[69,16,128]{2,1,0:T(8,128)(2,1)} %fields_ref.1, ...), custom_call_target="tpu_custom_call" | custom-call | flops 10000000 | bytes 20000 | tf_op jit(solution)/shard_map/pallas_call | solution.py:443
  2.0 2.7 %collective-permute-start = (bf16[8,1104]{1,0:T(8,128)(2,1)S(1)}, bf16[8,1104]{1,0:T(8,128)(2,1)S(1)}, u32[]{:S(2)}, u32[]{:S(2)}) collective-permute-start(bf16[8,1104]{1,0:T(8,128)(2,1)S(1)} %get-tuple-element.47), channel_id=1, source_target_pairs={{0,1},{1,2},{2,3},{3,4},{4,5},{5,6},{6,7},{7,8},{8,9},{9,10},{10,1... | collective-permute-start | bytes 53000 | tf_op jit(solution)/shard_map/ppermute | solution.py:454
  4.7 0.7 %collective-permute-start.1 = (bf16[8,1104]{1,0:T(8,128)(2,1)S(1)}, bf16[8,1104]{1,0:T(8,128)(2,1)S(1)}, u32[]{:S(2)}, u32[]{:S(2)}) collective-permute-start(bf16[8,1104]{1,0:T(8,128)(2,1)S(1)} %get-tuple-element.48), channel_id=1, source_target_pairs={{1,0},{2,1},{3,2},{4,3},{5,4},{6,5},{7,6},{8,7},{9,8},{10,9},{11,1... | collective-permute-start | bytes 53000 | tf_op jit(solution)/shard_map/ppermute | solution.py:455
  5.4 0.1 pad_add_fusion.flags_ref
  5.5 0.5 shard_map.76
  6.0 0.2 copy.12
  6.2 0.2 copy.13.gt_ref
  6.3 0.0 collective-permute-done.east_ref
  6.4 1.5 %collective-permute-done.1.west_ref = bf16[8,1104]{1,0:T(8,128)(2,1)S(1)} collective-permute-done((bf16[8,1104]{1,0:T(8,128)(2,1)S(1)}, bf16[8,1104]{1,0:T(8,128)(2,1)S(1)}, u32[]{:S(2)}, u32[]{:S(2)}) %collective-permute-start.1) | collective-permute-done | bytes 17696 | tf_op jit(solution)/shard_map/ppermute | solution.py:455
  7.9 0.9 %shard_map.78 = (bf16[4,72,128]{2,1,0:T(8,128)(2,1)S(1)}, bf16[4,72,128]{2,1,0:T(8,128)(2,1)S(1)}) custom-call(s32[4]{0:T(128)S(1)} %pad_add_fusion.flags_ref, bf16[16,80,128]{2,1,0:T(8,128)(2,1)S(1)} %get-tuple-element.45.x_ref, bf16[16,80,128]{2,1,0:T(8,128)(2,1)S(1)} %get-tuple-element.46.r_ref, bf16[8,1104]{1,0:T(8,128)(2,1)S(1)} %collective-permute-done.east_ref, ...), custom_call_target="tpu_custom_call" | custom-call | flops 10000000 | bytes 20000 | tf_op jit(solution)/shard_map/pallas_call | solution.py:464
  8.8 3.3 %collective-permute-start.2 = (bf16[4,72,128]{2,1,0:T(8,128)(2,1)S(1)}, bf16[4,72,128]{2,1,0:T(8,128)(2,1)S(1)}, u32[]{:S(2)}, u32[]{:S(2)}) collective-permute-start(bf16[4,72,128]{2,1,0:T(8,128)(2,1)S(1)} %get-tuple-element.54), channel_id=1, source_target_pairs={{0,16},{1,17},{2,18},{3,19},{4,20},{5,21},{6,22},{7,23},{8,0},{9,1... | collective-permute-start | bytes 221192 | tf_op jit(solution)/shard_map/ppermute | solution.py:468
  12.0 0.0 collective-permute-start.3
  12.0 3.7 %shard_map.77 = (bf16[14,256,128]{2,1,0:T(8,128)(2,1)S(1)}, bf16[14,256,128]{2,1,0:T(8,128)(2,1)S(1)}, f32[2,720,256]{2,1,0:T(8,128)S(1)}, bf16[4,240,128]{2,1,0:T(8,128)(2,1)S(1)}, bf16[4,240,128]{2,1,0:T(8,128)(2,1)S(1)}) custom-call(bf16[16,80,128]{2,1,0:T(8,128)(2,1)S(1)} %get-tuple-element.45.x_ref, bf16[16,80,128]{2,1,0:T(8,128)(2,1)S(1)} %get-tuple-element.46.r_ref, ...), custom_call_target="tpu_custom_call" | custom-call | flops 8999999488 | bytes 18000000 | tf_op jit(solution)/shard_map/pallas_call | solution.py:473
  15.7 0.0 collective-permute-done.2.pa_ref
  15.8 1.0 %collective-permute-done.3.pb_ref = bf16[4,72,128]{2,1,0:T(8,128)(2,1)S(1)} collective-permute-done((bf16[4,72,128]{2,1,0:T(8,128)(2,1)S(1)}, bf16[4,72,128]{2,1,0:T(8,128)(2,1)S(1)}, u32[]{:S(2)}, u32[]{:S(2)}) %collective-permute-start.3) | collective-permute-done | bytes 73760 | tf_op jit(solution)/shard_map/ppermute | solution.py:469
  16.8 1.6 %shard_map.79 = (bf16[2,256,128]{2,1,0:T(8,128)(2,1)S(1)}, bf16[2,256,128]{2,1,0:T(8,128)(2,1)S(1)}, bf16[1280,128]{1,0:T(8,128)(2,1)S(1)}, bf16[2,720,256]{2,1,...) custom-call(s32[4]{0:T(128)S(1)} %pad_add_fusion.flags_ref, ...), custom_call_target="tpu_custom_call" | custom-call | flops 1000000000 | bytes 2000000 | tf_op jit(solution)/shard_map/pallas_call | solution.py:493
  18.4 2.3 %collective-permute-start.4 = (bf16[1280,128]{1,0:T(8,128)(2,1)S(1)}, bf16[1280,128]{1,0:T(8,128)(2,1)S(1)}, u32[]{:S(2)}, u32[]{:S(2)}) collective-permute-start(bf16[1280,128]{1,0:T(8,128)(2,1)S(1)} %get-tuple-element.59), channel_id=1, source_target_pairs={{0,1},{1,0},{2,3},{3,2},{4,5},{5,4},{6,7},{7,6},{8,9},{9,8},{10,11... | collective-permute-start | bytes 983048 | tf_op jit(solution)/shard_map/ppermute | solution.py:402
  20.6 0.9 %shard_map.80 = f32[1280,128]{1,0:T(8,128)S(1)} custom-call(s32[4]{0:T(128)S(1)} %pad_add_fusion.flags_ref, f32[2,720,256]{2,1,0:T(8,128)S(1)} %get-tuple-element.51.acc_ref, bf16[2,720,256]{2,1,0:T(8,128)(2,1)S(1)} %get-tuple-element.56.lhs_ref, bf16[2,256,256]{2,1,0:T(8,128)(2,1)S(1)} %get-tuple-element.57.rhs_ref, ...), custom_call_target="tpu_custom_call" | custom-call | flops 1000000000 | bytes 2000000 | tf_op jit(solution)/shard_map/pallas_call | solution.py:509
  21.6 0.3 collective-permute-done.4
  21.9 0.8 %add_convert_fusion = bf16[1280,128]{1,0:T(8,128)(2,1)} fusion(f32[1280,128]{1,0:T(8,128)S(1)} %shard_map.80, bf16[1280,128]{1,0:T(8,128)(2,1)S(1)} %collective-permute-done.4), kind=kLoop, calls=%fused_computation | loop fusion | flops 491520 | bytes 1310720 | tf_op jit(solution)/shard_map/convert_element_type | solution.py:512
  22.7 5.9 %all-to-all-start = ((bf16[16,80,128]{2,1,0:T(8,128)(2,1)}), bf16[16,80,128]{2,1,0:T(8,128)(2,1)S(1)}, u32[]{:S(2)}, u32[]{:S(2)}) async-start(bf16[16,80,128]{2,1,0:T(8,128)(2,1)} %bitcast.11), calls=%async_computation | async-start | bytes 655360 | tf_op jit(solution)/shard_map/all_to_all | solution.py:554
  28.6 1.4 %shard_map.81.refs_0_ = bf16[256,16,128]{2,1,0:T(8,128)(2,1)} custom-call(bf16[14,256,128]{2,1,0:T(8,128)(2,1)S(1)} %get-tuple-element.72.mid_ref, bf16[2,256,128]{2,1,0:T(8,128)(2,1)S(1)} %get-tuple-element.73.edge_ref), custom_call_target="tpu_custom_call" | custom-call | flops 1000000000 | bytes 1000000 | tf_op jit(solution)/shard_map/pallas_call | solution.py:534
  30.0 1.7 %shard_map.82 = (bf16[2,256,128]{2,1,0:T(8,128)(2,1)S(1)}, bf16[256,128]{1,0:T(8,128)(2,1)S(1)}) custom-call(s32[4]{0:T(128)S(1)} %pad_add_fusion.flags_ref, bf16[16,80,128]{2,1,0:T(8,128)(2,1)S(1)} %get-tuple-element.45.x_ref, bf16[8,1104]{1,0:T(8,128)(2,1)S(1)} %collective-permute-done.east_ref, bf16[8,1104]{1,0:T(8,128)(2,1)S(1)} %collective-permute-done.1.west_ref, ...), custom_call_target="tpu_custom_call" | custom-call | flops 1000000000 | bytes 2000000 | tf_op jit(solution)/shard_map/pallas_call | solution.py:514
  31.7 2.1 %shard_map.83 = bf16[69,16,128]{2,1,0:T(8,128)(2,1)} custom-call(bf16[14,256,128]{2,1,0:T(8,128)(2,1)S(1)} %copy-done.1, bf16[2,256,128]{2,1,0:T(8,128)(2,1)S(1)} %get-tuple-element.65.edge_ref, bf16[2,256,128]{2,1,0:T(8,128)(2,1)S(1)} %get-tuple-element.67.halo_ref, bf16[256,128]{1,0:T(8,128)(2,1)S(1)} %get-tuple-element.68.strip_ref, ...), custom_call_target="tpu_custom_call" | custom-call | flops 4000000000 | bytes 8000000 | tf_op jit(solution)/shard_map/pallas_call | solution.py:520
  33.8 3.8 %all-to-all-done.pieces_ref = bf16[16,80,128]{2,1,0:T(8,128)(2,1)S(1)} async-done(((bf16[16,80,128]{2,1,0:T(8,128)(2,1)}), bf16[16,80,128]{2,1,0:T(8,128)(2,1)S(1)}, u32[]{:S(2)}, u32[]{:S(2)}) %all-to-all-start) | async-done | bytes 327712 | tf_op jit(solution)/shard_map/all_to_all | solution.py:554
  37.6 0.1 shard_map.84
  37.7 16.2 %all_to_all.15.pieces_ref = bf16[8,80,128]{2,1,0:T(8,128)(2,1)S(1)} all-to-all(bf16[8,80,128]{2,1,0:T(8,128)(2,1)S(1)} %shard_map.84), channel_id=1, replica_groups=mesh['z'=8,'y_hi'=2,'y_lo'=2,'x'=4,'core'=2] {'z'}, dimensions={0} | all-to-all | bytes 327680 | tf_op jit(solution)/shard_map/all_to_all | solution.py:554
  53.9 10.6 %all_to_all.16 = bf16[16,80,128]{2,1,0:T(8,128)(2,1)S(1)} all-to-all(bf16[16,80,128]{2,1,0:T(8,128)(2,1)S(1)} %shard_map.85), channel_id=1, replica_groups=mesh['z'=8,'y_hi'=2,'y_lo'=2,'x'=4,'core'=2] {'y_hi','y_lo','x'}, dimensions={0} | all-to-all | bytes 655360 | tf_op jit(solution)/shard_map/all_to_all | solution.py:554
  64.6 3.9 %collective-permute-start.5 = (bf16[1280,128]{1,0:T(8,128)(2,1)S(1)}, bf16[1280,128]{1,0:T(8,128)(2,1)S(1)}, u32[]{:S(2)}, u32[]{:S(2)}) collective-permute-start(bf16[1280,128]{1,0:T(8,128)(2,1)S(1)} %bitcast.19), channel_id=1, source_target_pairs={{0,1},{1,0},{2,3},{3,2},{4,5},{5,4},{6,7},{7,6},{8,9},{9,8},{10,11... | collective-permute-start | bytes 983048 | tf_op jit(solution)/shard_map/ppermute | solution.py:402
  68.5 1.4 %shard_map.86 = bf16[256,16,128]{2,1,0:T(8,128)(2,1)} custom-call(bf16[14,256,128]{2,1,0:T(8,128)(2,1)S(1)} %get-tuple-element.72.mid_ref, bf16[2,256,128]{2,1,0:T(8,128)(2,1)S(1)} %get-tuple-element.73.edge_ref, bf16[256,16,128]{2,1,0:T(8,128)(2,1)} %shard_map.81.refs_0_), custom_call_target="tpu_custom_call", output_to_operand_aliasing={{}: (2, {})} | custom-call | flops 1000000000 | bytes 1000000 | tf_op jit(solution)/shard_map/pallas_call | solution.py:534
  69.8 0.0 collective-permute-done.5.other_ref
  69.9 1.8 %shard_map.87 = (f32[9,69,256]{2,1,0:T(8,128)}, f32[9,69,256]{2,1,0:T(8,128)}) custom-call(s32[4]{0:T(128)S(1)} %pad_add_fusion.flags_ref, bf16[1280,128]{1,0:T(8,128)(2,1)S(1)} %bitcast.20, bf16[1280,128]{1,0:T(8,128)(2,1)S(1)} %collective-permute-done.5.other_ref), custom_call_target="tpu_custom_call" | custom-call | flops 10000000 | bytes 20000 | tf_op jit(solution)/shard_map/pallas_call | solution.py:572
  (5 shorter events, 0.0 us)
Async XLA Ops:
  2.0 4.4 %collective-permute-start = (bf16[8,1104]{1,0:T(8,128)(2,1)S(1)}, bf16[8,1104]{1,0:T(8,128)(2,1)S(1)}, u32[]{:S(2)}, u32[]{:S(2)}) collective-permute-start(bf16[8,1104]{1,0:T(8,128)(2,1)S(1)} %get-tuple-element.47), channel_id=1, source_target_pairs={{0,1},{1,2},{2,3},{3,4},{4,5},{5,6},{6,7},{7,8},{8,9},{9,10},{10,1... | collective-permute-start | bytes 53000 | tf_op jit(solution)/shard_map/ppermute | solution.py:454
  4.7 3.2 %collective-permute-start.1 = (bf16[8,1104]{1,0:T(8,128)(2,1)S(1)}, bf16[8,1104]{1,0:T(8,128)(2,1)S(1)}, u32[]{:S(2)}, u32[]{:S(2)}) collective-permute-start(bf16[8,1104]{1,0:T(8,128)(2,1)S(1)} %get-tuple-element.48), channel_id=1, source_target_pairs={{1,0},{2,1},{3,2},{4,3},{5,4},{6,5},{7,6},{8,7},{9,8},{10,9},{11,1... | collective-permute-start | bytes 53000 | tf_op jit(solution)/shard_map/ppermute | solution.py:455
  8.8 7.0 %collective-permute-start.2 = (bf16[4,72,128]{2,1,0:T(8,128)(2,1)S(1)}, bf16[4,72,128]{2,1,0:T(8,128)(2,1)S(1)}, u32[]{:S(2)}, u32[]{:S(2)}) collective-permute-start(bf16[4,72,128]{2,1,0:T(8,128)(2,1)S(1)} %get-tuple-element.54), channel_id=1, source_target_pairs={{0,16},{1,17},{2,18},{3,19},{4,20},{5,21},{6,22},{7,23},{8,0},{9,1... | collective-permute-start | bytes 221192 | tf_op jit(solution)/shard_map/ppermute | solution.py:468
  12.0 4.7 %collective-permute-start.3 = (bf16[4,72,128]{2,1,0:T(8,128)(2,1)S(1)}, bf16[4,72,128]{2,1,0:T(8,128)(2,1)S(1)}, u32[]{:S(2)}, u32[]{:S(2)}) collective-permute-start(bf16[4,72,128]{2,1,0:T(8,128)(2,1)S(1)} %get-tuple-element.55), channel_id=1, source_target_pairs={{16,0},{17,1},{18,2},{19,3},{20,4},{21,5},{22,6},{23,7},{0,8},{1,9... | collective-permute-start | bytes 221192 | tf_op jit(solution)/shard_map/ppermute | solution.py:469
  15.7 2.6 %copy-start = (bf16[14,256,128]{2,1,0:T(8,128)(2,1)}, bf16[14,256,128]{2,1,0:T(8,128)(2,1)S(1)}, u32[]{:S(2)}) copy-start(bf16[14,256,128]{2,1,0:T(8,128)(2,1)S(1)} %get-tuple-element.64.mid_ref) | copy-start | bytes 2752516
  18.4 3.5 %collective-permute-start.4 = (bf16[1280,128]{1,0:T(8,128)(2,1)S(1)}, bf16[1280,128]{1,0:T(8,128)(2,1)S(1)}, u32[]{:S(2)}, u32[]{:S(2)}) collective-permute-start(bf16[1280,128]{1,0:T(8,128)(2,1)S(1)} %get-tuple-element.59), channel_id=1, source_target_pairs={{0,1},{1,0},{2,3},{3,2},{4,5},{5,4},{6,7},{7,6},{8,9},{9,8},{10,11... | collective-permute-start | bytes 983048 | tf_op jit(solution)/shard_map/ppermute | solution.py:402
  22.7 15.0 %all-to-all-start = ((bf16[16,80,128]{2,1,0:T(8,128)(2,1)}), bf16[16,80,128]{2,1,0:T(8,128)(2,1)S(1)}, u32[]{:S(2)}, u32[]{:S(2)}) async-start(bf16[16,80,128]{2,1,0:T(8,128)(2,1)} %bitcast.11), calls=%async_computation | async-start | bytes 655360 | tf_op jit(solution)/shard_map/all_to_all | solution.py:554
  30.0 1.8 %copy-start.1 = (bf16[14,256,128]{2,1,0:T(8,128)(2,1)S(1)}, bf16[14,256,128]{2,1,0:T(8,128)(2,1)}, u32[]{:S(2)}) copy-start(bf16[14,256,128]{2,1,0:T(8,128)(2,1)} %copy-done) | copy-start | bytes 2752516
  64.6 5.3 %collective-permute-start.5 = (bf16[1280,128]{1,0:T(8,128)(2,1)S(1)}, bf16[1280,128]{1,0:T(8,128)(2,1)S(1)}, u32[]{:S(2)}, u32[]{:S(2)}) collective-permute-start(bf16[1280,128]{1,0:T(8,128)(2,1)S(1)} %bitcast.19), channel_id=1, source_target_pairs={{0,1},{1,0},{2,3},{3,2},{4,5},{5,4},{6,7},{7,6},{8,9},{9,8},{10,11... | collective-permute-start | bytes 983048 | tf_op jit(solution)/shard_map/ppermute | solution.py:402
